TPU v7x, 32 devices: a whole 2x2x4 slice. The times are simulated.
32 devices in a mesh: dp: 8 (over z, y), tensor: 4 (over x, core).
Axes of the slice: x: 2, y: 2, z: 4, core: 2. Of those that a mesh axis runs over, the one named last changes fastest.
Arguments:
- hidden: bfloat16 [16384, 768], P('dp'), may hold values from -6 to 6
- cotangent: bfloat16 [16384, 768], P('dp'), may hold values from -6 to 6
- seg_ids: int32 [16384], P('dp'), may hold values from 0 to 1024, as said below
- counts: int32 [8], P('dp'), may hold values from 1024 to 2048, as said below
- norm_gain: float32 [768], replicated, may hold values from 0.5 to 1.5
- w_x: bfloat16 [768, 1536], P(None, 'tensor'), may hold values from -0.21875 to 0.21875
- w_z: bfloat16 [768, 1536], P(None, 'tensor'), may hold values from -0.21875 to 0.21875
- w_dt: bfloat16 [768, 24], P(None, 'tensor'), may hold values from -0.21875 to 0.21875
- w_bc: bfloat16 [768, 256], replicated, may hold values from -0.21875 to 0.21875
- conv_x: float32 [4, 1536], P(None, 'tensor'), may hold values from -3 to 3
- conv_x_bias: float32 [1536], P('tensor'), may hold values from -0.5 to 0.5
- conv_bc: float32 [4, 256], replicated, may hold values from -3 to 3
- conv_bc_bias: float32 [256], replicated, may hold values from -0.5 to 0.5
- dt_bias: float32 [24], P('tensor'), may hold values from -4 to -1
- a_log: float32 [24], P('tensor'), may hold values from -1 to 2.5
- d_skip: float32 [24], P('tensor'), may hold values from 0.5 to 1.5
- gate_gain: float32 [1536], P('tensor'), may hold values from 0.5 to 1.5
- w_out: bfloat16 [1536, 768], P('tensor'), may hold values from -0.15625 to 0.15625
Outputs:
- block_out: bfloat16 [16384, 768], P('dp')
- grad_hidden: float32 [16384, 768], P('dp')
- grad_norm_gain: float32 [768], replicated
- grad_w_x: float32 [768, 1536], P(None, 'tensor')
- grad_w_z: float32 [768, 1536], P(None, 'tensor')
- grad_w_dt: float32 [768, 24], P(None, 'tensor')
- grad_w_bc: float32 [768, 256], replicated
- grad_conv_x: float32 [4, 1536], P(None, 'tensor')
- grad_conv_x_bias: float32 [1536], P('tensor')
- grad_conv_bc: float32 [4, 256], replicated
- grad_conv_bc_bias: float32 [256], replicated
- grad_dt_bias: float32 [24], P('tensor')
- grad_a_log: float32 [24], P('tensor')
- grad_d_skip: float32 [24], P('tensor')
- grad_gate_gain: float32 [1536], P('tensor')
- grad_w_out: float32 [1536, 768], P('tensor')
Inputs may be any that keep to these rules, and one draw needn't show every extreme that they name: `seg_ids`: within each shard of 2048 slots the ids start at 0, never fall and rise by at most 1 from slot to slot; slots 0 to 1023 have id 0 and slot 1024 starts a new id; in some shard every slot from 1024 on starts a new id. `counts`: each shard's count is at least 1024; some shard is full in every draw.
All inputs are finite; a program needn't handle non-finite values.
Results may differ from a plain program's by a relative error of at most 0.012.
Values sent between devices are 32-bit elements; how exact they have to be, the bound alone decides.
No kernel may reach another device: no remote copies, remote signals or barrier semaphores. Data moves between devices by JAX's collectives and lax.ppermute only.
A program may use at most 128 MiB of HBM per device.

v0:
```python
import jax
import jax.numpy as jnp
from jax import lax
from jax.sharding import PartitionSpec as P

INNER = 1536
SPAN = 256


EPS = 1e-05


def silu_grad(values):
    sigmoid_of = jax.nn.sigmoid(values)
    return sigmoid_of * (1.0 + values * (1.0 - sigmoid_of))


def lagged(values, offset):
    if offset == 0:
        return values
    padding = jnp.zeros((offset,) + values.shape[1:], values.dtype)
    return jnp.concatenate([padding, values[:-offset]], 0)


def leading(values, offset):
    padding = jnp.zeros((offset,) + values.shape[1:], values.dtype)
    return jnp.concatenate([values[offset:], padding], 0)


def conv_apply(values, weight, bias, conv_masks):
    total = bias + weight[0] * values
    for offset in range(1, len(conv_masks)):
        total = total + weight[offset] * lagged(values, offset) * conv_masks[offset]
    return total


def conv_back(values, weight, conv_masks, grad_pre):
    grad_weight = jnp.stack(
        [
            jnp.sum(grad_pre * conv_masks[offset] * lagged(values, offset), 0)
            for offset in range(len(conv_masks))
        ],
        0,
    )
    grad_bias = jnp.sum(grad_pre, 0)
    grad_values = grad_pre * weight[0]
    for offset in range(1, len(conv_masks)):
        grad_values = grad_values + leading(grad_pre * conv_masks[offset], offset) * weight[offset]
    return (grad_weight, grad_bias, grad_values)


def per_device(
    hidden,
    cotangent,
    seg_ids,
    counts,
    norm_gain,
    w_x,
    w_z,
    w_dt,
    w_bc,
    conv_x,
    conv_x_bias,
    conv_bc,
    conv_bc_bias,
    dt_bias,
    a_log,
    d_skip,
    gate_gain,
    w_out,
):
    row_count = hidden.shape[0]
    state_width = w_bc.shape[1] // 2
    heads_here = w_dt.shape[1]
    width_here = w_x.shape[1]
    head_size = width_here // heads_here
    tap_count = conv_x.shape[0]
    span_count = row_count // SPAN
    highest = lax.Precision.HIGHEST
    positions = jnp.arange(row_count)
    live_rows = (positions < counts[0]).astype(jnp.float32)[:, None]
    conv_masks = [
        ((lagged(seg_ids, offset) == seg_ids) & (positions >= offset)).astype(jnp.float32)[:, None]
        for offset in range(tap_count)
    ]
    hidden_wide = hidden.astype(jnp.float32)
    inv_rms = lax.rsqrt(jnp.mean(hidden_wide * hidden_wide, -1, keepdims=True) + EPS)
    normed = (hidden_wide * inv_rms * norm_gain).astype(jnp.bfloat16)
    normed_wide = normed.astype(jnp.float32)
    proj_x = jnp.dot(normed, w_x, preferred_element_type=jnp.float32)
    proj_z = jnp.dot(normed, w_z, preferred_element_type=jnp.float32)
    proj_dt = jnp.dot(normed, w_dt, preferred_element_type=jnp.float32)
    proj_bc = jnp.dot(normed, w_bc, preferred_element_type=jnp.float32)
    x_pre = conv_apply(proj_x, conv_x, conv_x_bias, conv_masks)
    bc_pre = conv_apply(proj_bc, conv_bc, conv_bc_bias, conv_masks)
    x_conv = jax.nn.silu(x_pre)
    bc_conv = jax.nn.silu(bc_pre)
    b_low = bc_conv[:, :state_width].astype(jnp.bfloat16)
    c_low = bc_conv[:, state_width:].astype(jnp.bfloat16)
    dt_in = proj_dt + dt_bias
    step_size = jax.nn.softplus(dt_in)
    rates = -jnp.exp(a_log)
    log_decay = jnp.cumsum(step_size * rates, 0)
    x_heads = x_conv.reshape(row_count, heads_here, head_size)
    inputs = (step_size[:, :, None] * x_heads).astype(jnp.bfloat16)
    ld_blocks = log_decay.reshape(span_count, SPAN, heads_here)
    seg_blocks = seg_ids.reshape(span_count, SPAN)
    local_pos = jnp.arange(SPAN)
    intra = (local_pos[:, None] >= local_pos[None, :])[None] & (
        seg_blocks[:, :, None] == seg_blocks[:, None, :]
    )
    ld_heads = jnp.transpose(ld_blocks, (0, 2, 1))
    exponent = jnp.where(
        intra[:, None], ld_heads[:, :, :, None] - ld_heads[:, :, None, :], -10000.0
    )
    decays = jnp.exp(exponent)
    b_blocks = b_low.reshape(span_count, SPAN, state_width)
    c_blocks = c_low.reshape(span_count, SPAN, state_width)
    inputs_blocks = inputs.reshape(span_count, SPAN, heads_here, head_size)
    kernel = jnp.einsum("cpn,cqn->cpq", c_blocks, b_blocks, preferred_element_type=jnp.float32)
    mixing = (kernel[:, None] * decays).astype(jnp.bfloat16)
    local_part = jnp.einsum(
        "chpq,cqhd->cphd", mixing, inputs_blocks, preferred_element_type=jnp.float32
    )
    ld_end = ld_blocks[:, -1]
    seg_end = seg_blocks[:, -1]
    in_keep = (seg_blocks == seg_end[:, None])[:, :, None]
    decay_in = jnp.where(in_keep, jnp.exp(ld_end[:, None, :] - ld_blocks), 0.0)
    b_blocks_wide = b_blocks.astype(jnp.float32)
    weighted_b = (b_blocks_wide[:, :, None, :] * decay_in[..., None]).astype(jnp.bfloat16)
    span_new = jnp.einsum(
        "cqhn,cqhd->chnd", weighted_b, inputs_blocks, preferred_element_type=jnp.float32
    )
    hop = jnp.where((seg_end[1:] == seg_end[:-1])[:, None], jnp.exp(ld_end[1:] - ld_end[:-1]), 0.0)
    state = jnp.zeros((heads_here, state_width, head_size), jnp.float32)
    befores = []
    for span in range(span_count):
        befores.append(state)
        if span == 0:
            state = span_new[0]
        else:
            state = hop[span - 1][:, None, None] * state + span_new[span]
    states_before = jnp.stack(befores, 0)
    carried_low = states_before.astype(jnp.bfloat16)
    prev_seg = jnp.concatenate([jnp.full((1,), -1, jnp.int32), seg_end[:-1]], 0)
    prev_ld = jnp.concatenate([jnp.zeros((1, heads_here), jnp.float32), ld_end[:-1]], 0)
    out_keep = (seg_blocks == prev_seg[:, None])[:, :, None]
    decay_out = jnp.where(out_keep, jnp.exp(ld_blocks - prev_ld[:, None, :]), 0.0)
    cross_raw = jnp.einsum(
        "cpn,chnd->cphd", c_blocks, carried_low, preferred_element_type=jnp.float32
    )
    scanned = (local_part + decay_out[..., None] * cross_raw).reshape(
        row_count, heads_here, head_size
    )
    y_flat = (scanned + d_skip[None, :, None] * x_heads).reshape(row_count, width_here)
    z_active = jax.nn.silu(proj_z)
    gated_out = y_flat * z_active
    squares = lax.psum(jnp.sum(gated_out * gated_out, -1), "tensor")
    inv_gate = lax.rsqrt(squares[:, None] / INNER + EPS)
    scaled = gated_out * inv_gate
    out_in = (scaled * gate_gain).astype(jnp.bfloat16)
    mixed = lax.psum(jnp.dot(out_in, w_out, preferred_element_type=jnp.float32), "tensor")
    output = (hidden_wide + live_rows * mixed).astype(jnp.bfloat16)
    grad_out = cotangent.astype(jnp.float32)
    grad_mix = (live_rows * grad_out).astype(jnp.bfloat16)
    grad_w_out = jnp.dot(out_in.T, grad_mix, preferred_element_type=jnp.float32)
    grad_in = jnp.dot(grad_mix, w_out.T, preferred_element_type=jnp.float32)
    grad_gate_gain = jnp.sum(grad_in * scaled, 0)
    grad_scaled = grad_in * gate_gain
    cross_sum = lax.psum(jnp.sum(grad_scaled * gated_out, -1), "tensor")
    grad_gated = inv_gate * grad_scaled - gated_out * inv_gate**3 * cross_sum[:, None] / INNER
    grad_y = (grad_gated * z_active).reshape(row_count, heads_here, head_size)
    grad_z = (grad_gated * y_flat * silu_grad(proj_z)).astype(jnp.bfloat16)
    grad_d_skip = jnp.sum(grad_y * x_heads, (0, 2))
    grad_scan = grad_y.astype(jnp.bfloat16)
    grad_scan_blocks = grad_scan.reshape(span_count, SPAN, heads_here, head_size)
    grad_mixing = jnp.einsum(
        "cphd,cqhd->chpq", grad_scan_blocks, inputs_blocks, preferred_element_type=jnp.float32
    )
    grad_inputs_blocks = jnp.einsum(
        "chpq,cphd->cqhd", mixing, grad_scan_blocks, preferred_element_type=jnp.float32
    )
    grad_kernel = (grad_mixing * decays).astype(jnp.bfloat16)
    grad_expo = grad_mixing * kernel[:, None] * decays
    grad_ld = jnp.transpose(jnp.sum(grad_expo, 3) - jnp.sum(grad_expo, 2), (0, 2, 1))
    grad_c_blocks = jnp.einsum(
        "chpq,cqn->cpn", grad_kernel, b_blocks, preferred_element_type=jnp.float32
    )
    grad_b_blocks = jnp.einsum(
        "chpq,cpn->cqn", grad_kernel, c_blocks, preferred_element_type=jnp.float32
    )
    grad_scan_wide = grad_scan_blocks.astype(jnp.float32)
    grad_decay_out = jnp.sum(grad_scan_wide * cross_raw, -1)
    grad_cross_raw = decay_out[..., None] * grad_scan_wide
    grad_c_blocks = grad_c_blocks + jnp.einsum(
        "cphd,chnd->cpn",
        grad_cross_raw,
        carried_low.astype(jnp.float32),
        precision=highest,
        preferred_element_type=jnp.float32,
    )
    grad_states = jnp.einsum(
        "cpn,cphd->chnd",
        c_blocks.astype(jnp.float32),
        grad_cross_raw,
        precision=highest,
        preferred_element_type=jnp.float32,
    )
    out_term = grad_decay_out * decay_out
    grad_ld = grad_ld + out_term
    grad_prev_ld = -jnp.sum(out_term, 1)
    grad_end = jnp.concatenate([grad_prev_ld[1:], jnp.zeros((1, heads_here), jnp.float32)], 0)
    flow = jnp.zeros((heads_here, state_width, head_size), jnp.float32)
    grad_new_list = [flow] * span_count
    hop_grads = []
    for span in reversed(range(span_count)):
        grad_new_list[span] = flow
        if span > 0:
            hop_grads.append(jnp.sum(flow * states_before[span], (1, 2)))
            flow = grad_states[span] + hop[span - 1][:, None, None] * flow
    grad_new = jnp.stack(grad_new_list, 0)
    hop_terms = jnp.stack(hop_grads[::-1], 0) * hop
    zero_row = jnp.zeros((1, heads_here), jnp.float32)
    grad_end = (
        grad_end
        + jnp.concatenate([zero_row, hop_terms], 0)
        - jnp.concatenate([hop_terms, zero_row], 0)
    )
    grad_weighted_b = jnp.einsum(
        "chnd,cqhd->cqhn",
        grad_new,
        inputs_blocks.astype(jnp.float32),
        precision=highest,
        preferred_element_type=jnp.float32,
    )
    grad_inputs_blocks = grad_inputs_blocks + jnp.einsum(
        "chnd,cqhn->cqhd",
        grad_new,
        weighted_b.astype(jnp.float32),
        precision=highest,
        preferred_element_type=jnp.float32,
    )
    grad_b_blocks = grad_b_blocks + jnp.sum(grad_weighted_b * decay_in[..., None], 2)
    in_term = jnp.sum(grad_weighted_b * b_blocks_wide[:, :, None, :], -1) * decay_in
    grad_end = grad_end + jnp.sum(in_term, 1)
    grad_ld = grad_ld - in_term
    end_mask = (local_pos == SPAN - 1).astype(jnp.float32)[None, :, None]
    grad_ld = grad_ld + end_mask * grad_end[:, None, :]
    grad_log = grad_ld.reshape(row_count, heads_here)
    grad_rate_sum = jnp.cumsum(grad_log[::-1], 0)[::-1]
    grad_inputs = grad_inputs_blocks.reshape(row_count, heads_here, head_size)
    grad_step = jnp.sum(grad_inputs * x_heads, -1) + grad_rate_sum * rates
    grad_a_log = jnp.sum(grad_rate_sum * step_size, 0) * rates
    grad_dt_in = grad_step * jax.nn.sigmoid(dt_in)
    grad_dt_bias = jnp.sum(grad_dt_in, 0)
    grad_x_heads = grad_y * d_skip[None, :, None] + grad_inputs * step_size[:, :, None]
    grad_bc = jnp.concatenate(
        [
            grad_b_blocks.reshape(row_count, state_width),
            grad_c_blocks.reshape(row_count, state_width),
        ],
        1,
    )
    grad_x_pre = grad_x_heads.reshape(row_count, width_here) * silu_grad(x_pre)
    grad_conv_x, grad_conv_x_bias, grad_proj_x = conv_back(proj_x, conv_x, conv_masks, grad_x_pre)
    grad_proj_low = grad_proj_x.astype(jnp.bfloat16)
    grad_w_x = jnp.dot(normed.T, grad_proj_low, preferred_element_type=jnp.float32)
    grad_w_z = jnp.dot(normed.T, grad_z, preferred_element_type=jnp.float32)
    grad_w_dt = jnp.dot(
        normed_wide.T, grad_dt_in, precision=highest, preferred_element_type=jnp.float32
    )
    partial_in = (
        jnp.dot(grad_proj_low, w_x.T, preferred_element_type=jnp.float32)
        + jnp.dot(grad_z, w_z.T, preferred_element_type=jnp.float32)
        + jnp.dot(
            grad_dt_in,
            w_dt.astype(jnp.float32).T,
            precision=highest,
            preferred_element_type=jnp.float32,
        )
    )
    bc_total = lax.psum(grad_bc, "tensor")
    grad_bc_pre = bc_total * silu_grad(bc_pre)
    grad_conv_bc, grad_conv_bc_bias, grad_proj_bc = conv_back(
        proj_bc, conv_bc, conv_masks, grad_bc_pre
    )
    grad_w_bc = jnp.dot(
        normed_wide.T, grad_proj_bc, precision=highest, preferred_element_type=jnp.float32
    )
    from_state = jnp.dot(
        grad_proj_bc,
        w_bc.astype(jnp.float32).T,
        precision=highest,
        preferred_element_type=jnp.float32,
    )
    summed_in = lax.psum(partial_in, "tensor")
    grad_normed = summed_in + from_state
    weighted = grad_normed * norm_gain
    grad_norm_gain = jnp.sum(grad_normed * hidden_wide * inv_rms, 0)
    grad_hidden = (
        grad_out
        + inv_rms * weighted
        - hidden_wide * inv_rms**3 * jnp.mean(weighted * hidden_wide, -1, keepdims=True)
    )
    main_sums = lax.psum(
        (
            grad_norm_gain,
            grad_w_x,
            grad_w_z,
            grad_w_dt,
            grad_conv_x,
            grad_conv_x_bias,
            grad_dt_bias,
            grad_a_log,
            grad_d_skip,
            grad_gate_gain,
            grad_w_out,
        ),
        "dp",
    )
    state_sums = lax.psum((grad_w_bc, grad_conv_bc, grad_conv_bc_bias), "dp")
    return (
        output,
        grad_hidden,
        main_sums[0],
        main_sums[1],
        main_sums[2],
        main_sums[3],
        state_sums[0],
        main_sums[4],
        main_sums[5],
        state_sums[1],
        state_sums[2],
        main_sums[6],
        main_sums[7],
        main_sums[8],
        main_sums[9],
        main_sums[10],
    )


def solution(mesh):
    return jax.shard_map(
        per_device,
        mesh=mesh,
        in_specs=(
            P("dp", None),
            P("dp", None),
            P("dp"),
            P("dp"),
            P(),
            P(None, "tensor"),
            P(None, "tensor"),
            P(None, "tensor"),
            P(),
            P(None, "tensor"),
            P("tensor"),
            P(),
            P(),
            P("tensor"),
            P("tensor"),
            P("tensor"),
            P("tensor"),
            P("tensor", None),
        ),
        out_specs=(
            P("dp", None),
            P("dp", None),
            P(),
            P(None, "tensor"),
            P(None, "tensor"),
            P(None, "tensor"),
            P(),
            P(None, "tensor"),
            P("tensor"),
            P(),
            P(),
            P("tensor"),
            P("tensor"),
            P("tensor"),
            P("tensor"),
            P("tensor", None),
        ),
        check_vma=False,
    )
```

profile of v0, /device:TPU:0, one launch (start us, length us, event | category | flops | bytes accessed | tf_op | source)
XLA Modules:
  0.0 647.3 jit_solution(8219857742431929211)
XLA Ops:
  7.3 2.7 fusion.6
  12.0 1.7 copy-done.3
  14.8 2.2 reduce-window.14
  20.6 3.7 fusion.94
  24.5 4.9 fusion.37
  29.4 3.6 copy.189
  33.0 5.2 copy.238
  39.3 3.4 multiply_convert_fusion.10
  43.7 2.2 copy.195
  46.8 1.6 fusion.96
  49.1 1.4 copy-done.26
  50.5 1.2 fusion.27
  53.8 4.8 bitcast_add_fusion.1
  58.6 1.8 copy.203
  60.4 3.1 copy.242
  63.5 3.5 copy.204
  67.2 9.4 %multiply_reduce_fusion.7 = (f32[2048]{0:T(1024)S(1)}, f32[2048,384]{1,0:T(8,128)}, f32[2048,384]{1,0:T(8,128)}) fusion(f32[2048,384]{1,0:T(8,128)} %copy.204, f32[2048,384]{1,0:T(8,128)} %get-tuple-element.98, f32[384]{0:T(512)S(1)} %mul.880, bf16[2048,768]{1,0:T(8,128)(2,1)} %copy-done.3, bf16[768,384]{1,0:T(8,128)(2,1)S(1)} %copy-done), kind=kOutput, calls=%fused_computation.67 | convolution fusion | flops 1218181120 | bytes 16328192 | tf_op jit(solution)/shard_map/dot_general | solution.py:91
  76.6 8.5 %psum.133 = f32[2048]{0:T(1024)S(1)} all-reduce(f32[2048]{0:T(1024)S(1)} %get-tuple-element.89), channel_id=1, replica_groups=mesh['dp'=8,'tensor'=4] {'tensor'}, use_global_device_ids=true, to_apply=%region_4.5 | all-reduce | flops 2048 | bytes 16384 | tf_op jit(solution)/shard_map/psum | solution.py:158
  85.8 7.4 %multiply_reduce_fusion = (f32[384]{0:T(512)}, f32[2048]{0:T(1024)S(1)}, f32[2048,384]{1,0:T(8,128)}) fusion(f32[2048,384]{1,0:T(8,128)} %get-tuple-element.90, f32[2048]{0:T(1024)S(1)} %get-tuple-element.122, f32[384]{0:T(512)S(1)} %copy-done.70, bf16[384,768]{1,0:T(8,128)(2,1)} %param.35, bf16[2048,768]{1,0:T(8,128)(2,1)} %param.19, f32[2048]{0:T(1024)S(1)} %fusion.72), kind=kOutput, calls=%fused_computation.55 | convolution fusion | flops 1217394304 | bytes 10054656 | tf_op jit(solution)/shard_map/dot_general | solution.py:167
  93.2 5.8 psum.135
  99.0 9.2 %multiply_reduce_fusion.1 = (f32[384]{0:T(512)}, f32[2048,384]{1,0:T(8,128)S(1)}, bf16[2048,384]{1,0:T(8,128)(2,1)}) fusion(f32[2048,384]{1,0:T(8,128)} %get-tuple-element.98, f32[2048,384]{1,0:T(8,128)} %get-tuple-element.136, f32[2048]{0:T(1024)S(1)} %psum.135, f32[2048,384]{1,0:T(8,128)} %get-tuple-element.90, f32[2048]{0:T(1024)S(1)} %get-tuple-element.121, ...), kind=kLoop, calls=%fused_computation.56 | loop fusion | flops 20446848 | bytes 20476416 | tf_op jit(solution)/shard_map/reduce_sum | solution.py:174
  108.3 1.6 copy-done.12
  109.9 1.3 convert_element_type.108
  111.2 2.6 copy.205
  113.8 2.0 copy.243
  116.0 9.8 %fusion = (f32[8,6,256]{2,1,0:T(8,128)}, f32[8,6,256]{2,1,0:T(8,128)}, bf16[8,256,256]{2,1,0:T(8,128)(2,1)}) fusion(f32[8,6,256]{2,1,0:T(8,128)S(1)} %copy.190, f32[8,256,256]{2,1,0:T(8,128)S(1)} %copy-done.31, pred[8,256,256]{2,1,0:T(8,128)(4,1)S(1)} %copy-done.55, bf16[8,256,6,64]{1,0,3,2:T(8,128)(2,1)} %copy-done.34, ...), kind=kOutput, calls=%fused_computation.11 | convolution fusion | flops 433561600 | bytes 6963200 | tf_op jit(solution)/shard_map/cphd,cqhd->chpq/dot_general | solution.py:177
  125.8 3.7 fusion.42
  129.6 1.8 fusion.41
  131.6 1.5 multiply_reduce_fusion.13
  133.1 1.3 fusion.30
  135.0 4.9 fusion.2
  139.9 4.5 fusion.85
  144.9 4.7 fusion.15
  149.6 2.6 copy.227
  152.2 3.2 convolution_add_fusion.3
  155.5 1.4 convolution_add_fusion.2
  159.9 1.7 reduce-window.16
  162.1 1.6 rev.7
  163.7 6.3 fusion.31
  170.0 1.8 copy.209
  171.8 3.1 copy.244
  174.9 3.6 copy.210
  178.5 2.0 mul.911
  180.6 3.6 copy.211
  184.2 6.5 %fusion.86 = (f32[384]{0:T(512)S(1)}, f32[384]{0:T(512)S(1)}, f32[2048,384]{1,0:T(8,128)S(1)}) fusion(f32[2048,384]{1,0:T(8,128)} %copy-done.1, f32[2048,384]{1,0:T(8,128)} %get-tuple-element.98, f32[2048,384]{1,0:T(8,128)} %copy.210, f32[2048,384]{1,0:T(8,128)} %copy.211, f32[2048,384]{1,0:T(8,128)} %copy-done.12, f32[384]{0:T(512)S(1)} %copy-done.101), kind=kLoop, calls=%fused_computation.247 | loop fusion | flops 11009280 | bytes 18878976 | tf_op jit(solution)/shard_map/reduce_sum | solution.py:45
  190.7 2.8 multiply_reduce_fusion.4
  195.7 1.8 fusion.98
  197.7 1.8 fusion.99
  199.5 1.5 pad_maximum_fusion
  201.3 4.7 add_add_fusion
  206.1 5.3 fusion.100
  211.4 2.8 fusion.101
  214.3 2.8 fusion.43
  217.1 244.0 %all-reduce.26.cloned.1.call-done = (f32[2048,768]{1,0:T(8,128)}, f32[2048,768]{1,0:T(8,128)}, f32[2048,256]{1,0:T(8,128)}) async-done(((f32[2048,768]{1,0:T(8,128)}, f32[2048,768]{1,0:T(8,128)}, f32[2048,256]{1,0:T(8,128)}), (f32[2048,768]{1,0:T(8,128)}, f32[2048,768]{1,0:T(8,128)}, f32[2048,256]{1,0:T(8,128)})) %all-reduce.26.cloned.1.call-update) | async-done | bytes 14680080 | tf_op jit(solution)/shard_map/psum | solution.py:162
  461.2 3.1 fusion.87
  464.3 2.1 multiply_reduce_fusion.10
  468.0 1.3 copy-done.6
  469.3 4.5 fusion.103
  474.7 3.3 fusion.102
  478.1 8.3 %fusion.13 = (f32[768]{0:T(1024)S(1)}, f32[2048]{0:T(1024)S(1)}, f32[2048,768]{1,0:T(8,128)}) fusion(bf16[2048,768]{1,0:T(8,128)(2,1)S(1)} %copy-done.8, f32[2048]{0:T(1024)S(1)} %copy-done.67, f32[768]{0:T(1024)S(1)} %copy-done.78, f32[2048,768]{1,0:T(8,128)} %get-tuple-element.61, f32[2048,256]{1,0:T(8,128)S(1)} %multiply_add_fusion.2, ...), kind=kOutput, calls=%fused_computation.26 | convolution fusion | flops 4844418048 | bytes 18241536 | tf_op jit(solution)/shard_map/dot_general | solution.py:290
  486.5 40.8 %all-reduce.18 = (f32[768]{0:T(1024)}, f32[768,6]{0,1:T(8,128)}, f32[4,384]{1,0:T(4,128)}, f32[384]{0:T(512)}, f32[4,256]{1,0:T(4,128)}, /*index=5*/f32[256]{0:T...) all-reduce(f32[768]{0:T(1024)S(1)} %get-tuple-element.19, ...), channel_id=1, replica_groups=mesh['dp'=8,'tensor'=4] {'dp'}, use_global_device_ids=true, to_apply=%region_30.31 | all-reduce | flops 8978 | bytes 71824 | tf_op jit(solution)/shard_map/psum | solution.py:305
  527.3 11.3 %fusion.5 = (f32[2048,768]{1,0:T(8,128)}, bf16[2048,768]{1,0:T(8,128)(2,1)}) fusion(bf16[2048,768]{1,0:T(8,128)(2,1)} %param.19, bf16[2048,768]{1,0:T(8,128)(2,1)} %param.18, f32[2048,768]{1,0:T(8,128)} %get-tuple-element.140, f32[2048]{0:T(1024)S(1)} %broadcast_multiply_fusion.6, f32[2048]{0:T(1024)S(1)} %copy-done.79, f32[768]{0:T(1024)S(1)} %copy-done.78, ...), kind=kLoop, calls=%fused_computation.18 | loop fusion | flops 17301504 | bytes 28347392 | tf_op jit(solution)/shard_map/sub | solution.py:301
  538.6 96.2 %all-reduce.24.cloned.1.call-done = (f32[768,384]{1,0:T(8,128)}, f32[768,384]{1,0:T(8,128)}, f32[768,256]{1,0:T(8,128)}, f32[384,768]{1,0:T(8,128)}) async-done(((f32[768,384]{1,0:T(8,128)}, f32[768,384]{1,0:T(8,128)}, f32[768,256]{1,0:T(8,128)}, f32[384,768]{1,0:T(8,128)}), (f32[768,384]{1,0:T(8,128)}, f32[768,384]{1,0:T(8,128)}, f32[768,256]{1,0:T(8,128)}, ...) | async-done | bytes 4325392 | tf_op jit(solution)/shard_map/psum | solution.py:305
  634.8 2.5 copy.314
  (369 shorter events, 24.9 us)
Async XLA Ops:
  7.2 60.0 %copy-start = (bf16[768,384]{1,0:T(8,128)(2,1)S(1)}, bf16[768,384]{1,0:T(8,128)(2,1)}, u32[]{:S(2)}) copy-start(bf16[768,384]{1,0:T(8,128)(2,1)} %param.24) | copy-start | bytes 1769476
  7.2 4.0 copy-start.77
  7.2 453.9 %all-reduce.26.cloned.1.call-start = ((), (), s32[]{:S(2)}) async-start(), calls=%async_computation.1 | async-start | bytes 29360128 | tf_op jit(solution)/shard_map/psum | solution.py:162
  10.6 4.0 copy-start.121
  13.7 6.9 %copy-start.52 = (bf16[768,384]{1,0:T(8,128)(2,1)S(1)}, bf16[768,384]{1,0:T(8,128)(2,1)}, u32[]{:S(2)}) copy-start(bf16[768,384]{1,0:T(8,128)(2,1)} %param.23) | copy-start | bytes 1769476
  14.6 9.7 %copy-start.46 = (f32[2048,6]{0,1:T(8,128)}, f32[2048,6]{0,1:T(8,128)S(1)}, u32[]{:S(2)}) copy-start(f32[2048,6]{0,1:T(8,128)S(1)} %get-tuple-element.135) | copy-start | bytes 147460
  14.7 23.5 %copy-start.44 = (f32[2048,6]{0,1:T(8,128)}, f32[2048,6]{0,1:T(8,128)S(1)}, u32[]{:S(2)}) copy-start(f32[2048,6]{0,1:T(8,128)S(1)} %get-tuple-element.134) | copy-start | bytes 147460
  24.3 5.1 copy-start.1
  24.4 5.0 copy-start.86
  24.4 5.0 copy-start.88
  24.4 5.0 copy-start.90
  24.4 5.0 copy-start.92
  24.5 14.8 %copy-start.58 = (f32[2048]{0:T(1024)}, f32[2048]{0:T(1024)S(1)}, u32[]{:S(2)}) copy-start(f32[2048]{0:T(1024)S(1)} %get-tuple-element.125) | copy-start | bytes 24580
  24.5 14.8 %copy-start.60 = (f32[2048]{0:T(1024)}, f32[2048]{0:T(1024)S(1)}, u32[]{:S(2)}) copy-start(f32[2048]{0:T(1024)S(1)} %get-tuple-element.126) | copy-start | bytes 24580
  24.5 14.8 %copy-start.62 = (f32[2048]{0:T(1024)}, f32[2048]{0:T(1024)S(1)}, u32[]{:S(2)}) copy-start(f32[2048]{0:T(1024)S(1)} %get-tuple-element.127) | copy-start | bytes 24580
  33.0 5.2 copy-start.4
  33.0 5.2 copy-start.36
  46.8 4.9 copy-start.115
  46.8 5.2 copy-start.80
  46.8 5.2 copy-start.97
  46.8 5.5 copy-start.83
  46.8 5.5 copy-start.94
  46.8 5.6 copy-start.104
  48.5 5.3 copy-start.30
  49.0 4.8 copy-start.34
  53.1 5.5 copy-start.19
  53.2 62.7 %copy-start.73 = (f32[8,6,256]{2,1,0:T(8,128)}, f32[8,6,256]{2,1,0:T(8,128)S(1)}, u32[]{:S(2)}) copy-start(f32[8,6,256]{2,1,0:T(8,128)S(1)} %copy.190) | copy-start | bytes 147460
  53.7 4.9 copy-start.54
  67.2 31.8 %copy-start.100 = (f32[384]{0:T(512)}, f32[384]{0:T(512)S(1)}, u32[]{:S(2)}) copy-start(f32[384]{0:T(512)S(1)} %mul.880) | copy-start | bytes 4612
  67.2 18.5 %copy-start.70 = (f32[384]{0:T(512)S(1)}, f32[384]{0:T(512)}, u32[]{:S(2)}) copy-start(f32[384]{0:T(512)} %param.34) | copy-start | bytes 4612
  85.7 7.4 %copy-start.68 = (f32[2048]{0:T(1024)}, f32[2048]{0:T(1024)S(1)}, u32[]{:S(2)}) copy-start(f32[2048]{0:T(1024)S(1)} %fusion.72) | copy-start | bytes 24580
  116.0 9.8 %copy-start.43 = (bf16[8,6,128,64]{2,3,1,0:T(8,128)(2,1)S(1)}, bf16[8,6,128,64]{2,3,1,0:T(8,128)(2,1)}, u32[]{:S(2)}) copy-start(bf16[8,6,128,64]{2,3,1,0:T(8,128)(2,1)} %copy-done.42) | copy-start | bytes 2359300
  125.8 5.6 copy-start.81
  125.8 5.6 copy-start.84
  125.8 5.6 copy-start.95
  125.8 5.6 copy-start.98
  125.8 5.6 copy-start.102
  125.8 5.6 copy-start.105
  125.8 5.6 copy-start.116
  131.3 13.4 %copy-start.16 = (f32[8,6,128,64]{2,3,1,0:T(8,128)}, f32[8,6,128,64]{2,3,1,0:T(8,128)S(1)}, u32[]{:S(2)}) copy-start(f32[8,6,128,64]{2,3,1,0:T(8,128)S(1)} %fusion.41) | copy-start | bytes 4718596
  135.0 4.9 copy-start.9
  135.0 4.9 copy-start.51
  139.9 4.9 copy-start.27
  139.9 4.9 copy-start.35
  144.8 4.7 copy-start.32
  152.1 4.7 copy-start.17
  152.1 4.7 copy-start.23
  152.1 4.7 copy-start.33
  152.1 4.7 copy-start.85
  152.2 4.7 copy-start.96
  184.1 6.5 %copy-start.2 = (f32[2048,384]{1,0:T(8,128)S(1)}, f32[2048,384]{1,0:T(8,128)}, u32[]{:S(2)}) copy-start(f32[2048,384]{1,0:T(8,128)} %copy-done.1) | copy-start | bytes 9437188
  184.1 6.5 %copy-start.59 = (f32[2048]{0:T(1024)S(1)}, f32[2048]{0:T(1024)}, u32[]{:S(2)}) copy-start(f32[2048]{0:T(1024)} %copy-done.58) | copy-start | bytes 24580
  184.1 6.5 %copy-start.61 = (f32[2048]{0:T(1024)S(1)}, f32[2048]{0:T(1024)}, u32[]{:S(2)}) copy-start(f32[2048]{0:T(1024)} %copy-done.60) | copy-start | bytes 24580
  184.2 6.5 %copy-start.63 = (f32[2048]{0:T(1024)S(1)}, f32[2048]{0:T(1024)}, u32[]{:S(2)}) copy-start(f32[2048]{0:T(1024)} %copy-done.62) | copy-start | bytes 24580
  206.0 428.8 %all-reduce.24.cloned.1.call-start = ((), (), s32[]{:S(2)}) async-start(), calls=%async_computation | async-start | bytes 8650752 | tf_op jit(solution)/shard_map/psum | solution.py:305
  206.1 5.4 copy-start.5
  206.1 5.4 copy-start.14
  206.1 8.2 %copy-start.18 = (bf16[2048,768]{1,0:T(8,128)(2,1)S(1)}, bf16[2048,768]{1,0:T(8,128)(2,1)}, u32[]{:S(2)}) copy-start(bf16[2048,768]{1,0:T(8,128)(2,1)} %param.19) | copy-start | bytes 9437188
  473.8 4.3 copy-start.37
  473.8 4.3 copy-start.67
  473.8 4.3 copy-start.78
  478.1 8.4 %copy-start.124 = (f32[384]{0:T(512)S(1)}, f32[384]{0:T(512)}, u32[]{:S(2)}) copy-start(f32[384]{0:T(512)} %get-tuple-element.21) | copy-start | bytes 4612
  478.1 49.2 %copy-start.79 = (f32[2048]{0:T(1024)S(1)}, f32[2048]{0:T(1024)}, u32[]{:S(2)}) copy-start(f32[2048]{0:T(1024)} %get-tuple-element.119) | copy-start | bytes 24580
  634.8 4.4 copy-start.38
  (69 other events, 153.7 us)
Sparse Core Ops, SparseCore 0:
  206.1 254.9 all-reduce.25
  473.9 160.7 all-reduce.23
where the time goes:
time: 650 us; the launch traced here: 647 us
  waiting for transfers between devices  340 us (52%)
  matrix products  107 us (16%)
  other arithmetic  64.6 us (10%)
  local copies, waits for them, and re-layouts  64 us (10%)
  blocking collectives  55.1 us (8%)
  between operations  16.7 us (3%)
    psum x1, waiting for transfers between devices, per_device(): lax.psum(jnp.dot(out_in, w_out, preferred_element_type=jnp.float32), 'ten...  244 us
    psum x1, waiting for transfers between devices, per_device(): lax.psum((grad_norm_gain, grad_w_x, grad_w_z, grad_w_dt, grad_conv_x, gra...  96.2 us
    psum x1, blocking collectives, per_device(): lax.psum((grad_norm_gain, grad_w_x, grad_w_z, grad_w_dt, grad_conv_x, gra...  40.8 us
    unnamed x284, local copies, waits for them, and re-layouts  29.6 us
  transfers between devices with their start and end apart: 2, of which 2 were waited for; matrix products, arithmetic and copies ran while one was open for 5% of the time, Pallas kernels for 0%

commit v1 on v0

--- a/solution.py
+++ b/solution.py
@@ -1,3 +1,5 @@
+import functools
+
 import jax
 import jax.numpy as jnp
 from jax import lax
@@ -49,7 +51,71 @@
     return (grad_weight, grad_bias, grad_values)
 
 
+def partners(count, step):
+    return [(place, place ^ step) for place in range(count)]
+
+
+def steps_of(count):
+    return [1 << level for level in range((count - 1).bit_length())]
+
+
+def axis_sum_small(values, axis, count):
+    for step in steps_of(count):
+        values = values + lax.ppermute(values, axis, partners(count, step))
+    return values
+
+
+def take_half(values, which):
+    half = values.shape[0] // 2
+    return lax.dynamic_slice_in_dim(values, which * half, half, 0)
+
+
+def axis_scatter(values, axis, count, order):
+    place = lax.axis_index(axis)
+    for step in order:
+        mine = (place // step) % 2
+        sent = lax.ppermute(take_half(values, 1 - mine), axis, partners(count, step))
+        values = take_half(values, mine) + sent
+    return values
+
+
+def axis_gather(values, axis, count, order):
+    place = lax.axis_index(axis)
+    for step in reversed(order):
+        mine = (place // step) % 2
+        other = lax.ppermute(values, axis, partners(count, step))
+        values = join_halves(values, other, mine)
+    return values
+
+
+def join_halves(own, other, mine):
+    return jnp.where(
+        mine == 0, jnp.concatenate([own, other], 0), jnp.concatenate([other, own], 0)
+    )
+
+
+def dp_sum(values, count, first):
+    order = steps_of(count)
+    order = order[first:2] + order[:first] + order[2:]
+    return axis_gather(axis_scatter(values, "dp", count, order), "dp", count, order)
+
+
+def wide_tensor_sum(compute, count):
+    mine = lax.axis_index("tensor") % 2
+    values = compute(mine) + lax.ppermute(compute(1 - mine), "tensor", partners(count, 1))
+    for step in steps_of(count)[1:]:
+        values = values + lax.ppermute(values, "tensor", partners(count, step))
+    return values, lax.ppermute(values, "tensor", partners(count, 1)), mine
+
+
+def pad_rows(values, multiple):
+    missing = -values.shape[0] % multiple
+    return jnp.pad(values, ((0, missing), (0, 0)))
+
+
 def per_device(
+    n_dp,
+    n_tensor,
     hidden,
     cotangent,
     seg_ids,
@@ -155,19 +221,31 @@
     y_flat = (scanned + d_skip[None, :, None] * x_heads).reshape(row_count, width_here)
     z_active = jax.nn.silu(proj_z)
     gated_out = y_flat * z_active
-    squares = lax.psum(jnp.sum(gated_out * gated_out, -1), "tensor")
+    grad_out = cotangent.astype(jnp.float32)
+    grad_mix = (live_rows * grad_out).astype(jnp.bfloat16)
+    grad_in = jnp.dot(grad_mix, w_out.T, preferred_element_type=jnp.float32)
+    grad_scaled = grad_in * gate_gain
+    row_sums = axis_sum_small(
+        jnp.stack([jnp.sum(gated_out * gated_out, -1), jnp.sum(grad_scaled * gated_out, -1)], 0),
+        "tensor",
+        n_tensor,
+    )
+    squares, cross_sum = row_sums[0], row_sums[1]
     inv_gate = lax.rsqrt(squares[:, None] / INNER + EPS)
     scaled = gated_out * inv_gate
     out_in = (scaled * gate_gain).astype(jnp.bfloat16)
-    mixed = lax.psum(jnp.dot(out_in, w_out, preferred_element_type=jnp.float32), "tensor")
+    half_rows = row_count // 2
+
+    def mixed_half(which):
+        rows = lax.dynamic_slice_in_dim(out_in, which * half_rows, half_rows, 0)
+        return jnp.dot(rows, w_out, preferred_element_type=jnp.float32)
+
+    mixed = join_halves(*wide_tensor_sum(mixed_half, n_tensor))
     output = (hidden_wide + live_rows * mixed).astype(jnp.bfloat16)
-    grad_out = cotangent.astype(jnp.float32)
-    grad_mix = (live_rows * grad_out).astype(jnp.bfloat16)
-    grad_w_out = jnp.dot(out_in.T, grad_mix, preferred_element_type=jnp.float32)
-    grad_in = jnp.dot(grad_mix, w_out.T, preferred_element_type=jnp.float32)
+    grad_w_out = dp_sum(
+        jnp.dot(out_in.T, grad_mix, preferred_element_type=jnp.float32), n_dp, 0
+    )
     grad_gate_gain = jnp.sum(grad_in * scaled, 0)
-    grad_scaled = grad_in * gate_gain
-    cross_sum = lax.psum(jnp.sum(grad_scaled * gated_out, -1), "tensor")
     grad_gated = inv_gate * grad_scaled - gated_out * inv_gate**3 * cross_sum[:, None] / INNER
     grad_y = (grad_gated * z_active).reshape(row_count, heads_here, head_size)
     grad_z = (grad_gated * y_flat * silu_grad(proj_z)).astype(jnp.bfloat16)
@@ -265,83 +343,104 @@
     grad_conv_x, grad_conv_x_bias, grad_proj_x = conv_back(proj_x, conv_x, conv_masks, grad_x_pre)
     grad_proj_low = grad_proj_x.astype(jnp.bfloat16)
     grad_w_x = jnp.dot(normed.T, grad_proj_low, preferred_element_type=jnp.float32)
-    grad_w_z = jnp.dot(normed.T, grad_z, preferred_element_type=jnp.float32)
+    part_w_z = jnp.dot(normed.T, grad_z, preferred_element_type=jnp.float32)
+    grad_w_z = dp_sum(part_w_z, n_dp, 1)
     grad_w_dt = jnp.dot(
         normed_wide.T, grad_dt_in, precision=highest, preferred_element_type=jnp.float32
     )
-    partial_in = (
-        jnp.dot(grad_proj_low, w_x.T, preferred_element_type=jnp.float32)
-        + jnp.dot(grad_z, w_z.T, preferred_element_type=jnp.float32)
-        + jnp.dot(
-            grad_dt_in,
-            w_dt.astype(jnp.float32).T,
-            precision=highest,
-            preferred_element_type=jnp.float32,
-        )
-    )
-    bc_total = lax.psum(grad_bc, "tensor")
-    grad_bc_pre = bc_total * silu_grad(bc_pre)
+    grad_bc_pre = grad_bc * silu_grad(bc_pre)
     grad_conv_bc, grad_conv_bc_bias, grad_proj_bc = conv_back(
         proj_bc, conv_bc, conv_masks, grad_bc_pre
     )
-    grad_w_bc = jnp.dot(
-        normed_wide.T, grad_proj_bc, precision=highest, preferred_element_type=jnp.float32
-    )
-    from_state = jnp.dot(
-        grad_proj_bc,
-        w_bc.astype(jnp.float32).T,
-        precision=highest,
-        preferred_element_type=jnp.float32,
-    )
-    summed_in = lax.psum(partial_in, "tensor")
-    grad_normed = summed_in + from_state
+    grad_bc_low = grad_proj_bc.astype(jnp.bfloat16)
+    grad_w_bc = jnp.dot(normed.T, grad_bc_low, preferred_element_type=jnp.float32)
+    low_all = jnp.concatenate(
+        [grad_proj_low, grad_z, grad_bc_low, grad_dt_in.astype(jnp.bfloat16)], 1
+    )
+    w_all = jnp.concatenate([w_x, w_z, w_bc, w_dt], 1)
+
+    def in_half(which):
+        rows = lax.dynamic_slice_in_dim(low_all, which * half_rows, half_rows, 0)
+        return jnp.dot(rows, w_all.T, preferred_element_type=jnp.float32)
+
+    own_in, other_in, mine = wide_tensor_sum(in_half, n_tensor)
+    grad_normed = join_halves(own_in, other_in, mine)
     weighted = grad_normed * norm_gain
-    grad_norm_gain = jnp.sum(grad_normed * hidden_wide * inv_rms, 0)
+    grad_norm_gain = (
+        jnp.sum(grad_w_x * w_x.astype(jnp.float32), 1)
+        + jnp.sum(part_w_z * w_z.astype(jnp.float32), 1)
+        + jnp.sum(grad_w_dt * w_dt.astype(jnp.float32), 1)
+        + jnp.sum(grad_w_bc * w_bc.astype(jnp.float32), 1)
+    ) / norm_gain
     grad_hidden = (
         grad_out
         + inv_rms * weighted
         - hidden_wide * inv_rms**3 * jnp.mean(weighted * hidden_wide, -1, keepdims=True)
     )
-    main_sums = lax.psum(
-        (
-            grad_norm_gain,
+    model_width = hidden.shape[1]
+    bc_width = w_bc.shape[1]
+    bc_parts = jnp.concatenate(
+        [
+            grad_w_bc,
+            grad_conv_bc,
+            grad_conv_bc_bias[None],
+            grad_norm_gain.reshape(-1, bc_width),
+        ],
+        0,
+    )
+    bc_parts = pad_rows(bc_parts, 16 * n_dp)
+    order = steps_of(n_dp)
+    order = order[1:2] + order[:1] + order[2:]
+    bc_parts = axis_scatter(bc_parts, "tensor", n_tensor, [1])
+    bc_parts = axis_scatter(bc_parts, "dp", n_dp, order)
+    for step in steps_of(n_tensor)[1:]:
+        bc_parts = bc_parts + lax.ppermute(bc_parts, "tensor", partners(n_tensor, step))
+    bc_parts = axis_gather(bc_parts, "dp", n_dp, order)
+    bc_parts = axis_gather(bc_parts, "tensor", n_tensor, [1])
+    conv_at = model_width + tap_count
+    head_parts = jnp.stack([grad_dt_bias, grad_a_log, grad_d_skip], 0).reshape(1, -1)
+    head_parts = jnp.pad(head_parts, ((0, 0), (0, width_here - head_parts.shape[1])))
+    dt_parts = jnp.pad(grad_w_dt.T, ((0, 0), (0, -model_width % width_here)))
+    x_parts = jnp.concatenate(
+        [
             grad_w_x,
-            grad_w_z,
-            grad_w_dt,
             grad_conv_x,
-            grad_conv_x_bias,
-            grad_dt_bias,
-            grad_a_log,
-            grad_d_skip,
-            grad_gate_gain,
-            grad_w_out,
-        ),
-        "dp",
-    )
-    state_sums = lax.psum((grad_w_bc, grad_conv_bc, grad_conv_bc_bias), "dp")
+            grad_conv_x_bias[None],
+            grad_gate_gain[None],
+            head_parts,
+            dt_parts.reshape(-1, width_here),
+        ],
+        0,
+    )
+    x_parts = dp_sum(pad_rows(x_parts, 8 * n_dp), n_dp, 0)
+    at = model_width + tap_count
+    heads_sum = x_parts[at + 2, : 3 * heads_here].reshape(3, heads_here)
+    dt_rows = dt_parts.size // width_here
+    dt_sum = x_parts[at + 3 : at + 3 + dt_rows].reshape(heads_here, -1)[:, :model_width].T
+    norm_rows = model_width // bc_width
     return (
         output,
         grad_hidden,
-        main_sums[0],
-        main_sums[1],
-        main_sums[2],
-        main_sums[3],
-        state_sums[0],
-        main_sums[4],
-        main_sums[5],
-        state_sums[1],
-        state_sums[2],
-        main_sums[6],
-        main_sums[7],
-        main_sums[8],
-        main_sums[9],
-        main_sums[10],
+        bc_parts[conv_at + 1 : conv_at + 1 + norm_rows].reshape(-1),
+        x_parts[:model_width],
+        grad_w_z,
+        dt_sum,
+        bc_parts[:model_width],
+        x_parts[model_width:at],
+        x_parts[at],
+        bc_parts[model_width:conv_at],
+        bc_parts[conv_at],
+        heads_sum[0],
+        heads_sum[1],
+        heads_sum[2],
+        x_parts[at + 1],
+        grad_w_out,
     )
 
 
 def solution(mesh):
     return jax.shard_map(
-        per_device,
+        functools.partial(per_device, mesh.shape["dp"], mesh.shape["tensor"]),
         mesh=mesh,
         in_specs=(
             P("dp", None),

time: 650 us -> 497 us (0.76)
  waiting for transfers between devices: 340 us -> 169 us
  blocking collectives: 55.1 us -> 0 us
  other arithmetic: 64.6 us -> 103 us
  starting transfers between devices: 0.08 us -> 33.8 us
  local copies, waits for them, and re-layouts: 64 us -> 87.7 us
  matrix products: 107 us -> 91.3 us
  between operations: 16.7 us -> 3.98 us
    psum x2 -> x0, waiting for transfers between devices: 340 us -> none  [the longest x1 244 us: per_device(): lax.psum(jnp.dot(out_in, w_out, preferred_element_type=jnp.float32), 'ten...]
    ppermute x0 -> x35, waiting for transfers between devices: none -> 169 us  [the longest x1 109 us: per_device(): lax.ppermute(bc_parts, 'tensor', partners(n_tensor, step))]
    psum x3 -> x0, blocking collectives: 55.1 us -> none  [the longest x1 40.8 us: per_device(): lax.psum((grad_norm_gain, grad_w_x, grad_w_z, grad_w_dt, grad_conv_x, gra...]
    ppermute x0 -> x35, starting transfers between devices: none -> 33.8 us  [the longest x13 16.4 us: axis_scatter(): lax.ppermute(take_half(values, 1 - mine), axis, partners(count, step))]
    dot_general x8 -> x7, matrix products: 31.4 us -> 19.3 us  [the longest x2 9.02 us: in_half(): return jnp.dot(rows, w_all.T, preferred_element_type=jnp.float32)]
    another operation x8, local copies, waits for them, and re-layouts: 0.73 us -> 10.5 us  [per_device(): hop_terms = jnp.stack(hop_grads[::-1], 0) * hop]
    select_n x0 -> x13, other arithmetic: none -> 9.29 us  [join_halves(): jnp.where(mine == 0, jnp.concatenate([own, other], 0), jnp.concatenate([o...]
    mul x3 -> x0, local copies, waits for them, and re-layouts: 9.16 us -> none  [the longest x2 5.6 us: per_device(): inputs = (step_size[:, :, None] * x_heads).astype(jnp.bfloat16)]
  transfers between devices with their start and end apart: 2 -> 35, of which waited for: 2 -> 16; matrix products, arithmetic and copies ran while one was open for 5% -> 31% of each run, Pallas kernels for 0% -> 0%
where the time goes in v1:
time: 497 us; the launch traced here: 489 us
  waiting for transfers between devices  169 us (34%)
  other arithmetic  103 us (21%)
  matrix products  91.3 us (18%)
  local copies, waits for them, and re-layouts  87.7 us (18%)
  starting transfers between devices  33.8 us (7%)
    ppermute x1, waiting for transfers between devices, per_device(): lax.ppermute(bc_parts, 'tensor', partners(n_tensor, step))  109 us
    ppermute x13, waiting for transfers between devices, axis_gather(): other = lax.ppermute(values, axis, partners(count, step))  42.2 us
    unnamed x310, local copies, waits for them, and re-layouts  31.9 us
    ppermute x13, waiting for transfers between devices, axis_scatter(): lax.ppermute(take_half(values, 1 - mine), axis, partners(count, step))  17.3 us
    ppermute x13, starting transfers between devices, axis_scatter(): lax.ppermute(take_half(values, 1 - mine), axis, partners(count, step))  16.4 us
    sub x1, other arithmetic, per_device(): grad_out + inv_rms * weighted  15.4 us
    another operation x8, local copies, waits for them, and re-layouts, per_device(): hop_terms = jnp.stack(hop_grads[::-1], 0) * hop  10.5 us
    dot_general x1, matrix products, per_device(): grad_in = jnp.dot(grad_mix, w_out.T, preferred_element_type=jnp.float32)  10.1 us
  transfers between devices with their start and end apart: 35, of which 16 were waited for; matrix products, arithmetic and copies ran while one was open for 31% of the time, Pallas kernels for 0%

profile of v1, /device:TPU:0, one launch (start us, length us, event | category | flops | bytes accessed | tf_op | source)
XLA Modules:
  0.0 488.7 jit_solution(8097849030897710192)
XLA Ops:
  0.7 2.7 fusion.6
  13.4 3.4 fusion.112
  17.0 4.4 fusion.38
  21.5 3.1 copy.290
  25.8 3.7 multiply_convert_fusion.10
  35.2 2.3 copy.237
  37.7 3.0 multiply_convert_fusion.9
  45.1 4.5 bitcast_add_fusion.1
  51.4 3.1 copy.296
  54.5 3.2 fusion.116
  58.6 10.1 %multiply_reduce_fusion.8 = (f32[2048]{0:T(1024)S(1)}, f32[2048]{0:T(1024)S(1)}, f32[2048,384]{0,1:T(8,128)}, f32[2048,384]{0,1:T(8,128)}) fusion(f32[384]{0:T(512)S(1)} %copy-done.133, f32[2048,384]{0,1:T(8,128)} %fusion.116, f32[2048,384]{0,1:T(8,128)} %bitcast.301, f32[2048,384]{0,1:T(8,128)} %get-tuple-element.80, f32[384]{0:T(512)S(1)} %mul.967, ...), kind=kOutput, calls=%fused_computation.68 | convolution fusion | flops 1225256960 | bytes 19491840 | tf_op jit(solution)/shard_map/dot_general | solution.py:226
  70.1 2.9 collective-permute-start.1
  74.8 8.8 %multiply_reduce_fusion = (f32[384]{0:T(512)}, f32[2048,384]{0,1:T(8,128)S(1)}, bf16[2048,384]{0,1:T(8,128)(2,1)}, f32[384]{0:T(512)}, bf16[2048,384]{0,1:T(8,128)(2,1)S(1)}) fusion(f32[2048,384]{0,1:T(8,128)} %get-tuple-element.80, f32[2048,384]{0,1:T(8,128)} %fusion.116, f32[2048]{0:T(1024)S(1)} %bitcast.342, f32[2048,384]{0,1:T(8,128)} %get-tuple-element.72, ...), kind=kLoop, calls=%fused_computation.56 | loop fusion | flops 24378624 | bytes 22050816 | tf_op jit(solution)/shard_map/reduce_sum | solution.py:252
  85.4 1.9 copy-done.15
  88.6 1.9 fusion.49
  92.5 9.5 %fusion = (f32[8,6,256]{2,1,0:T(8,128)}, f32[8,6,256]{2,1,0:T(8,128)}, bf16[8,256,256]{2,1,0:T(8,128)(2,1)}) fusion(f32[8,6,256]{2,1,0:T(8,128)S(1)} %copy-done.77, f32[8,256,256]{2,1,0:T(8,128)S(1)} %copy-done.34, pred[8,256,256]{2,1,0:T(8,128)(4,1)S(1)} %copy-done.53, bf16[8,256,6,64]{1,3,2,0:T(8,128)(2,1)S(1)} %copy-done.38, ...), kind=kOutput, calls=%fused_computation.10 | convolution fusion | flops 433561600 | bytes 6963200 | tf_op jit(solution)/shard_map/cphd,cqhd->chpq/dot_general | solution.py:255
  102.1 4.9 fusion.2
  107.0 3.8 fusion.50
  113.3 2.1 collective-permute-start.29
  138.0 6.7 %fusion.14 = (f32[8,256,128]{1,2,0:T(8,128)}, f32[8,256,6]{1,2,0:T(8,128)S(1)}) fusion(f32[8,256,6]{1,2,0:T(8,128)S(1)} %get-tuple-element.103, f32[8,256,128]{1,2,0:T(8,128)} %copy.242, bf16[8,256,6,64]{1,3,2,0:T(8,128)(2,1)} %copy-done.37, f32[8,6,128,64]{2,3,1,0:T(8,128)} %broadcast_dynamic-update-slice_fusion), kind=kOutput, calls=%fused_computation.30 | convolution fusion | flops 1213976576 | bytes 5341184 | tf_op jit(solution)/shard_map/chnd,cqhd->cqhn/dot_general | solution.py:307
  156.8 6.4 %multiply_reduce_fusion.6 = (f32[8,256,6]{1,2,0:T(8,128)S(1)}, f32[8,256,6,64]{1,3,2,0:T(8,128)S(1)}) fusion(f32[8,256,6,64]{1,0,3,2:T(8,128)} %bitcast.294, f32[8,6,128,64]{2,3,1,0:T(8,128)} %broadcast_dynamic-update-slice_fusion, f32[8,256,6]{1,2,0:T(8,128)S(1)} %get-tuple-element.103, f32[8,256,128]{1,2,0:T(8,128)} %copy.242, f32[8,6,64,256]{3,2,1,0:T(8,128)} %fusion.2), kind=kOutput, calls=%fused_computation.62 | convolution fusion | flops 1213452288 | bytes 12156928 | tf_op jit(solution)/shard_map/chnd,cqhn->cqhd/dot_general | solution.py:314
  167.9 3.1 multiply_reduce_fusion.2
  171.0 4.4 fusion.102
  175.4 2.6 slice.366
  178.0 2.6 slice.367
  180.6 2.5 slice.368
  183.1 2.5 copy.259
  185.6 3.0 convolution_add_fusion.3
  188.6 2.6 copy.286
  191.2 3.1 convolution_add_fusion.2
  194.3 2.5 copy.287
  196.9 4.1 multiply_reduce_fusion.9
  200.9 2.5 fusion.103
  213.1 4.0 fusion.39
  217.2 2.7 fusion.60
  221.5 1.9 multiply_reduce_fusion.13
  227.6 3.4 multiply_reduce_fusion.24
  231.2 4.0 multiply_reduce_fusion.14
  236.5 3.6 concatenate.207
  241.5 5.0 %fusion.43 = f32[1024,768]{1,0:T(8,128)S(1)} fusion(f32[1024,768]{1,0:T(8,128)} %collective-permute-done.5, bf16[2048,1030]{0,1:T(8,128)(2,1)} %copy-done.30, s32[]{:T(128)S(6)} %select_n.334, bf16[768,6]{1,0:T(8,128)(2,1)S(1)} %copy-done.69, bf16[768,256]{1,0:T(8,128)(2,1)S(1)} %copy-done.57, bf16[768,384]{1,0:T(8,128)(2,1)S(1)} %copy-done.142, ...), kind=kOutput, calls=%fused_computation.97 | convolution fusion | flops 1627164672 | bytes 9987076 | tf_op jit(solution)/shard_map/dot_general | solution.py:364
  251.9 2.9 convolution_add_fusion.1
  257.7 8.3 %collective-permute-done.10 = f32[112,256]{1,0:T(8,128)S(1)} collective-permute-done((f32[112,256]{1,0:T(8,128)S(1)}, f32[112,256]{1,0:T(8,128)S(1)}, u32[]{:S(2)}, u32[]{:S(2)}) %collective-permute-start.10) | collective-permute-done | bytes 114720 | tf_op jit(solution)/shard_map/ppermute | solution.py:77
  266.1 2.7 collective-permute-start.11
  268.8 3.2 collective-permute-done.11
  273.9 2.8 collective-permute-start.31
  276.8 108.8 %collective-permute-done.12 = f32[56,256]{1,0:T(8,128)S(1)} collective-permute-done((f32[56,256]{1,0:T(8,128)S(1)}, f32[56,256]{1,0:T(8,128)S(1)}, u32[]{:S(2)}, u32[]{:S(2)}) %collective-permute-start.12) | collective-permute-done | bytes 57376 | tf_op jit(solution)/shard_map/ppermute | solution.py:397
  385.5 2.6 collective-permute-start.25
  388.5 2.0 add.582
  390.6 6.6 %collective-permute-done.13 = f32[56,256]{1,0:T(8,128)S(1)} collective-permute-done((f32[56,256]{1,0:T(8,128)S(1)}, f32[56,256]{1,0:T(8,128)S(1)}, u32[]{:S(2)}, u32[]{:S(2)}) %collective-permute-start.13) | collective-permute-done | bytes 57376 | tf_op jit(solution)/shard_map/ppermute | solution.py:86
  398.1 3.0 collective-permute-start.32
  402.4 2.7 collective-permute-start.26
  405.5 2.1 add.541
  407.6 5.7 %collective-permute-done.19 = f32[104,384]{1,0:T(8,128)S(1)} collective-permute-done((f32[104,384]{1,0:T(8,128)S(1)}, f32[104,384]{1,0:T(8,128)S(1)}, u32[]{:S(2)}, u32[]{:S(2)}) %collective-permute-start.19) | collective-permute-done | bytes 159776 | tf_op jit(solution)/shard_map/ppermute | solution.py:77
  413.4 3.1 collective-permute-done.32
  416.5 6.5 %collective-permute-done.26 = f32[96,384]{1,0:T(8,128)S(1)} collective-permute-done((f32[96,384]{1,0:T(8,128)S(1)}, f32[96,384]{1,0:T(8,128)S(1)}, u32[]{:S(2)}, u32[]{:S(2)}) %collective-permute-start.26) | collective-permute-done | bytes 147488 | tf_op jit(solution)/shard_map/ppermute | solution.py:86
  423.1 2.3 collective-permute-start.27
  426.5 6.2 %collective-permute-done.33 = f32[96,768]{1,0:T(8,128)S(1)} collective-permute-done((f32[96,768]{1,0:T(8,128)S(1)}, f32[96,768]{1,0:T(8,128)S(1)}, u32[]{:S(2)}, u32[]{:S(2)}) %collective-permute-start.33) | collective-permute-done | bytes 294944 | tf_op jit(solution)/shard_map/ppermute | solution.py:86
  433.7 8.3 %collective-permute-done.21 = f32[208,384]{1,0:T(8,128)S(1)} collective-permute-done((f32[208,384]{1,0:T(8,128)S(1)}, f32[208,384]{1,0:T(8,128)S(1)}, u32[]{:S(2)}, u32[]{:S(2)}) %collective-permute-start.21) | collective-permute-done | bytes 319520 | tf_op jit(solution)/shard_map/ppermute | solution.py:86
  449.1 2.4 maximum_select_fusion.4
  451.5 5.2 %collective-permute-done.28 = f32[384,384]{1,0:T(8,128)} collective-permute-done((f32[384,384]{1,0:T(8,128)}, f32[384,384]{1,0:T(8,128)}, u32[]{:S(2)}, u32[]{:S(2)}) %collective-permute-start.28) | collective-permute-done | bytes 589856 | tf_op jit(solution)/shard_map/ppermute | solution.py:86
  456.7 2.8 maximum_select_fusion.3
  459.5 2.2 collective-permute-done.22
  466.6 6.2 %fusion.11 = f32[2048]{0:T(1024)S(1)} fusion(bf16[2048,768]{1,0:T(8,128)(2,1)} %param.18, f32[1024,768]{1,0:T(8,128)} %add.582, f32[1024,768]{1,0:T(8,128)} %collective-permute-done.7, f32[768]{0:T(1024)S(1)} %copy-done.75, pred[]{:T(512)S(6)} %eq.118), kind=kLoop, calls=%fused_computation.23 | loop fusion | flops 11008000 | bytes 9448449 | tf_op jit(solution)/shard_map/reduce_sum | solution.py:378
  472.9 15.4 %fusion.5 = (f32[2048,768]{1,0:T(8,128)}, bf16[2048,768]{1,0:T(8,128)(2,1)}) fusion(bf16[2048,768]{1,0:T(8,128)(2,1)} %param.19, bf16[2048,768]{1,0:T(8,128)(2,1)} %param.18, f32[1024,768]{1,0:T(8,128)} %add.582, f32[1024,768]{1,0:T(8,128)} %collective-permute-done.7, f32[2048]{0:T(1024)S(1)} %broadcast_multiply_fusion.6, f32[2048]{0:T(1024)S(1)} %copy-done.78, ...), kind=kLoop, calls=%fused_computation.17 | loop fusion | flops 26738688 | bytes 28347392 | tf_op jit(solution)/shard_map/sub | solution.py:376
  (521 shorter events, 118.2 us)
Async XLA Ops:
  0.6 57.9 %copy-start = (bf16[384,768]{1,0:T(8,128)(2,1)S(1)}, bf16[384,768]{1,0:T(8,128)(2,1)}, u32[]{:S(2)}) copy-start(bf16[384,768]{1,0:T(8,128)(2,1)} %param.35) | copy-start | bytes 1769476
  7.1 6.3 %copy-start.137 = (bf16[768,384]{1,0:T(8,128)(2,1)S(1)}, bf16[768,384]{1,0:T(8,128)(2,1)}, u32[]{:S(2)}) copy-start(bf16[768,384]{1,0:T(8,128)(2,1)} %param.23) | copy-start | bytes 1769476
  8.1 8.8 %copy-start.46 = (f32[2048,6]{0,1:T(8,128)}, f32[2048,6]{0,1:T(8,128)S(1)}, u32[]{:S(2)}) copy-start(f32[2048,6]{0,1:T(8,128)S(1)} %get-tuple-element.122) | copy-start | bytes 147460
  17.0 8.8 %copy-start.60 = (f32[2048]{0:T(1024)}, f32[2048]{0:T(1024)S(1)}, u32[]{:S(2)}) copy-start(f32[2048]{0:T(1024)S(1)} %get-tuple-element.114) | copy-start | bytes 24580
  17.0 8.8 %copy-start.62 = (f32[2048]{0:T(1024)}, f32[2048]{0:T(1024)S(1)}, u32[]{:S(2)}) copy-start(f32[2048]{0:T(1024)S(1)} %get-tuple-element.112) | copy-start | bytes 24580
  17.0 8.8 %copy-start.64 = (f32[2048]{0:T(1024)}, f32[2048]{0:T(1024)S(1)}, u32[]{:S(2)}) copy-start(f32[2048]{0:T(1024)S(1)} %get-tuple-element.113) | copy-start | bytes 24580
  32.9 9.5 %copy-start.111 = (f32[6]{0:T(128)}, f32[6]{0:T(128)S(1)}, u32[]{:S(2)}) copy-start(f32[6]{0:T(128)S(1)} %get-tuple-element.45) | copy-start | bytes 76
  32.9 9.8 %copy-start.82 = (f32[6]{0:T(128)}, f32[6]{0:T(128)S(1)}, u32[]{:S(2)}) copy-start(f32[6]{0:T(128)S(1)} %get-tuple-element.44) | copy-start | bytes 76
  32.9 9.8 %copy-start.96 = (f32[6]{0:T(128)}, f32[6]{0:T(128)S(1)}, u32[]{:S(2)}) copy-start(f32[6]{0:T(128)S(1)} %get-tuple-element.43) | copy-start | bytes 76
  32.9 10.1 %copy-start.84 = (f32[6]{0:T(128)}, f32[6]{0:T(128)S(1)}, u32[]{:S(2)}) copy-start(f32[6]{0:T(128)S(1)} %get-tuple-element.42) | copy-start | bytes 76
  44.0 5.6 %copy-start.14 = (f32[8,256,384]{1,2,0}, f32[8,256,384]{1,2,0:S(1)}, u32[]{:S(2)}) copy-start(f32[8,256,384]{1,2,0:S(1)} %fusion.115) | copy-start | bytes 9437188
  58.4 10.3 %copy-start.79 = (f32[2048]{0:T(1024)}, f32[2048]{0:T(1024)S(1)}, u32[]{:S(2)}) copy-start(f32[2048]{0:T(1024)S(1)} %fusion.83) | copy-start | bytes 24580
  58.6 16.2 %copy-start.98 = (f32[384]{0:T(512)}, f32[384]{0:T(512)S(1)}, u32[]{:S(2)}) copy-start(f32[384]{0:T(512)S(1)} %mul.967) | copy-start | bytes 4612
  58.6 15.0 %copy-start.71 = (bf16[768,6]{0,1:T(8,128)(2,1)S(1)}, bf16[768,6]{0,1:T(8,128)(2,1)}, u32[]{:S(2)}) copy-start(bf16[768,6]{0,1:T(8,128)(2,1)} %param.25) | copy-start | bytes 27652
  68.7 1.4 collective-permute-start
  70.1 4.6 collective-permute-start.1
  83.6 27.1 %copy-start.25 = (bf16[2048,384]{0,1:T(8,128)(2,1)}, bf16[2048,384]{0,1:T(8,128)(2,1)S(1)}, u32[]{:S(2)}) copy-start(bf16[2048,384]{0,1:T(8,128)(2,1)S(1)} %get-tuple-element.85) | copy-start | bytes 4718596
  90.5 25.0 %copy-start.21 = (f32[8,6,128,64]{2,3,1,0:T(8,128)}, f32[8,6,128,64]{2,3,1,0:T(8,128)S(1)}, u32[]{:S(2)}) copy-start(f32[8,6,128,64]{2,3,1,0:T(8,128)S(1)} %fusion.49) | copy-start | bytes 4718596
  113.3 133.1 %collective-permute-start.29 = (f32[192,768]{1,0:T(8,128)}, f32[192,768]{1,0:T(8,128)}, u32[]{:S(2)}, u32[]{:S(2)}) collective-permute-start(f32[192,768]{1,0:T(8,128)} %constant_dynamic-slice_fusion.2), channel_id=1, source_target_pairs={{0,4},{4,0},{8,12},{12,8},{16,20},{20,16},{24,28},{28,24},{1,5},{5... | collective-permute-start | bytes 1769480 | tf_op jit(solution)/shard_map/ppermute | solution.py:77
  138.0 6.7 %copy-start.48 = (f32[8,256,6]{1,2,0:T(8,128)S(1)}, f32[8,256,6]{1,2,0:T(8,128)}, u32[]{:S(2)}) copy-start(f32[8,256,6]{1,2,0:T(8,128)} %fusion.30) | copy-start | bytes 147460
  138.0 6.7 %copy-start.51 = (f32[8,256,6]{1,2,0:T(8,128)S(1)}, f32[8,256,6]{1,2,0:T(8,128)}, u32[]{:S(2)}) copy-start(f32[8,256,6]{1,2,0:T(8,128)} %copy-done.49) | copy-start | bytes 147460
  144.7 6.3 %copy-start.59 = (f32[8,256,6]{1,2,0:T(8,128)}, f32[8,256,6]{1,2,0:T(8,128)S(1)}, u32[]{:S(2)}) copy-start(f32[8,256,6]{1,2,0:T(8,128)S(1)} %get-tuple-element.20) | copy-start | bytes 147460
  217.2 23.7 %collective-permute-start.5 = (f32[1024,768]{1,0:T(8,128)}, f32[1024,768]{1,0:T(8,128)}, u32[]{:S(2)}, u32[]{:S(2)}) collective-permute-start(f32[1024,768]{1,0:T(8,128)} %fusion.39), channel_id=1, source_target_pairs={{0,1},{1,0},{2,3},{3,2},{4,5},{5,4},{6,7},{7,6},{8,9},{9,8},{10,11... | collective-permute-start | bytes 9437192 | tf_op jit(solution)/shard_map/ppermute | solution.py:105
  219.9 31.9 %collective-permute-start.2 = (f32[1024,768]{1,0:T(8,128)}, f32[1024,768]{1,0:T(8,128)}, u32[]{:S(2)}, u32[]{:S(2)}) collective-permute-start(f32[1024,768]{1,0:T(8,128)} %fusion.60), channel_id=1, source_target_pairs={{0,1},{1,0},{2,3},{3,2},{4,5},{5,4},{6,7},{7,6},{8,9},{9,8},{10,11... | collective-permute-start | bytes 9437192 | tf_op jit(solution)/shard_map/ppermute | solution.py:105
  221.5 5.4 %copy-start.119 = (f32[384]{0:T(512)S(1)}, f32[384]{0:T(512)}, u32[]{:S(2)}) copy-start(f32[384]{0:T(512)} %get-tuple-element.48) | copy-start | bytes 4612
  221.5 9.5 %copy-start.23 = (bf16[2048,384]{0,1:T(8,128)(2,1)S(1)}, bf16[2048,384]{0,1:T(8,128)(2,1)}, u32[]{:S(2)}) copy-start(bf16[2048,384]{0,1:T(8,128)(2,1)} %copy-done.22) | copy-start | bytes 4718596
  225.3 23.9 %collective-permute-start.23 = (f32[384,384]{1,0:T(8,128)}, f32[384,384]{1,0:T(8,128)}, u32[]{:S(2)}, u32[]{:S(2)}) collective-permute-start(f32[384,384]{1,0:T(8,128)} %constant_dynamic-slice_fusion.5), channel_id=1, source_target_pairs={{0,8},{4,12},{8,0},{12,4},{16,24},{20,28},{24,16},{28,20},{1,9},{5... | collective-permute-start | bytes 1769480 | tf_op jit(solution)/shard_map/ppermute | solution.py:77
  231.2 5.3 %copy-start.118 = (f32[384]{0:T(512)S(1)}, f32[384]{0:T(512)}, u32[]{:S(2)}) copy-start(f32[384]{0:T(512)} %get-tuple-element.84) | copy-start | bytes 4612
  236.2 4.0 collective-permute-start.8
  240.2 16.9 %collective-permute-start.17 = (f32[416,384]{1,0:T(8,128)S(1)}, f32[416,384]{1,0:T(8,128)S(1)}, u32[]{:S(2)}, u32[]{:S(2)}) collective-permute-start(f32[416,384]{1,0:T(8,128)S(1)} %pad_dynamic-slice_fusion), channel_id=1, source_target_pairs={{0,4},{4,0},{8,12},{12,8},{16,20},{20,16},{24,28},{28,24},{1,5},{5... | collective-permute-start | bytes 1916936 | tf_op jit(solution)/shard_map/ppermute | solution.py:77
  240.9 7.1 %copy-start.40 = (f32[384,768]{1,0:T(8,128)S(1)}, f32[384,768]{1,0:T(8,128)}, u32[]{:S(2)}) copy-start(f32[384,768]{1,0:T(8,128)} %copy-done.39) | copy-start | bytes 3538948
  240.9 9.8 %copy-start.42 = (f32[768,384]{1,0:T(8,128)S(1)}, f32[768,384]{1,0:T(8,128)}, u32[]{:S(2)}) copy-start(f32[768,384]{1,0:T(8,128)} %copy-done.41) | copy-start | bytes 3538948
  240.9 14.5 %collective-permute-start.9 = (f32[224,256]{1,0:T(8,128)S(1)}, f32[224,256]{1,0:T(8,128)S(1)}, u32[]{:S(2)}, u32[]{:S(2)}) collective-permute-start(f32[224,256]{1,0:T(8,128)S(1)} %constant_dynamic-slice_fusion.10), channel_id=1, source_target_pairs={{0,8},{4,12},{8,0},{12,4},{16,24},{20,28},{24,16},{28,20},{1,9},{5... | collective-permute-start | bytes 688136 | tf_op jit(solution)/shard_map/ppermute | solution.py:77
  246.4 5.4 %copy-start.27 = (bf16[2048,384]{0,1:T(8,128)(2,1)S(1)}, bf16[2048,384]{0,1:T(8,128)(2,1)}, u32[]{:S(2)}) copy-start(bf16[2048,384]{0,1:T(8,128)(2,1)} %copy-done.25) | copy-start | bytes 4718596
  246.5 141.7 %collective-permute-start.6 = (f32[1024,768]{1,0:T(8,128)S(1)}, f32[1024,768]{1,0:T(8,128)S(1)}, u32[]{:S(2)}, u32[]{:S(2)}) collective-permute-start(f32[1024,768]{1,0:T(8,128)S(1)} %fusion.43), channel_id=1, source_target_pairs={{0,2},{1,3},{2,0},{3,1},{4,6},{5,7},{6,4},{7,5},{8,10},{9,11},{10,... | collective-permute-start | bytes 9437192 | tf_op jit(solution)/shard_map/ppermute | solution.py:107
  249.2 23.2 %collective-permute-start.30 = (f32[96,768]{1,0:T(8,128)S(1)}, f32[96,768]{1,0:T(8,128)S(1)}, u32[]{:S(2)}, u32[]{:S(2)}) collective-permute-start(f32[96,768]{1,0:T(8,128)S(1)} %constant_dynamic-slice_fusion.1), channel_id=1, source_target_pairs={{0,8},{4,12},{8,0},{12,4},{16,24},{20,28},{24,16},{28,20},{1,9},{5... | collective-permute-start | bytes 884744 | tf_op jit(solution)/shard_map/ppermute | solution.py:77
  254.8 150.3 %collective-permute-start.3 = (f32[1024,768]{1,0:T(8,128)S(1)}, f32[1024,768]{1,0:T(8,128)S(1)}, u32[]{:S(2)}, u32[]{:S(2)}) collective-permute-start(f32[1024,768]{1,0:T(8,128)S(1)} %convolution_add_fusion.1), channel_id=1, source_target_pairs={{0,2},{1,3},{2,0},{3,1},{4,6},{5,7},{6,4},{7,5},{8,10},{9,11},{10,... | collective-permute-start | bytes 9437192 | tf_op jit(solution)/shard_map/ppermute | solution.py:107
  255.4 18.5 %collective-permute-start.24 = (f32[192,384]{1,0:T(8,128)S(1)}, f32[192,384]{1,0:T(8,128)S(1)}, u32[]{:S(2)}, u32[]{:S(2)}) collective-permute-start(f32[192,384]{1,0:T(8,128)S(1)} %constant_dynamic-slice_fusion.4), channel_id=1, source_target_pairs={{0,4},{4,0},{8,12},{12,8},{16,20},{20,16},{24,28},{28,24},{1,5},{5... | collective-permute-start | bytes 884744 | tf_op jit(solution)/shard_map/ppermute | solution.py:77
  257.1 9.0 %collective-permute-start.10 = (f32[112,256]{1,0:T(8,128)S(1)}, f32[112,256]{1,0:T(8,128)S(1)}, u32[]{:S(2)}, u32[]{:S(2)}) collective-permute-start(f32[112,256]{1,0:T(8,128)S(1)} %constant_dynamic-slice_fusion.9), channel_id=1, source_target_pairs={{0,4},{4,0},{8,12},{12,8},{16,20},{20,16},{24,28},{28,24},{1,5},{5... | collective-permute-start | bytes 344072 | tf_op jit(solution)/shard_map/ppermute | solution.py:77
  266.1 5.9 %collective-permute-start.11 = (f32[56,256]{1,0:T(8,128)S(1)}, f32[56,256]{1,0:T(8,128)S(1)}, u32[]{:S(2)}, u32[]{:S(2)}) collective-permute-start(f32[56,256]{1,0:T(8,128)S(1)} %constant_dynamic-slice_fusion.8), channel_id=1, source_target_pairs={{0,16},{4,20},{8,24},{12,28},{16,0},{20,4},{24,8},{28,12},{1,17},{... | collective-permute-start | bytes 172040 | tf_op jit(solution)/shard_map/ppermute | solution.py:77
  272.0 118.6 %collective-permute-start.18 = (f32[208,384]{1,0:T(8,128)S(1)}, f32[208,384]{1,0:T(8,128)S(1)}, u32[]{:S(2)}, u32[]{:S(2)}) collective-permute-start(f32[208,384]{1,0:T(8,128)S(1)} %constant_dynamic-slice_fusion.7), channel_id=1, source_target_pairs={{0,8},{4,12},{8,0},{12,4},{16,24},{20,28},{24,16},{28,20},{1,9},{5... | collective-permute-start | bytes 958472 | tf_op jit(solution)/shard_map/ppermute | solution.py:77
  272.4 113.1 %collective-permute-start.12 = (f32[56,256]{1,0:T(8,128)S(1)}, f32[56,256]{1,0:T(8,128)S(1)}, u32[]{:S(2)}, u32[]{:S(2)}) collective-permute-start(f32[56,256]{1,0:T(8,128)S(1)} %dynamic-slice_add_fusion.10), channel_id=1, source_target_pairs={{0,2},{1,3},{2,0},{3,1},{4,6},{5,7},{6,4},{7,5},{8,10},{9,11},{10,... | collective-permute-start | bytes 172040 | tf_op jit(solution)/shard_map/ppermute | solution.py:397
  273.9 123.4 %collective-permute-start.31 = (f32[48,768]{1,0:T(8,128)S(1)}, f32[48,768]{1,0:T(8,128)S(1)}, u32[]{:S(2)}, u32[]{:S(2)}) collective-permute-start(f32[48,768]{1,0:T(8,128)S(1)} %constant_dynamic-slice_fusion), channel_id=1, source_target_pairs={{0,16},{4,20},{8,24},{12,28},{16,0},{20,4},{24,8},{28,12},{1,17},{... | collective-permute-start | bytes 442376 | tf_op jit(solution)/shard_map/ppermute | solution.py:77
  385.5 12.6 %collective-permute-start.25 = (f32[96,384]{1,0:T(8,128)S(1)}, f32[96,384]{1,0:T(8,128)S(1)}, u32[]{:S(2)}, u32[]{:S(2)}) collective-permute-start(f32[96,384]{1,0:T(8,128)S(1)} %constant_dynamic-slice_fusion.3), channel_id=1, source_target_pairs={{0,16},{4,20},{8,24},{12,28},{16,0},{20,4},{24,8},{28,12},{1,17},{... | collective-permute-start | bytes 442376 | tf_op jit(solution)/shard_map/ppermute | solution.py:77
  388.1 9.1 %collective-permute-start.13 = (f32[56,256]{1,0:T(8,128)S(1)}, f32[56,256]{1,0:T(8,128)S(1)}, u32[]{:S(2)}, u32[]{:S(2)}) collective-permute-start(f32[56,256]{1,0:T(8,128)S(1)} %add.602), channel_id=1, source_target_pairs={{0,16},{4,20},{8,24},{12,28},{16,0},{20,4},{24,8},{28,12},{1,17},{... | collective-permute-start | bytes 172040 | tf_op jit(solution)/shard_map/ppermute | solution.py:86
  390.6 76.1 %collective-permute-start.7 = (f32[1024,768]{1,0:T(8,128)}, f32[1024,768]{1,0:T(8,128)}, u32[]{:S(2)}, u32[]{:S(2)}) collective-permute-start(f32[1024,768]{1,0:T(8,128)} %add.582), channel_id=1, source_target_pairs={{0,1},{1,0},{2,3},{3,2},{4,5},{5,4},{6,7},{7,6},{8,9},{9,8},{10,11... | collective-permute-start | bytes 9437192 | tf_op jit(solution)/shard_map/ppermute | solution.py:108
  397.3 16.1 %collective-permute-start.19 = (f32[104,384]{1,0:T(8,128)S(1)}, f32[104,384]{1,0:T(8,128)S(1)}, u32[]{:S(2)}, u32[]{:S(2)}) collective-permute-start(f32[104,384]{1,0:T(8,128)S(1)} %constant_dynamic-slice_fusion.6), channel_id=1, source_target_pairs={{0,16},{4,20},{8,24},{12,28},{16,0},{20,4},{24,8},{28,12},{1,17},{... | collective-permute-start | bytes 479240 | tf_op jit(solution)/shard_map/ppermute | solution.py:77
  397.3 5.1 %collective-permute-start.14 = (f32[112,256]{1,0:T(8,128)S(1)}, f32[112,256]{1,0:T(8,128)S(1)}, u32[]{:S(2)}, u32[]{:S(2)}) collective-permute-start(f32[112,256]{1,0:T(8,128)S(1)} %maximum_select_fusion.14), channel_id=1, source_target_pairs={{0,4},{4,0},{8,12},{12,8},{16,20},{20,16},{24,28},{28,24},{1,5},{5... | collective-permute-start | bytes 344072 | tf_op jit(solution)/shard_map/ppermute | solution.py:86
  398.1 18.4 %collective-permute-start.32 = (f32[48,768]{1,0:T(8,128)S(1)}, f32[48,768]{1,0:T(8,128)S(1)}, u32[]{:S(2)}, u32[]{:S(2)}) collective-permute-start(f32[48,768]{1,0:T(8,128)S(1)} %dynamic-slice_add_fusion.7), channel_id=1, source_target_pairs={{0,16},{4,20},{8,24},{12,28},{16,0},{20,4},{24,8},{28,12},{1,17},{... | collective-permute-start | bytes 442376 | tf_op jit(solution)/shard_map/ppermute | solution.py:86
  402.4 20.7 %collective-permute-start.26 = (f32[96,384]{1,0:T(8,128)S(1)}, f32[96,384]{1,0:T(8,128)S(1)}, u32[]{:S(2)}, u32[]{:S(2)}) collective-permute-start(f32[96,384]{1,0:T(8,128)S(1)} %dynamic-slice_add_fusion.8), channel_id=1, source_target_pairs={{0,16},{4,20},{8,24},{12,28},{16,0},{20,4},{24,8},{28,12},{1,17},{... | collective-permute-start | bytes 442376 | tf_op jit(solution)/shard_map/ppermute | solution.py:86
  405.1 18.0 %collective-permute-start.15 = (f32[224,256]{1,0:T(8,128)S(1)}, f32[224,256]{1,0:T(8,128)S(1)}, u32[]{:S(2)}, u32[]{:S(2)}) collective-permute-start(f32[224,256]{1,0:T(8,128)S(1)} %maximum_select_fusion.13), channel_id=1, source_target_pairs={{0,8},{4,12},{8,0},{12,4},{16,24},{20,28},{24,16},{28,20},{1,9},{5... | collective-permute-start | bytes 688136 | tf_op jit(solution)/shard_map/ppermute | solution.py:86
  413.3 59.5 %collective-permute-start.4 = (f32[1024,768]{1,0:T(8,128)}, f32[1024,768]{1,0:T(8,128)}, u32[]{:S(2)}, u32[]{:S(2)}) collective-permute-start(f32[1024,768]{1,0:T(8,128)} %add.541), channel_id=1, source_target_pairs={{0,1},{1,0},{2,3},{3,2},{4,5},{5,4},{6,7},{7,6},{8,9},{9,8},{10,11... | collective-permute-start | bytes 9437192 | tf_op jit(solution)/shard_map/ppermute | solution.py:108
  416.5 9.9 %collective-permute-start.20 = (f32[104,384]{1,0:T(8,128)S(1)}, f32[104,384]{1,0:T(8,128)S(1)}, u32[]{:S(2)}, u32[]{:S(2)}) collective-permute-start(f32[104,384]{1,0:T(8,128)S(1)} %dynamic-slice_add_fusion.6), channel_id=1, source_target_pairs={{0,16},{4,20},{8,24},{12,28},{16,0},{20,4},{24,8},{28,12},{1,17},{... | collective-permute-start | bytes 479240 | tf_op jit(solution)/shard_map/ppermute | solution.py:86
  423.0 9.6 %collective-permute-start.33 = (f32[96,768]{1,0:T(8,128)S(1)}, f32[96,768]{1,0:T(8,128)S(1)}, u32[]{:S(2)}, u32[]{:S(2)}) collective-permute-start(f32[96,768]{1,0:T(8,128)S(1)} %maximum_select_fusion.12), channel_id=1, source_target_pairs={{0,8},{4,12},{8,0},{12,4},{16,24},{20,28},{24,16},{28,20},{1,9},{5... | collective-permute-start | bytes 884744 | tf_op jit(solution)/shard_map/ppermute | solution.py:86
  423.1 9.7 %collective-permute-start.27 = (f32[192,384]{1,0:T(8,128)S(1)}, f32[192,384]{1,0:T(8,128)S(1)}, u32[]{:S(2)}, u32[]{:S(2)}) collective-permute-start(f32[192,384]{1,0:T(8,128)S(1)} %maximum_select_fusion.11), channel_id=1, source_target_pairs={{0,4},{4,0},{8,12},{12,8},{16,20},{20,16},{24,28},{28,24},{1,5},{5... | collective-permute-start | bytes 884744 | tf_op jit(solution)/shard_map/ppermute | solution.py:86
  425.4 17.7 %copy-start.36 = (f32[448,256]{1,0:T(8,128)}, f32[448,256]{1,0:T(8,128)S(1)}, u32[]{:S(2)}) copy-start(f32[448,256]{1,0:T(8,128)S(1)} %maximum_select_fusion.9) | copy-start | bytes 1376260
  426.4 15.9 %collective-permute-start.16 = (f32[448,256]{1,0:T(8,128)S(1)}, f32[448,256]{1,0:T(8,128)S(1)}, u32[]{:S(2)}, u32[]{:S(2)}) collective-permute-start(f32[448,256]{1,0:T(8,128)S(1)} %maximum_select_fusion.9), channel_id=1, source_target_pairs={{0,1},{1,0},{2,3},{3,2},{4,5},{5,4},{6,7},{7,6},{8,9},{9,8},{10,11... | collective-permute-start | bytes 1376264 | tf_op jit(solution)/shard_map/ppermute | solution.py:86
  432.7 9.3 %collective-permute-start.21 = (f32[208,384]{1,0:T(8,128)S(1)}, f32[208,384]{1,0:T(8,128)S(1)}, u32[]{:S(2)}, u32[]{:S(2)}) collective-permute-start(f32[208,384]{1,0:T(8,128)S(1)} %maximum_select_fusion.10), channel_id=1, source_target_pairs={{0,8},{4,12},{8,0},{12,4},{16,24},{20,28},{24,16},{28,20},{1,9},{5... | collective-permute-start | bytes 958472 | tf_op jit(solution)/shard_map/ppermute | solution.py:86
  432.7 16.4 %collective-permute-start.34 = (f32[192,768]{1,0:T(8,128)S(1)}, f32[192,768]{1,0:T(8,128)}, u32[]{:S(2)}, u32[]{:S(2)}) collective-permute-start(f32[192,768]{1,0:T(8,128)S(1)} %maximum_select_fusion.8), channel_id=1, source_target_pairs={{0,4},{4,0},{8,12},{12,8},{16,20},{20,16},{24,28},{28,24},{1,5},{5... | collective-permute-start | bytes 1769480 | tf_op jit(solution)/shard_map/ppermute | solution.py:86
  442.0 14.7 %collective-permute-start.28 = (f32[384,384]{1,0:T(8,128)}, f32[384,384]{1,0:T(8,128)}, u32[]{:S(2)}, u32[]{:S(2)}) collective-permute-start(f32[384,384]{1,0:T(8,128)} %maximum_select_fusion.7), channel_id=1, source_target_pairs={{0,8},{4,12},{8,0},{12,4},{16,24},{20,28},{24,16},{28,20},{1,9},{5... | collective-permute-start | bytes 1769480 | tf_op jit(solution)/shard_map/ppermute | solution.py:86
  443.1 18.6 %collective-permute-start.22 = (f32[416,384]{1,0:T(8,128)S(1)}, f32[416,384]{1,0:T(8,128)}, u32[]{:S(2)}, u32[]{:S(2)}) collective-permute-start(f32[416,384]{1,0:T(8,128)S(1)} %maximum_select_fusion.6), channel_id=1, source_target_pairs={{0,4},{4,0},{8,12},{12,8},{16,20},{20,16},{24,28},{28,24},{1,5},{5... | collective-permute-start | bytes 1916936 | tf_op jit(solution)/shard_map/ppermute | solution.py:86
  466.6 6.3 %copy-start.73 = (f32[2048]{0:T(1024)S(1)}, f32[2048]{0:T(1024)}, u32[]{:S(2)}) copy-start(f32[2048]{0:T(1024)} %copy-done.72) | copy-start | bytes 24580
  466.6 6.3 %copy-start.78 = (f32[2048]{0:T(1024)S(1)}, f32[2048]{0:T(1024)}, u32[]{:S(2)}) copy-start(f32[2048]{0:T(1024)} %get-tuple-element.108) | copy-start | bytes 24580
  466.6 6.3 %copy-start.81 = (f32[2048]{0:T(1024)S(1)}, f32[2048]{0:T(1024)}, u32[]{:S(2)}) copy-start(f32[2048]{0:T(1024)} %copy-done.79) | copy-start | bytes 24580
  (116 other events, 368.1 us)

commit v2 on v0

v2 whole, which is shorter than its diff:
```python
import functools

import jax
import jax.numpy as jnp
from jax import lax
from jax.experimental import pallas as pl
from jax.experimental.pallas import tpu as pltpu
from jax.sharding import PartitionSpec as P

SPAN = 256
LANES = 128
EPS = 1e-05
FAR = -10000.0
FIRST = ((0,), (0,))
LAST = ((1,), (1,))


def dot(left, right, dims=((1,), (0,))):
    return lax.dot_general(left, right, (dims, ((), ())), preferred_element_type=jnp.float32)


def parts_of(values, count):
    parts = []
    for _ in range(count):
        part = values.astype(jnp.bfloat16)
        values = values - part.astype(jnp.float32)
        parts.append(part)
    return parts


def dot_left_exact(left, values, count):
    total = None
    for part in parts_of(values, count):
        product = dot(left, part)
        total = product if total is None else total + product
    return total


def dot_right_exact(values, right, dims):
    total = None
    for part in parts_of(values, 2):
        product = dot(part, right, dims)
        total = product if total is None else total + product
    return total


def sigmoid(values):
    return 1.0 / (1.0 + jnp.exp(-values))


def softplus(values):
    return jnp.maximum(values, 0.0) + jnp.log1p(jnp.exp(-jnp.abs(values)))


def lower_ones():
    down = lax.broadcasted_iota(jnp.int32, (SPAN, SPAN), 0)
    across = lax.broadcasted_iota(jnp.int32, (SPAN, SPAN), 1)
    return down >= across


def as_low(flags):
    return jnp.where(flags, 1.0, 0.0).astype(jnp.bfloat16)


def span_decays(dt_part, cols, seg_row, head_rows, spread, lower):
    dt_in = dt_part + head_rows[0:1]
    step = softplus(dt_in)
    falls = dot_left_exact(as_low(lower), step * head_rows[1:2], 3)
    falls_t = falls.T
    decay_in = jnp.exp(falls[SPAN - 1 : SPAN] - falls) * cols[:, 5:6]
    decay_out = jnp.exp(falls) * cols[:, 6:7]
    linked = lower & (cols[:, 0:1] == seg_row)
    wide = lambda values: dot_right_exact(values, spread, ((1,), (0,)))
    return dt_in, step, falls, falls_t, wide(step), wide(decay_in), wide(decay_out), linked


def fwd_kernel(
    hid_ref, cot_ref, cols_ref, seg_ref, gain_ref, wcat_ref, wout_ref, conv_ref, head_ref,
    spread_ref, chan_ref, normed_ref, conv_in_ref, z_ref, dt_ref, pre_ref, y_ref, gin_ref,
    carried_ref, sums_ref, ext_ref, state_ref, *, heads, inner, conv_width,
):
    @pl.when(pl.program_id(0) == 0)
    def _():
        ext_ref[0:8, :] = jnp.zeros((8, conv_width), jnp.float32)
        state_ref[...] = jnp.zeros_like(state_ref)

    cols = cols_ref[...]
    hid = hid_ref[...].astype(jnp.float32)
    inv_rms = lax.rsqrt(jnp.mean(hid * hid, -1, keepdims=True) + EPS)
    normed = (hid * inv_rms * gain_ref[...]).astype(jnp.bfloat16)
    normed_ref[...] = normed
    conv_in = dot(normed, wcat_ref[:, 0:conv_width])
    gate_in = dot(normed, wcat_ref[:, conv_width : conv_width + inner])
    dt_part = dot(normed, wcat_ref[:, conv_width + inner :])
    conv_in_ref[...] = conv_in
    z_ref[...] = gate_in
    dt_ref[...] = dt_part
    ext_ref[8 : 8 + SPAN, :] = conv_in
    pre = conv_ref[4:5] + conv_ref[0:1] * conv_in
    for lag in range(1, 4):
        earlier = ext_ref[8 - lag : 8 - lag + SPAN, :]
        pre = pre + conv_ref[lag : lag + 1] * (earlier * cols[:, lag : lag + 1])
    ext_ref[0:8, :] = conv_in[SPAN - 8 :]
    pre_ref[...] = pre
    active = pre * sigmoid(pre)
    x_conv = active[:, :inner]
    states = (conv_width - inner) // 2
    b_low = active[:, inner : inner + states].astype(jnp.bfloat16)
    c_low = active[:, inner + states :].astype(jnp.bfloat16)
    lower = lower_ones()
    _, _, falls, falls_t, step_x, in_x, out_x, linked = span_decays(
        dt_part, cols, seg_ref[0], head_ref[...], spread_ref[...], lower
    )
    kernel = dot(c_low, b_low, LAST)
    inputs = (step_x * x_conv).astype(jnp.bfloat16)
    size = inner // heads
    group = LANES // size
    lane_head = lax.broadcasted_iota(jnp.int32, (SPAN, LANES), 1) // size
    local = []
    for first in range(0, heads, group):
        at = first * size
        total = None
        for head in range(first, first + group):
            decay = jnp.exp(
                jnp.where(linked, falls[:, head : head + 1] - falls_t[head : head + 1, :], FAR)
            )
            mixing = (kernel * decay).astype(jnp.bfloat16)
            own = jnp.where(lane_head == head - first, inputs[:, at : at + LANES], 0)
            part = dot(mixing, own.astype(jnp.bfloat16))
            total = part if total is None else total + part
        local.append(total)
    local = jnp.concatenate(local, 1)
    carried = state_ref[...].astype(jnp.bfloat16)
    carried_ref[0] = carried
    y_flat = local + out_x * dot(c_low, carried) + chan_ref[0:1] * x_conv
    entering = (inputs.astype(jnp.float32) * in_x).astype(jnp.bfloat16)
    state_ref[...] = out_x[SPAN - 1 : SPAN] * state_ref[...] + dot(b_low, entering, FIRST)
    y_ref[...] = y_flat
    gated = y_flat * (gate_in * sigmoid(gate_in))
    grad_mix = (cols[:, 4:5] * cot_ref[...].astype(jnp.float32)).astype(jnp.bfloat16)
    grad_in = dot(grad_mix, wout_ref[...], LAST)
    gin_ref[...] = grad_in
    squares = jnp.sum(gated * gated, -1, keepdims=True)
    cross = jnp.sum(grad_in * chan_ref[1:2] * gated, -1, keepdims=True)
    lane = lax.broadcasted_iota(jnp.int32, (SPAN, LANES), 1)
    sums_ref[0] = jnp.where(lane == 0, squares, cross).T[0:2]


def gate_kernel(
    shift_ref, sums_ref, z_ref, y_ref, gin_ref, cot_ref, cols_ref, normed_ref, wout_ref, chan_ref,
    sent_ref, kept_ref, gy_ref, gz_ref, weights_ref, gain_ref, *, inner, inner_all,
):
    index = pl.program_id(0)
    half = pl.num_programs(0) // 2

    @pl.when(index == 0)
    def _():
        weights_ref[...] = jnp.zeros_like(weights_ref)
        gain_ref[...] = jnp.zeros_like(gain_ref)

    sums = sums_ref[0]
    copies = inner // LANES
    over = lambda row: jnp.concatenate([jnp.broadcast_to(row, (LANES, SPAN)).T] * copies, 1)
    squares, cross = over(sums[0:1]), over(sums[1:2])
    inv_gate = lax.rsqrt(squares / inner_all + EPS)
    gate_in = z_ref[...]
    y_flat = y_ref[...]
    sig = sigmoid(gate_in)
    active = gate_in * sig
    gated = y_flat * active
    scaled = gated * inv_gate
    out_in = (scaled * chan_ref[1:2]).astype(jnp.bfloat16)
    mixed = dot(out_in, wout_ref[...])

    @pl.when(index < half)
    def _():
        sent_ref[...] = mixed

    @pl.when(index >= half)
    def _():
        kept_ref[...] = mixed

    grad_mix = (cols_ref[:, 4:5] * cot_ref[...].astype(jnp.float32)).astype(jnp.bfloat16)
    weights_ref[0:inner, :] += dot(out_in, grad_mix, FIRST)
    grad_in = gin_ref[...]
    gain_ref[0:1, :] += jnp.sum(grad_in * scaled, 0, keepdims=True)
    grad_gated = inv_gate * (
        grad_in * chan_ref[1:2] - scaled * inv_gate * (cross * (1.0 / inner_all))
    )
    gy_ref[...] = grad_gated * active
    grad_z = (grad_gated * y_flat * (sig * (1.0 + gate_in * (1.0 - sig)))).astype(jnp.bfloat16)
    gz_ref[...] = grad_z
    weights_ref[inner : 2 * inner, :] += dot(grad_z, normed_ref[...], FIRST)


def bwd_kernel(
    shift_ref, cols_ref, seg_ref, normed_ref, conv_in_ref, dt_ref, pre_ref, y_ref, gy_ref, gz_ref,
    carried_ref, wcat_ref, conv_ref, head_ref, spread_ref, chan_ref,
    sent_ref, kept_ref, weights_ref, conv_grad_ref, head_grad_ref, ext_ref, flow_ref,
    *, heads, inner, conv_width,
):
    index = pl.program_id(0)
    half = pl.num_programs(0) // 2

    @pl.when(index == 0)
    def _():
        weights_ref[...] = jnp.zeros_like(weights_ref)
        conv_grad_ref[...] = jnp.zeros_like(conv_grad_ref)
        head_grad_ref[...] = jnp.zeros_like(head_grad_ref)

    @pl.when((index == 0) | (index == half))
    def _():
        ext_ref[SPAN : SPAN + 8, :] = jnp.zeros((8, conv_width), jnp.float32)
        flow_ref[...] = jnp.zeros_like(flow_ref)

    cols = cols_ref[...]
    pre = pre_ref[...]
    sig = sigmoid(pre)
    active = pre * sig
    slope = sig * (1.0 + pre * (1.0 - sig))
    x_conv = active[:, :inner]
    states = (conv_width - inner) // 2
    b_low = active[:, inner : inner + states].astype(jnp.bfloat16)
    c_low = active[:, inner + states :].astype(jnp.bfloat16)
    lower = lower_ones()
    spread = spread_ref[...]
    head_rows = head_ref[...]
    dt_in, step, falls, falls_t, step_x, in_x, out_x, linked = span_decays(
        dt_ref[...], cols, seg_ref[0], head_rows, spread, lower
    )
    kernel = dot(c_low, b_low, LAST)
    inputs = (step_x * x_conv).astype(jnp.bfloat16)
    grad_y = gy_ref[...]
    grad_scan = grad_y.astype(jnp.bfloat16)
    size = inner // heads
    group = LANES // size
    lane_head = lax.broadcasted_iota(jnp.int32, (SPAN, LANES), 1) // size
    grad_kernel = None
    grad_inputs = []
    for first in range(0, heads, group):
        at = first * size
        total = None
        for head in range(first, first + group):
            decay = jnp.exp(
                jnp.where(linked, falls[:, head : head + 1] - falls_t[head : head + 1, :], FAR)
            )
            mixing = (kernel * decay).astype(jnp.bfloat16)
            here = lane_head == head - first
            own = jnp.where(here, grad_scan[:, at : at + LANES], 0).astype(jnp.bfloat16)
            grad_part = dot(own, inputs[:, at : at + LANES], LAST) * decay
            grad_kernel = grad_part if grad_kernel is None else grad_kernel + grad_part
            part = dot(mixing, own, FIRST)
            total = part if total is None else total + part
        grad_inputs.append(total)
    flow = flow_ref[...]
    flow_low = flow.astype(jnp.bfloat16)
    grad_inputs = jnp.concatenate(grad_inputs, 1) + in_x * dot(b_low, flow_low)
    grad_kernel = grad_kernel.astype(jnp.bfloat16)
    inputs_wide = inputs.astype(jnp.float32)
    leaving, leaving_rest = parts_of(out_x * grad_scan.astype(jnp.float32), 2)
    entering = (in_x * inputs_wide).astype(jnp.bfloat16)
    grad_c = dot(grad_kernel, b_low) + dot(leaving, carried_ref[0], LAST)
    grad_b = dot(grad_kernel, c_low, FIRST) + dot(entering, flow_low, LAST)
    grad_carried = dot(c_low, leaving, FIRST) + dot(c_low, leaving_rest, FIRST)
    flow = out_x[SPAN - 1 : SPAN] * flow + grad_carried
    flow_ref[...] = flow
    crossing = jnp.sum(flow * carried_ref[0].astype(jnp.float32), 0, keepdims=True)
    crossing = dot_right_exact(jnp.broadcast_to(crossing, (8, inner)), spread, LAST)
    scanned = y_ref[...] - chan_ref[0:1] * x_conv
    grad_log = dot_right_exact(
        grad_scan.astype(jnp.float32) * scanned - inputs_wide * grad_inputs, spread, LAST
    )
    earlier = as_low(jnp.logical_not(upper_ones()))
    rate_sum = crossing[0:1] - dot_left_exact(earlier, grad_log, 3)
    grad_step = dot_right_exact(grad_inputs * x_conv, spread, LAST) + rate_sum * head_rows[1:2]
    grad_dt = grad_step * sigmoid(dt_in)
    head_grad_ref[0:1, :] += jnp.sum(grad_dt, 0, keepdims=True)
    head_grad_ref[1:2, :] += jnp.sum(rate_sum * step, 0, keepdims=True) * head_rows[1:2]
    grad_x = grad_y * chan_ref[0:1] + grad_inputs * step_x
    conv_grad_ref[5:6, 0:inner] += jnp.sum(grad_y * x_conv, 0, keepdims=True)
    grad_pre = jnp.concatenate([grad_x, grad_b, grad_c], 1) * slope
    conv_in = conv_in_ref[...]
    ext_ref[0:SPAN, :] = grad_pre
    grad_conv_in = conv_ref[0:1] * grad_pre
    conv_grad_ref[0:1, :] += jnp.sum(grad_pre * conv_in, 0, keepdims=True)
    conv_grad_ref[4:5, :] += jnp.sum(grad_pre, 0, keepdims=True)
    for lag in range(1, 4):
        term = ext_ref[lag : lag + SPAN, :] * cols[:, 7 + lag : 8 + lag]
        grad_conv_in = grad_conv_in + conv_ref[lag : lag + 1] * term
        conv_grad_ref[lag : lag + 1, :] += jnp.sum(term * conv_in, 0, keepdims=True)
    ext_ref[SPAN : SPAN + 8, :] = grad_pre[0:8]
    conv_low = grad_conv_in.astype(jnp.bfloat16)
    dt_low = grad_dt.astype(jnp.bfloat16)
    low = jnp.concatenate([conv_low, gz_ref[...], dt_low], 1)
    partial = dot(low, wcat_ref[...], LAST)

    @pl.when(index < half)
    def _():
        sent_ref[...] = partial

    @pl.when(index >= half)
    def _():
        kept_ref[...] = partial

    normed = normed_ref[...]
    weights_ref[0:conv_width, :] += dot(conv_low, normed, FIRST)
    weights_ref[conv_width:, :] += dot(dt_low, normed, FIRST)


def upper_ones():
    down = lax.broadcasted_iota(jnp.int32, (SPAN, SPAN), 0)
    across = lax.broadcasted_iota(jnp.int32, (SPAN, SPAN), 1)
    return down <= across


def finish_kernel(place_ref, own_ref, other_ref, hid_ref, cot_ref, gain_ref, out_ref):
    half = pl.num_programs(0) // 2
    mine = pl.program_id(0) // half == place_ref[0]
    hid = hid_ref[...].astype(jnp.float32)
    inv_rms = lax.rsqrt(jnp.mean(hid * hid, -1, keepdims=True) + EPS)

    def write(values):
        weighted = values * gain_ref[...]
        inner = jnp.mean(weighted * hid, -1, keepdims=True)
        out_ref[...] = (
            cot_ref[...].astype(jnp.float32)
            + inv_rms * weighted
            - hid * (inv_rms * inv_rms * inv_rms * inner)
        )

    @pl.when(mine)
    def _():
        write(own_ref[...])

    @pl.when(jnp.logical_not(mine))
    def _():
        write(other_ref[...])


def partners(count, step):
    return [(place, place ^ step) for place in range(count)]


def steps_of(count):
    return [1 << level for level in range((count - 1).bit_length())]


def take_half(values, which):
    half = values.shape[0] // 2
    return lax.dynamic_slice_in_dim(values, which * half, half, 0)


def join_halves(own, other, mine):
    return jnp.where(
        mine == 0, jnp.concatenate([own, other], 0), jnp.concatenate([other, own], 0)
    )


def axis_scatter(values, axis, count, order):
    place = lax.axis_index(axis)
    for step in order:
        mine = (place // step) % 2
        sent = lax.ppermute(take_half(values, 1 - mine), axis, partners(count, step))
        values = take_half(values, mine) + sent
    return values


def axis_gather(values, axis, count, order):
    place = lax.axis_index(axis)
    for step in reversed(order):
        other = lax.ppermute(values, axis, partners(count, step))
        values = join_halves(values, other, (place // step) % 2)
    return values


def dp_sum(values, count, first):
    order = steps_of(count)
    order = order[first:2] + order[:first] + order[2:]
    return axis_gather(axis_scatter(values, "dp", count, order), "dp", count, order)


def wide_tensor_sum(sent, kept, count):
    values = kept + lax.ppermute(sent, "tensor", partners(count, 1))
    for step in steps_of(count)[1:]:
        values = values + lax.ppermute(values, "tensor", partners(count, step))
    return values, lax.ppermute(values, "tensor", partners(count, 1))


def pad_rows(values, multiple):
    return jnp.pad(values, ((0, -values.shape[0] % multiple), (0, 0)))


def call(kernel, grid, prefetch, ins, in_specs, outs, out_specs, scratch, flops):
    moved = sum(a.size * a.dtype.itemsize for a in ins) + sum(
        o.size * o.dtype.itemsize for o in outs
    )
    return pl.pallas_call(
        kernel,
        grid_spec=pltpu.PrefetchScalarGridSpec(
            num_scalar_prefetch=len(prefetch),
            grid=grid,
            in_specs=in_specs,
            out_specs=out_specs,
            scratch_shapes=scratch,
        ),
        out_shape=outs,
        cost_estimate=pl.CostEstimate(flops=flops, bytes_accessed=moved, transcendentals=0),
    )(*prefetch, *ins)


def per_device(
    n_dp,
    n_tensor,
    hidden,
    cotangent,
    seg_ids,
    counts,
    norm_gain,
    w_x,
    w_z,
    w_dt,
    w_bc,
    conv_x,
    conv_x_bias,
    conv_bc,
    conv_bc_bias,
    dt_bias,
    a_log,
    d_skip,
    gate_gain,
    w_out,
):
    f32, bf16 = jnp.float32, jnp.bfloat16
    rows, width = hidden.shape
    bc_width = w_bc.shape[1]
    states = bc_width // 2
    heads = w_dt.shape[1]
    inner = w_x.shape[1]
    taps = conv_x.shape[0]
    size = inner // heads
    spans = rows // SPAN
    half_spans = spans // 2
    conv_width = inner + bc_width
    all_width = conv_width + inner + LANES
    mine = lax.axis_index("tensor") % 2
    positions = jnp.arange(rows)
    seg_spans = seg_ids.reshape(spans, SPAN)
    seg_end = seg_spans[:, -1:]
    seg_prev = jnp.concatenate([jnp.full((1, 1), -1, jnp.int32), seg_end[:-1]], 0)

    def conv_link(lag):
        ahead = jnp.concatenate([jnp.full((lag,), -1, jnp.int32), seg_ids[:-lag]])
        return ahead == seg_ids

    def conv_link_next(lag):
        behind = jnp.concatenate([seg_ids[lag:], jnp.full((lag,), -1, jnp.int32)])
        return behind == seg_ids

    cols = jnp.stack(
        [
            seg_ids.astype(f32),
            conv_link(1).astype(f32),
            conv_link(2).astype(f32),
            conv_link(3).astype(f32),
            (positions < counts[0]).astype(f32),
            (seg_spans == seg_end).reshape(rows).astype(f32),
            (seg_spans == seg_prev).reshape(rows).astype(f32),
            jnp.zeros((rows,), f32),
            conv_link_next(1).astype(f32),
            conv_link_next(2).astype(f32),
            conv_link_next(3).astype(f32),
        ],
        1,
    )
    cols = jnp.pad(cols, ((0, 0), (0, 16 - cols.shape[1])))
    seg_rows = seg_spans.astype(f32)[:, None, :]
    w_cat = jnp.concatenate([w_x, w_bc, w_z, jnp.pad(w_dt, ((0, 0), (0, LANES - heads)))], 1)
    conv_rows = jnp.concatenate(
        [
            jnp.concatenate([conv_x, conv_bc], 1),
            jnp.concatenate([conv_x_bias, conv_bc_bias])[None],
        ],
        0,
    )
    conv_rows = jnp.pad(conv_rows, ((0, 8 - conv_rows.shape[0]), (0, 0)))
    head_rows = jnp.pad(
        jnp.stack([dt_bias, -jnp.exp(a_log)], 0), ((0, 6), (0, LANES - heads))
    )
    spread = (jnp.arange(LANES)[:, None] == jnp.arange(inner)[None, :] // size).astype(bf16)
    chan = jnp.pad(jnp.stack([jnp.repeat(d_skip, size), gate_gain], 0), ((0, 6), (0, 0)))
    gain = norm_gain[None]

    def shape(*dims, dtype=f32):
        return jax.ShapeDtypeStruct(dims, dtype)

    def whole(array):
        return pl.BlockSpec(array.shape, lambda *_: (0,) * len(array.shape))

    def plain(columns):
        return pl.BlockSpec((SPAN, columns), lambda i: (i, 0))

    normed, conv_in, gate_in, dt_part, pre, y_flat, grad_in, carried, sums = call(
        functools.partial(fwd_kernel, heads=heads, inner=inner, conv_width=conv_width),
        (spans,),
        (),
        (hidden, cotangent, cols, seg_rows, gain, w_cat, w_out, conv_rows, head_rows, spread, chan),
        [plain(width), plain(width), plain(16), pl.BlockSpec((1, 1, SPAN), lambda i: (i, 0, 0))]
        + [whole(a) for a in (gain, w_cat, w_out, conv_rows, head_rows, spread, chan)],
        (
            shape(rows, width, dtype=bf16),
            shape(rows, conv_width),
            shape(rows, inner),
            shape(rows, LANES),
            shape(rows, conv_width),
            shape(rows, inner),
            shape(rows, inner),
            shape(spans, states, inner, dtype=bf16),
            shape(spans, 2, SPAN),
        ),
        [
            plain(width), plain(conv_width), plain(inner), plain(LANES), plain(conv_width),
            plain(inner), plain(inner),
            pl.BlockSpec((1, states, inner), lambda i: (i, 0, 0)),
            pl.BlockSpec((1, 2, SPAN), lambda i: (i, 0, 0)),
        ],
        [pltpu.VMEM((SPAN + 8, conv_width), f32), pltpu.VMEM((states, inner), f32)],
        2 * rows * (width * (all_width + inner) + heads * SPAN * LANES),
    )
    for step in steps_of(n_tensor):
        sums = sums + lax.ppermute(sums, "tensor", partners(n_tensor, step))
    shift = (half_spans * (1 - mine)).astype(jnp.int32).reshape(1)

    def turned(columns):
        return pl.BlockSpec((SPAN, columns), lambda i, s: ((i + s[0]) % spans, 0))

    sent_spec = pl.BlockSpec((SPAN, width), lambda i, s: (jnp.minimum(i, half_spans - 1), 0))
    kept_spec = pl.BlockSpec((SPAN, width), lambda i, s: (jnp.maximum(i - half_spans, 0), 0))
    mixed_sent, mixed_kept, grad_y, grad_z, early, gate_grad = call(
        functools.partial(gate_kernel, inner=inner, inner_all=inner * n_tensor),
        (spans,),
        (shift,),
        (sums, gate_in, y_flat, grad_in, cotangent, cols, normed, w_out, chan),
        [
            pl.BlockSpec((1, 2, SPAN), lambda i, s: ((i + s[0]) % spans, 0, 0)),
            turned(inner), turned(inner), turned(inner), turned(width), turned(16),
            turned(width), whole(w_out), whole(chan),
        ],
        (
            shape(rows // 2, width),
            shape(rows // 2, width),
            shape(rows, inner),
            shape(rows, inner, dtype=bf16),
            shape(2 * inner, width),
            shape(8, inner),
        ),
        [
            sent_spec, kept_spec, turned(inner), turned(inner),
            pl.BlockSpec((2 * inner, width), lambda i, s: (0, 0)),
            pl.BlockSpec((8, inner), lambda i, s: (0, 0)),
        ],
        [],
        2 * rows * width * inner * 3,
    )
    mixed_own, mixed_other = wide_tensor_sum(mixed_sent, mixed_kept, n_tensor)
    early_sum = dp_sum(early, n_dp, 0)

    def back_at(i, s):
        turn = i // half_spans
        return ((turn + s[0] // half_spans) % 2) * half_spans + half_spans - 1 - i % half_spans

    def back(columns):
        return pl.BlockSpec((SPAN, columns), lambda i, s: (back_at(i, s), 0))

    def low_at(i):
        return half_spans - 1 - i % half_spans

    partial_sent, partial_kept, late, conv_grad, head_grad = call(
        functools.partial(bwd_kernel, heads=heads, inner=inner, conv_width=conv_width),
        (spans,),
        (shift,),
        (
            cols, seg_rows, normed, conv_in, dt_part, pre, y_flat, grad_y, grad_z, carried, w_cat,
            conv_rows, head_rows, spread, chan,
        ),
        [
            back(16), pl.BlockSpec((1, 1, SPAN), lambda i, s: (back_at(i, s), 0, 0)),
            back(width), back(conv_width), back(LANES), back(conv_width), back(inner),
            back(inner), back(inner),
            pl.BlockSpec((1, states, inner), lambda i, s: (back_at(i, s), 0, 0)),
        ]
        + [whole(a) for a in (w_cat, conv_rows, head_rows, spread, chan)],
        (
            shape(rows // 2, width),
            shape(rows // 2, width),
            shape(conv_width + LANES, width),
            shape(8, conv_width),
            shape(8, LANES),
        ),
        [
            pl.BlockSpec((SPAN, width), lambda i, s: (jnp.where(i < half_spans, low_at(i), 0), 0)),
            pl.BlockSpec(
                (SPAN, width),
                lambda i, s: (jnp.where(i < half_spans, half_spans - 1, low_at(i)), 0),
            ),
            pl.BlockSpec((conv_width + LANES, width), lambda i, s: (0, 0)),
            pl.BlockSpec((8, conv_width), lambda i, s: (0, 0)),
            pl.BlockSpec((8, LANES), lambda i, s: (0, 0)),
        ],
        [
            pltpu.VMEM((SPAN + 8, conv_width), f32),
            pltpu.VMEM((states, inner), f32),
        ],
        2 * rows * (width * all_width * 2 + heads * SPAN * LANES * 2),
    )
    normed_own, normed_other = wide_tensor_sum(partial_sent, partial_kept, n_tensor)
    w_wide = w_cat.T.astype(f32)
    norm_grad = (
        jnp.sum(late[:conv_width] * w_wide[:conv_width], 0)
        + jnp.sum(late[conv_width:] * w_wide[conv_width + inner :], 0)
        + jnp.sum(early[inner:] * w_wide[conv_width : conv_width + inner], 0)
    ) / norm_gain

    def widen(values):
        flat = values.reshape(-1)
        return jnp.pad(flat, (0, -flat.size % width)).reshape(-1, width)

    bc_small = jnp.concatenate([conv_grad[:5, inner:].reshape(-1), norm_grad])
    bc_parts = pad_rows(
        jnp.concatenate([late[inner:conv_width], widen(bc_small)], 0), 16 * n_dp
    )
    order = steps_of(n_dp)
    order = order[1:2] + order[:1] + order[2:]
    bc_parts = axis_scatter(bc_parts, "tensor", n_tensor, [1])
    bc_parts = axis_scatter(bc_parts, "dp", n_dp, order)
    for step in steps_of(n_tensor)[1:]:
        bc_parts = bc_parts + lax.ppermute(bc_parts, "tensor", partners(n_tensor, step))
    bc_parts = axis_gather(bc_parts, "dp", n_dp, order)
    bc_parts = axis_gather(bc_parts, "tensor", n_tensor, [1])
    x_small = jnp.concatenate(
        [
            conv_grad[:5, :inner].reshape(-1),
            gate_grad[0],
            head_grad[0, :heads],
            head_grad[1, :heads],
            jnp.sum(conv_grad[5, :inner].reshape(heads, size), 1),
        ]
    )
    x_parts = pad_rows(
        jnp.concatenate(
            [late[:inner], late[conv_width : conv_width + heads], widen(x_small)], 0
        ),
        8 * n_dp,
    )
    x_parts = dp_sum(x_parts, n_dp, 0)
    x_small = x_parts[inner + heads :].reshape(-1)
    bc_small = bc_parts[bc_width:].reshape(-1)
    at = (taps + 1) * inner
    bc_at = (taps + 1) * bc_width
    mixed = join_halves(mixed_own, mixed_other, mine)
    output = (hidden.astype(f32) + cols[:, 4:5] * mixed).astype(bf16)
    place = mine.astype(jnp.int32).reshape(1)
    half_spec = pl.BlockSpec((SPAN, width), lambda i, s: (i % half_spans, 0))
    row_spec = pl.BlockSpec((SPAN, width), lambda i, s: (i, 0))
    (grad_hidden,) = call(
        finish_kernel,
        (spans,),
        (place,),
        (normed_own, normed_other, hidden, cotangent, gain),
        [half_spec, half_spec, row_spec, row_spec, whole(gain)],
        (shape(rows, width),),
        [row_spec],
        [],
        rows * width * 10,
    )
    return (
        output,
        grad_hidden,
        bc_small[bc_at : bc_at + width],
        x_parts[:inner].T,
        early_sum[inner:].T,
        x_parts[inner : inner + heads].T,
        bc_parts[:bc_width].T,
        x_small[: taps * inner].reshape(taps, inner),
        x_small[taps * inner : at],
        bc_small[: taps * bc_width].reshape(taps, bc_width),
        bc_small[taps * bc_width : bc_at],
        x_small[at + inner : at + inner + heads],
        x_small[at + inner + heads : at + inner + 2 * heads],
        x_small[at + inner + 2 * heads : at + inner + 3 * heads],
        x_small[at : at + inner],
        early_sum[:inner],
    )


def solution(mesh):
    return jax.shard_map(
        functools.partial(per_device, mesh.shape["dp"], mesh.shape["tensor"]),
        mesh=mesh,
        in_specs=(
            P("dp", None),
            P("dp", None),
            P("dp"),
            P("dp"),
            P(),
            P(None, "tensor"),
            P(None, "tensor"),
            P(None, "tensor"),
            P(),
            P(None, "tensor"),
            P("tensor"),
            P(),
            P(),
            P("tensor"),
            P("tensor"),
            P("tensor"),
            P("tensor"),
            P("tensor", None),
        ),
        out_specs=(
            P("dp", None),
            P("dp", None),
            P(),
            P(None, "tensor"),
            P(None, "tensor"),
            P(None, "tensor"),
            P(),
            P(None, "tensor"),
            P("tensor"),
            P(),
            P(),
            P("tensor"),
            P("tensor"),
            P("tensor"),
            P("tensor"),
            P("tensor", None),
        ),
        check_vma=False,
    )
```

time: 650 us -> 408 us (0.63)
  waiting for transfers between devices: 340 us -> 175 us
  matrix products: 107 us -> 0 us
  Pallas kernels: 0 us -> 97 us
  blocking collectives: 55.1 us -> 0 us
  starting transfers between devices: 0.08 us -> 32.5 us
  local copies, waits for them, and re-layouts: 64 us -> 49 us
  between operations: 16.7 us -> 1.8 us
  other arithmetic: 64.6 us -> 51 us
    psum x2 -> x0, waiting for transfers between devices: 340 us -> none  [the longest x1 244 us: per_device(): lax.psum(jnp.dot(out_in, w_out, preferred_element_type=jnp.float32), 'ten...]
    ppermute x0 -> x29, waiting for transfers between devices: none -> 175 us  [the longest x1 92.4 us: per_device(): lax.ppermute(bc_parts, 'tensor', partners(n_tensor, step))]
    dot_general x26 -> x0, matrix products: 106 us -> none  [the longest x1 9.81 us: per_device(): jnp.einsum('cphd,cqhd->chpq', grad_scan_blocks, inputs_blocks, preferred_...]
    pallas_call x0 -> x4, Pallas kernels: none -> 97 us  [call(): pl.pallas_call(kernel, grid_spec=pltpu.PrefetchScalarGridSpec(num_scalar_...]
    psum x3 -> x0, blocking collectives: 55.1 us -> none  [the longest x1 40.8 us: per_device(): lax.psum((grad_norm_gain, grad_w_x, grad_w_z, grad_w_dt, grad_conv_x, gra...]
    ppermute x0 -> x29, starting transfers between devices: none -> 32.5 us  [the longest x10 12.4 us: axis_gather(): other = lax.ppermute(values, axis, partners(count, step))]
    reduce_sum x12 -> x4, other arithmetic: 30 us -> 3.77 us  [the longest x1 1.46 us: per_device(): jnp.sum(early[inner:] * w_wide[conv_width:conv_width + inner], 0)]
    add x4 -> x17, other arithmetic: 0.86 us -> 23.9 us  [the longest x2 8.89 us: wide_tensor_sum(): values = values + lax.ppermute(values, 'tensor', partners(count, step))]
  transfers between devices with their start and end apart: 2 -> 29, of which waited for: 2 -> 14; matrix products, arithmetic and copies ran while one was open for 5% -> 20% of each run, Pallas kernels for 0% -> 11%
where the time goes in v2:
time: 408 us; the launch traced here: 406 us
  waiting for transfers between devices  175 us (43%)
  Pallas kernels  97 us (24%)
  other arithmetic  51 us (12%)
  local copies, waits for them, and re-layouts  49 us (12%)
  starting transfers between devices  32.5 us (8%)
    pallas_call x4, Pallas kernels, call(): pl.pallas_call(kernel, grid_spec=pltpu.PrefetchScalarGridSpec(num_scalar_...  97 us
    ppermute x1, waiting for transfers between devices, per_device(): lax.ppermute(bc_parts, 'tensor', partners(n_tensor, step))  92.4 us
    ppermute x10, waiting for transfers between devices, axis_gather(): other = lax.ppermute(values, axis, partners(count, step))  51.3 us
    ppermute x10, waiting for transfers between devices, axis_scatter(): lax.ppermute(take_half(values, 1 - mine), axis, partners(count, step))  28.3 us
    ppermute x10, starting transfers between devices, axis_gather(): other = lax.ppermute(values, axis, partners(count, step))  12.4 us
    ppermute x10, starting transfers between devices, axis_scatter(): lax.ppermute(take_half(values, 1 - mine), axis, partners(count, step))  11.4 us
    unnamed x50, local copies, waits for them, and re-layouts  8.9 us
    add x2, other arithmetic, wide_tensor_sum(): values = values + lax.ppermute(values, 'tensor', partners(count, step))  8.89 us
  transfers between devices with their start and end apart: 29, of which 14 were waited for; matrix products, arithmetic and copies ran while one was open for 20% of the time, Pallas kernels for 11%

profile of v2, /device:TPU:0, one launch (start us, length us, event | category | flops | bytes accessed | tf_op | source)
XLA Modules:
  0.0 406.4 jit_solution(15063812532032631892)
XLA Ops:
  7.3 1.0 pad.40.cols_ref
  12.5 3.1 convert_bitcast_fusion
  15.6 24.8 %shard_map.297 = (bf16[2048,768]{1,0:T(8,128)(2,1)}, f32[2048,640]{1,0:T(8,128)}, f32[2048,384]{1,0:T(8,128)}, f32[2048,128]{1,0:T(8,128)}, f32[2048,640]{1,0:T(...) custom-call(bf16[2048,768]{1,0:T(8,128)(2,1)} %hid_ref.3, ...), custom_call_target="tpu_custom_call" | custom-call | flops 5637144576 | bytes 33848320 | tf_op jit(solution)/shard_map/pallas_call | solution.py:397
  40.9 1.0 collective-permute-done
  42.7 2.9 collective-permute-start.1
  45.6 1.8 collective-permute-done.1
  47.4 1.3 add.188.sums_ref
  48.7 16.4 %shard_map.298 = (f32[1024,768]{1,0:T(8,128)}, f32[1024,768]{1,0:T(8,128)}, f32[2048,384]{1,0:T(8,128)}, bf16[2048,384]{1,0:T(8,128)(2,1)}, f32[768,768]{1,0:T(8,128)}, /*index=5*/f32[8,384]{1,0:T(8,128)}) custom-call(s32[1]{0:T(128)} %bitcast.1.shift_ref, f32[8,2,256]{2,1,0:T(2,128)} %add.188.sums_ref, f32[2048,384]{1,0:T(8,128)} %get-tuple-element.37.z_ref, ...), custom_call_target="tpu_custom_call" | custom-call | flops 3623878656 | bytes 29859840 | tf_op jit(solution)/shard_map/pallas_call | solution.py:397
  65.2 44.1 %shard_map.299 = (f32[1024,768]{1,0:T(8,128)}, f32[1024,768]{1,0:T(8,128)}, f32[768,768]{1,0:T(8,128)}, f32[8,640]{1,0:T(8,128)}, f32[8,128]{1,0:T(8,128)}) custom-call(s32[1]{0:T(128)} %bitcast.1.shift_ref, f32[2048,16]{1,0:T(8,128)} %pad.40.cols_ref, f32[8,1,256]{2,1,0:T(1,128)} %bitcast.50, bf16[2048,768]{1,0:T(8,128)(2,1)} %get-tuple-element.40.normed_ref, ...), custom_call_target="tpu_custom_call" | custom-call | flops 8858370048 | bytes 34050048 | tf_op jit(solution)/shard_map/pallas_call | solution.py:397
  109.8 3.0 copy.76
  112.9 2.1 slice.133
  114.9 1.3 slice.134
  116.9 1.3 slice.144
  118.3 2.4 slice.143
  120.6 3.0 copy.78
  123.7 1.3 reshape.133
  125.0 1.3 fusion.7
  126.3 1.5 fusion.6
  128.5 1.3 select_maximum_fusion.2
  132.8 1.3 slice_bitcast_fusion.4
  137.0 1.0 constant_dynamic-slice_fusion.5
  138.0 2.0 collective-permute-start.17
  141.6 1.6 collective-permute-start.9
  143.2 3.4 add.189
  146.6 1.6 collective-permute-start.3
  148.2 1.1 constant_dynamic-slice_fusion.2
  149.8 1.1 collective-permute-done.9
  150.9 1.0 dynamic-slice_add_fusion.6
  152.4 5.0 %add.192 = f32[1024,768]{1,0:T(8,128)} add(f32[1024,768]{1,0:T(8,128)} %get-tuple-element.49, f32[1024,768]{1,0:T(8,128)} %collective-permute-done.5) | non-fusion elementwise | flops 786432 | bytes 9437184 | tf_op jit(solution)/shard_map/add | solution.py:383
  157.4 1.6 collective-permute-start.6
  159.0 1.2 dynamic-slice_add_fusion.1
  160.2 1.6 collective-permute-start.18
  161.9 22.8 %collective-permute-done.10 = f32[48,768]{1,0:T(8,128)S(1)} collective-permute-done((f32[48,768]{1,0:T(8,128)S(1)}, f32[48,768]{1,0:T(8,128)S(1)}, u32[]{:S(2)}, u32[]{:S(2)}) %collective-permute-start.10) | collective-permute-done | bytes 147488 | tf_op jit(solution)/shard_map/ppermute | solution.py:363
  184.7 2.9 collective-permute-start.11
  187.6 1.4 dynamic-slice_add_fusion
  189.1 1.6 collective-permute-start.24
  191.6 1.5 collective-permute-start.12
  193.1 92.4 %collective-permute-done.12 = f32[24,768]{1,0:T(8,128)S(1)} collective-permute-done((f32[24,768]{1,0:T(8,128)S(1)}, f32[24,768]{1,0:T(8,128)S(1)}, u32[]{:S(2)}, u32[]{:S(2)}) %collective-permute-start.12) | collective-permute-done | bytes 73760 | tf_op jit(solution)/shard_map/ppermute | solution.py:636
  285.5 2.6 collective-permute-start.13
  288.6 10.5 %collective-permute-done.13 = f32[24,768]{1,0:T(8,128)S(1)} collective-permute-done((f32[24,768]{1,0:T(8,128)S(1)}, f32[24,768]{1,0:T(8,128)S(1)}, u32[]{:S(2)}, u32[]{:S(2)}) %collective-permute-start.13) | collective-permute-done | bytes 73760 | tf_op jit(solution)/shard_map/ppermute | solution.py:371
  299.8 3.0 collective-permute-done.19
  303.5 0.8 collective-permute-done.14
  304.4 8.3 %collective-permute-start.15 = (f32[96,768]{1,0:T(8,128)S(1)}, f32[96,768]{1,0:T(8,128)}, u32[]{:S(2)}, u32[]{:S(2)}) collective-permute-start(f32[96,768]{1,0:T(8,128)S(1)} %maximum_select_fusion.9), channel_id=1, source_target_pairs={{0,8},{4,12},{8,0},{12,4},{16,24},{20,28},{24,16},{28,20},{1,9},{5... | collective-permute-start | bytes 884744 | tf_op jit(solution)/shard_map/ppermute | solution.py:371
  312.7 4.0 add.190
  317.3 1.8 collective-permute-done.20
  319.1 1.2 maximum_select_fusion.8
  320.7 1.1 maximum_select_fusion.6
  321.9 11.0 %collective-permute-done.26 = f32[96,768]{1,0:T(8,128)S(1)} collective-permute-done((f32[96,768]{1,0:T(8,128)S(1)}, f32[96,768]{1,0:T(8,128)S(1)}, u32[]{:S(2)}, u32[]{:S(2)}) %collective-permute-start.26) | collective-permute-done | bytes 294944 | tf_op jit(solution)/shard_map/ppermute | solution.py:371
  333.1 4.9 %add.193.own_ref = f32[1024,768]{1,0:T(8,128)} add(f32[1024,768]{1,0:T(8,128)} %add.192, f32[1024,768]{1,0:T(8,128)} %collective-permute-done.6) | non-fusion elementwise | flops 786432 | bytes 9437184 | tf_op jit(solution)/shard_map/add | solution.py:385
  338.5 9.9 %collective-permute-done.27 = f32[192,768]{1,0:T(8,128)} collective-permute-done((f32[192,768]{1,0:T(8,128)S(1)}, f32[192,768]{1,0:T(8,128)}, u32[]{:S(2)}, u32[]{:S(2)}) %collective-permute-start.27) | collective-permute-done | bytes 589856 | tf_op jit(solution)/shard_map/ppermute | solution.py:371
  348.4 1.4 maximum_select_fusion.4
  351.6 1.3 slice.174
  352.8 1.2 slice.183
  354.1 1.1 copy.81
  355.2 1.3 slice.182
  356.6 1.4 maximum_select_fusion.2
  358.1 1.1 slice_bitcast_fusion.1
  359.2 2.7 copy.79
  364.2 17.2 %collective-permute-done.28 = f32[384,768]{1,0:T(8,128)} collective-permute-done((f32[384,768]{1,0:T(8,128)S(1)}, f32[384,768]{1,0:T(8,128)}, u32[]{:S(2)}, u32[]{:S(2)}) %collective-permute-start.28) | collective-permute-done | bytes 1179680 | tf_op jit(solution)/shard_map/ppermute | solution.py:371
  381.4 1.9 maximum_select_fusion.1
  383.3 1.6 fusion.19
  384.8 2.9 copy.80
  387.7 6.9 %fusion.2 = bf16[2048,768]{1,0:T(8,128)(2,1)} fusion(f32[1024,768]{1,0:T(8,128)} %collective-permute-done.4, f32[1024,768]{1,0:T(8,128)} %add.190, bf16[2048,768]{1,0:T(8,128)(2,1)S(1)} %copy-done, f32[2048]{0:T(1024)S(1)} %fusion.9, pred[]{:T(512)S(6)} %eq.104), kind=kLoop, calls=%fused_computation.3 | loop fusion | flops 11010048 | bytes 12591105 | tf_op jit(solution)/shard_map/convert_element_type | solution.py:660
  394.6 11.8 %shard_map.300 = f32[2048,768]{1,0:T(8,128)} custom-call(s32[1]{0:T(128)} %bitcast.15.place_ref, f32[1024,768]{1,0:T(8,128)} %add.193.own_ref, f32[1024,768]{1,0:T(8,128)} %collective-permute-done.7.other_ref, bf16[2048,768]{1,0:T(8,128)(2,1)} %hid_ref.3, bf16[2048,768]{1,0:T(8,128)(2,1)} %cot_ref.5, f32[1,768]{1,0:T(1,128)} %broadcast_in_dim.12.gain_ref), custom_call_target="tpu_custom_call" | custom-call | flops 15728640 | bytes 18877440 | tf_op jit(solution)/shard_map/pallas_call | solution.py:397
  (156 shorter events, 30.5 us)
Async XLA Ops:
  1.3 7.0 %copy-start.8 = (f32[2048]{0:T(1024)}, f32[2048]{0:T(1024)S(1)}, u32[]{:S(2)}) copy-start(f32[2048]{0:T(1024)S(1)} %convert_element_type.72) | copy-start | bytes 24580
  6.6 1.7 copy-start.10
  6.6 2.3 copy-start.12
  6.8 2.9 copy-start.15
  6.8 2.9 copy-start.17
  6.8 2.9 copy-start.20
  6.9 3.6 copy-start.16
  6.9 3.6 copy-start.18
  6.9 3.8 copy-start.19
  6.9 4.9 %copy-start.13 = (f32[4,384]{1,0:T(4,128)S(1)}, f32[4,384]{1,0:T(4,128)}, u32[]{:S(2)}) copy-start(f32[4,384]{1,0:T(4,128)} %param.27) | copy-start | bytes 18436
  6.9 4.9 %copy-start.14 = (f32[4,256]{1,0:T(4,128)S(1)}, f32[4,256]{1,0:T(4,128)}, u32[]{:S(2)}) copy-start(f32[4,256]{1,0:T(4,128)} %param.29) | copy-start | bytes 12292
  40.3 1.6 collective-permute-start
  42.7 4.7 %collective-permute-start.1 = (f32[8,2,256]{2,1,0:T(2,128)S(1)}, f32[8,2,256]{2,1,0:T(2,128)}, u32[]{:S(2)}, u32[]{:S(2)}) collective-permute-start(f32[8,2,256]{2,1,0:T(2,128)S(1)} %add.187), channel_id=1, source_target_pairs={{0,2},{1,3},{2,0},{3,1},{4,6},{5,7},{6,4},{7,5},{8,10},{9,11},{10,... | collective-permute-start | bytes 49160 | tf_op jit(solution)/shard_map/ppermute | solution.py:530
  65.1 78.1 %collective-permute-start.2 = (f32[1024,768]{1,0:T(8,128)}, f32[1024,768]{1,0:T(8,128)}, u32[]{:S(2)}, u32[]{:S(2)}) collective-permute-start(f32[1024,768]{1,0:T(8,128)} %get-tuple-element.42), channel_id=1, source_target_pairs={{0,1},{1,0},{2,3},{3,2},{4,5},{5,4},{6,7},{7,6},{8,9},{9,8},{10,11... | collective-permute-start | bytes 9437192 | tf_op jit(solution)/shard_map/ppermute | solution.py:383
  109.3 43.1 %collective-permute-start.5 = (f32[1024,768]{1,0:T(8,128)}, f32[1024,768]{1,0:T(8,128)}, u32[]{:S(2)}, u32[]{:S(2)}) collective-permute-start(f32[1024,768]{1,0:T(8,128)} %get-tuple-element.50), channel_id=1, source_target_pairs={{0,1},{1,0},{2,3},{3,2},{4,5},{5,4},{6,7},{7,6},{8,9},{9,8},{10,11... | collective-permute-start | bytes 9437192 | tf_op jit(solution)/shard_map/ppermute | solution.py:383
  125.0 2.8 copy-start.1
  127.8 0.7 copy-start.11
  127.8 0.7 copy-start.9
  128.5 7.7 %copy-start.6 = (f32[384,768]{1,0:T(8,128)S(1)}, f32[384,768]{1,0:T(8,128)}, u32[]{:S(2)}) copy-start(f32[384,768]{1,0:T(8,128)} %slice.143) | copy-start | bytes 3538948
  129.9 10.2 %collective-permute-start.8 = (f32[192,768]{1,0:T(8,128)S(1)}, f32[192,768]{1,0:T(8,128)S(1)}, u32[]{:S(2)}, u32[]{:S(2)}) collective-permute-start(f32[192,768]{1,0:T(8,128)S(1)} %constant_dynamic-slice_fusion.9), channel_id=1, source_target_pairs={{0,1},{1,0},{2,3},{3,2},{4,5},{5,4},{6,7},{7,6},{8,9},{9,8},{10,11... | collective-permute-start | bytes 1769480 | tf_op jit(solution)/shard_map/ppermute | solution.py:363
  137.0 4.7 %copy-start.4 = (f32[448,768]{1,0:T(8,128)}, f32[448,768]{1,0:T(8,128)S(1)}, u32[]{:S(2)}) copy-start(f32[448,768]{1,0:T(8,128)S(1)} %select_maximum_fusion) | copy-start | bytes 4128772
  138.0 21.0 %collective-permute-start.17 = (f32[224,768]{1,0:T(8,128)}, f32[224,768]{1,0:T(8,128)}, u32[]{:S(2)}, u32[]{:S(2)}) collective-permute-start(f32[224,768]{1,0:T(8,128)} %constant_dynamic-slice_fusion.5), channel_id=1, source_target_pairs={{0,4},{4,0},{8,12},{12,8},{16,20},{20,16},{24,28},{28,24},{1,5},{5... | collective-permute-start | bytes 2064392 | tf_op jit(solution)/shard_map/ppermute | solution.py:363
  140.1 0.8 copy-start.7
  141.6 9.3 %collective-permute-start.9 = (f32[96,768]{1,0:T(8,128)}, f32[96,768]{1,0:T(8,128)S(1)}, u32[]{:S(2)}, u32[]{:S(2)}) collective-permute-start(f32[96,768]{1,0:T(8,128)} %constant_dynamic-slice_fusion.8), channel_id=1, source_target_pairs={{0,8},{4,12},{8,0},{12,4},{16,24},{20,28},{24,16},{28,20},{1,9},{5... | collective-permute-start | bytes 884744 | tf_op jit(solution)/shard_map/ppermute | solution.py:363
  143.2 4.9 %copy-start.2 = (f32[768,768]{1,0:T(8,128)S(1)}, f32[768,768]{1,0:T(8,128)}, u32[]{:S(2)}) copy-start(f32[768,768]{1,0:T(8,128)} %get-tuple-element.53) | copy-start | bytes 7077892
  146.6 166.1 %collective-permute-start.3 = (f32[1024,768]{1,0:T(8,128)S(1)}, f32[1024,768]{1,0:T(8,128)}, u32[]{:S(2)}, u32[]{:S(2)}) collective-permute-start(f32[1024,768]{1,0:T(8,128)S(1)} %add.189), channel_id=1, source_target_pairs={{0,2},{1,3},{2,0},{3,1},{4,6},{5,7},{6,4},{7,5},{8,10},{9,11},{10,... | collective-permute-start | bytes 9437192 | tf_op jit(solution)/shard_map/ppermute | solution.py:385
  149.2 38.4 %collective-permute-start.23 = (f32[384,768]{1,0:T(8,128)}, f32[384,768]{1,0:T(8,128)}, u32[]{:S(2)}, u32[]{:S(2)}) collective-permute-start(f32[384,768]{1,0:T(8,128)} %constant_dynamic-slice_fusion.2), channel_id=1, source_target_pairs={{0,4},{4,0},{8,12},{12,8},{16,20},{20,16},{24,28},{28,24},{1,5},{5... | collective-permute-start | bytes 3538952 | tf_op jit(solution)/shard_map/ppermute | solution.py:363
  151.9 32.8 %collective-permute-start.10 = (f32[48,768]{1,0:T(8,128)S(1)}, f32[48,768]{1,0:T(8,128)S(1)}, u32[]{:S(2)}, u32[]{:S(2)}) collective-permute-start(f32[48,768]{1,0:T(8,128)S(1)} %constant_dynamic-slice_fusion.7), channel_id=1, source_target_pairs={{0,4},{4,0},{8,12},{12,8},{16,20},{20,16},{24,28},{28,24},{1,5},{5... | collective-permute-start | bytes 442376 | tf_op jit(solution)/shard_map/ppermute | solution.py:363
  152.4 6.6 %copy-start.5 = (f32[448,768]{1,0:T(8,128)S(1)}, f32[448,768]{1,0:T(8,128)}, u32[]{:S(2)}) copy-start(f32[448,768]{1,0:T(8,128)} %copy-done.4) | copy-start | bytes 4128772
  157.4 30.2 %copy-start.3 = (f32[768,768]{1,0:T(8,128)S(1)}, f32[768,768]{1,0:T(8,128)}, u32[]{:S(2)}) copy-start(f32[768,768]{1,0:T(8,128)} %get-tuple-element.53) | copy-start | bytes 7077892
  157.4 175.7 %collective-permute-start.6 = (f32[1024,768]{1,0:T(8,128)}, f32[1024,768]{1,0:T(8,128)}, u32[]{:S(2)}, u32[]{:S(2)}) collective-permute-start(f32[1024,768]{1,0:T(8,128)} %add.192), channel_id=1, source_target_pairs={{0,2},{1,3},{2,0},{3,1},{4,6},{5,7},{6,4},{7,5},{8,10},{9,11},{10,... | collective-permute-start | bytes 9437192 | tf_op jit(solution)/shard_map/ppermute | solution.py:385
  160.2 32.8 %collective-permute-start.18 = (f32[112,768]{1,0:T(8,128)S(1)}, f32[112,768]{1,0:T(8,128)S(1)}, u32[]{:S(2)}, u32[]{:S(2)}) collective-permute-start(f32[112,768]{1,0:T(8,128)S(1)} %constant_dynamic-slice_fusion.4), channel_id=1, source_target_pairs={{0,8},{4,12},{8,0},{12,4},{16,24},{20,28},{24,16},{28,20},{1,9},{5... | collective-permute-start | bytes 1032200 | tf_op jit(solution)/shard_map/ppermute | solution.py:363
  184.7 6.8 %collective-permute-start.11 = (f32[24,768]{1,0:T(8,128)S(1)}, f32[24,768]{1,0:T(8,128)S(1)}, u32[]{:S(2)}, u32[]{:S(2)}) collective-permute-start(f32[24,768]{1,0:T(8,128)S(1)} %constant_dynamic-slice_fusion.6), channel_id=1, source_target_pairs={{0,16},{4,20},{8,24},{12,28},{16,0},{20,4},{24,8},{28,12},{1,17},{... | collective-permute-start | bytes 221192 | tf_op jit(solution)/shard_map/ppermute | solution.py:363
  189.1 110.5 %collective-permute-start.24 = (f32[192,768]{1,0:T(8,128)S(1)}, f32[192,768]{1,0:T(8,128)S(1)}, u32[]{:S(2)}, u32[]{:S(2)}) collective-permute-start(f32[192,768]{1,0:T(8,128)S(1)} %constant_dynamic-slice_fusion.1), channel_id=1, source_target_pairs={{0,8},{4,12},{8,0},{12,4},{16,24},{20,28},{24,16},{28,20},{1,9},{5... | collective-permute-start | bytes 1769480 | tf_op jit(solution)/shard_map/ppermute | solution.py:363
  191.6 94.0 %collective-permute-start.12 = (f32[24,768]{1,0:T(8,128)S(1)}, f32[24,768]{1,0:T(8,128)S(1)}, u32[]{:S(2)}, u32[]{:S(2)}) collective-permute-start(f32[24,768]{1,0:T(8,128)S(1)} %dynamic-slice_add_fusion.9), channel_id=1, source_target_pairs={{0,2},{1,3},{2,0},{3,1},{4,6},{5,7},{6,4},{7,5},{8,10},{9,11},{10,... | collective-permute-start | bytes 221192 | tf_op jit(solution)/shard_map/ppermute | solution.py:636
  285.5 13.6 %collective-permute-start.13 = (f32[24,768]{1,0:T(8,128)S(1)}, f32[24,768]{1,0:T(8,128)S(1)}, u32[]{:S(2)}, u32[]{:S(2)}) collective-permute-start(f32[24,768]{1,0:T(8,128)S(1)} %add.211), channel_id=1, source_target_pairs={{0,16},{4,20},{8,24},{12,28},{16,0},{20,4},{24,8},{28,12},{1,17},{... | collective-permute-start | bytes 221192 | tf_op jit(solution)/shard_map/ppermute | solution.py:371
  288.2 14.6 %collective-permute-start.19 = (f32[56,768]{1,0:T(8,128)S(1)}, f32[56,768]{1,0:T(8,128)S(1)}, u32[]{:S(2)}, u32[]{:S(2)}) collective-permute-start(f32[56,768]{1,0:T(8,128)S(1)} %constant_dynamic-slice_fusion.3), channel_id=1, source_target_pairs={{0,16},{4,20},{8,24},{12,28},{16,0},{20,4},{24,8},{28,12},{1,17},{... | collective-permute-start | bytes 516104 | tf_op jit(solution)/shard_map/ppermute | solution.py:363
  299.1 5.2 %collective-permute-start.14 = (f32[48,768]{1,0:T(8,128)S(1)}, f32[48,768]{1,0:T(8,128)S(1)}, u32[]{:S(2)}, u32[]{:S(2)}) collective-permute-start(f32[48,768]{1,0:T(8,128)S(1)} %maximum_select_fusion.10), channel_id=1, source_target_pairs={{0,4},{4,0},{8,12},{12,8},{16,20},{20,16},{24,28},{28,24},{1,5},{5... | collective-permute-start | bytes 442376 | tf_op jit(solution)/shard_map/ppermute | solution.py:371
  299.7 17.5 %collective-permute-start.25 = (f32[96,768]{1,0:T(8,128)S(1)}, f32[96,768]{1,0:T(8,128)S(1)}, u32[]{:S(2)}, u32[]{:S(2)}) collective-permute-start(f32[96,768]{1,0:T(8,128)S(1)} %constant_dynamic-slice_fusion), channel_id=1, source_target_pairs={{0,16},{4,20},{8,24},{12,28},{16,0},{20,4},{24,8},{28,12},{1,17},{... | collective-permute-start | bytes 884744 | tf_op jit(solution)/shard_map/ppermute | solution.py:363
  303.5 15.6 %collective-permute-start.20 = (f32[56,768]{1,0:T(8,128)}, f32[56,768]{1,0:T(8,128)}, u32[]{:S(2)}, u32[]{:S(2)}) collective-permute-start(f32[56,768]{1,0:T(8,128)} %dynamic-slice_add_fusion.7), channel_id=1, source_target_pairs={{0,16},{4,20},{8,24},{12,28},{16,0},{20,4},{24,8},{28,12},{1,17},{... | collective-permute-start | bytes 516104 | tf_op jit(solution)/shard_map/ppermute | solution.py:371
  304.4 16.4 %collective-permute-start.15 = (f32[96,768]{1,0:T(8,128)S(1)}, f32[96,768]{1,0:T(8,128)}, u32[]{:S(2)}, u32[]{:S(2)}) collective-permute-start(f32[96,768]{1,0:T(8,128)S(1)} %maximum_select_fusion.9), channel_id=1, source_target_pairs={{0,8},{4,12},{8,0},{12,4},{16,24},{20,28},{24,16},{28,20},{1,9},{5... | collective-permute-start | bytes 884744 | tf_op jit(solution)/shard_map/ppermute | solution.py:371
  316.7 71.1 %collective-permute-start.4 = (f32[1024,768]{1,0:T(8,128)}, f32[1024,768]{1,0:T(8,128)}, u32[]{:S(2)}, u32[]{:S(2)}) collective-permute-start(f32[1024,768]{1,0:T(8,128)} %add.190), channel_id=1, source_target_pairs={{0,1},{1,0},{2,3},{3,2},{4,5},{5,4},{6,7},{7,6},{8,9},{9,8},{10,11... | collective-permute-start | bytes 9437192 | tf_op jit(solution)/shard_map/ppermute | solution.py:386
  317.2 15.7 %collective-permute-start.26 = (f32[96,768]{1,0:T(8,128)S(1)}, f32[96,768]{1,0:T(8,128)S(1)}, u32[]{:S(2)}, u32[]{:S(2)}) collective-permute-start(f32[96,768]{1,0:T(8,128)S(1)} %dynamic-slice_add_fusion.5), channel_id=1, source_target_pairs={{0,16},{4,20},{8,24},{12,28},{16,0},{20,4},{24,8},{28,12},{1,17},{... | collective-permute-start | bytes 884744 | tf_op jit(solution)/shard_map/ppermute | solution.py:371
  320.3 17.7 %collective-permute-start.21 = (f32[112,768]{1,0:T(8,128)S(1)}, f32[112,768]{1,0:T(8,128)S(1)}, u32[]{:S(2)}, u32[]{:S(2)}) collective-permute-start(f32[112,768]{1,0:T(8,128)S(1)} %maximum_select_fusion.8), channel_id=1, source_target_pairs={{0,8},{4,12},{8,0},{12,4},{16,24},{20,28},{24,16},{28,20},{1,9},{5... | collective-permute-start | bytes 1032200 | tf_op jit(solution)/shard_map/ppermute | solution.py:371
  321.9 16.5 %collective-permute-start.16 = (f32[192,768]{1,0:T(8,128)S(1)}, f32[192,768]{1,0:T(8,128)S(1)}, u32[]{:S(2)}, u32[]{:S(2)}) collective-permute-start(f32[192,768]{1,0:T(8,128)S(1)} %maximum_select_fusion.6), channel_id=1, source_target_pairs={{0,1},{1,0},{2,3},{3,2},{4,5},{5,4},{6,7},{7,6},{8,9},{9,8},{10,11... | collective-permute-start | bytes 1769480 | tf_op jit(solution)/shard_map/ppermute | solution.py:371
  333.0 15.4 %collective-permute-start.27 = (f32[192,768]{1,0:T(8,128)S(1)}, f32[192,768]{1,0:T(8,128)}, u32[]{:S(2)}, u32[]{:S(2)}) collective-permute-start(f32[192,768]{1,0:T(8,128)S(1)} %maximum_select_fusion.7), channel_id=1, source_target_pairs={{0,8},{4,12},{8,0},{12,4},{16,24},{20,28},{24,16},{28,20},{1,9},{5... | collective-permute-start | bytes 1769480 | tf_op jit(solution)/shard_map/ppermute | solution.py:371
  338.0 56.6 %collective-permute-start.7 = (f32[1024,768]{1,0:T(8,128)}, f32[1024,768]{1,0:T(8,128)}, u32[]{:S(2)}, u32[]{:S(2)}) collective-permute-start(f32[1024,768]{1,0:T(8,128)} %add.193.own_ref), channel_id=1, source_target_pairs={{0,1},{1,0},{2,3},{3,2},{4,5},{5,4},{6,7},{7,6},{8,9},{9,8},{10,11... | collective-permute-start | bytes 9437192 | tf_op jit(solution)/shard_map/ppermute | solution.py:386
  338.1 18.5 %collective-permute-start.22 = (f32[224,768]{1,0:T(8,128)S(1)}, f32[224,768]{1,0:T(8,128)}, u32[]{:S(2)}, u32[]{:S(2)}) collective-permute-start(f32[224,768]{1,0:T(8,128)S(1)} %maximum_select_fusion.5), channel_id=1, source_target_pairs={{0,4},{4,0},{8,12},{12,8},{16,20},{20,16},{24,28},{28,24},{1,5},{5... | collective-permute-start | bytes 2064392 | tf_op jit(solution)/shard_map/ppermute | solution.py:371
  349.7 31.7 %collective-permute-start.28 = (f32[384,768]{1,0:T(8,128)S(1)}, f32[384,768]{1,0:T(8,128)}, u32[]{:S(2)}, u32[]{:S(2)}) collective-permute-start(f32[384,768]{1,0:T(8,128)S(1)} %maximum_select_fusion.4), channel_id=1, source_target_pairs={{0,4},{4,0},{8,12},{12,8},{16,20},{20,16},{24,28},{28,24},{1,5},{5... | collective-permute-start | bytes 3538952 | tf_op jit(solution)/shard_map/ppermute | solution.py:371
  383.3 4.5 %copy-start = (bf16[2048,768]{1,0:T(8,128)(2,1)S(1)}, bf16[2048,768]{1,0:T(8,128)(2,1)}, u32[]{:S(2)}) copy-start(bf16[2048,768]{1,0:T(8,128)(2,1)} %hid_ref.3) | copy-start | bytes 9437188

commit v3 on v2

--- a/solution.py
+++ b/solution.py
@@ -146,17 +146,50 @@
     sums_ref[0] = jnp.where(lane == 0, squares, cross).T[0:2]
 
 
+def split_refs(refs, count):
+    return (refs[:count], refs[count:]) if len(refs) > 7 else ((), refs)
+
+
+def begin_sums(targets, sources):
+    @pl.when(pl.program_id(0) == 0)
+    def _():
+        for place, target in enumerate(targets):
+            target[...] = sources[place][...] if sources else jnp.zeros_like(target)
+
+
+def store_halves(place_ref, values, sent_ref, kept_ref):
+    half = values.shape[1] // 2
+
+    @pl.when(place_ref[0] == 0)
+    def _():
+        kept_ref[...] = values[:, :half]
+        sent_ref[...] = values[:, half:]
+
+    @pl.when(place_ref[0] == 1)
+    def _():
+        kept_ref[...] = values[:, half:]
+        sent_ref[...] = values[:, :half]
+
+
+def join_columns(place_ref, own_ref, other_ref, write):
+    own, other = own_ref[...], other_ref[...]
+
+    @pl.when(place_ref[0] == 0)
+    def _():
+        write(jnp.concatenate([own, other], 1))
+
+    @pl.when(place_ref[0] == 1)
+    def _():
+        write(jnp.concatenate([other, own], 1))
+
+
 def gate_kernel(
-    shift_ref, sums_ref, z_ref, y_ref, gin_ref, cot_ref, cols_ref, normed_ref, wout_ref, chan_ref,
-    sent_ref, kept_ref, gy_ref, gz_ref, weights_ref, gain_ref, *, inner, inner_all,
+    place_ref, sums_ref, z_ref, y_ref, gin_ref, cot_ref, cols_ref, normed_ref, wout_ref, chan_ref,
+    *refs, inner, inner_all,
 ):
-    index = pl.program_id(0)
-    half = pl.num_programs(0) // 2
-
-    @pl.when(index == 0)
-    def _():
-        weights_ref[...] = jnp.zeros_like(weights_ref)
-        gain_ref[...] = jnp.zeros_like(gain_ref)
+    sums_of, outs = split_refs(refs, 3)
+    sent_ref, kept_ref, gy_ref, gz_ref, wout_grad_ref, wz_grad_ref, gain_ref = outs
+    begin_sums((wout_grad_ref, wz_grad_ref, gain_ref), sums_of)
 
     sums = sums_ref[0]
     copies = inner // LANES
@@ -170,18 +203,9 @@
     gated = y_flat * active
     scaled = gated * inv_gate
     out_in = (scaled * chan_ref[1:2]).astype(jnp.bfloat16)
-    mixed = dot(out_in, wout_ref[...])
-
-    @pl.when(index < half)
-    def _():
-        sent_ref[...] = mixed
-
-    @pl.when(index >= half)
-    def _():
-        kept_ref[...] = mixed
-
+    store_halves(place_ref, dot(out_in, wout_ref[...]), sent_ref, kept_ref)
     grad_mix = (cols_ref[:, 4:5] * cot_ref[...].astype(jnp.float32)).astype(jnp.bfloat16)
-    weights_ref[0:inner, :] += dot(out_in, grad_mix, FIRST)
+    wout_grad_ref[...] += dot(out_in, grad_mix, FIRST)
     grad_in = gin_ref[...]
     gain_ref[0:1, :] += jnp.sum(grad_in * scaled, 0, keepdims=True)
     grad_gated = inv_gate * (
@@ -190,25 +214,20 @@
     gy_ref[...] = grad_gated * active
     grad_z = (grad_gated * y_flat * (sig * (1.0 + gate_in * (1.0 - sig)))).astype(jnp.bfloat16)
     gz_ref[...] = grad_z
-    weights_ref[inner : 2 * inner, :] += dot(grad_z, normed_ref[...], FIRST)
+    wz_grad_ref[...] += dot(normed_ref[...], grad_z, FIRST)
 
 
 def bwd_kernel(
-    shift_ref, cols_ref, seg_ref, normed_ref, conv_in_ref, dt_ref, pre_ref, y_ref, gy_ref, gz_ref,
-    carried_ref, wcat_ref, conv_ref, head_ref, spread_ref, chan_ref,
-    sent_ref, kept_ref, weights_ref, conv_grad_ref, head_grad_ref, ext_ref, flow_ref,
-    *, heads, inner, conv_width,
+    place_ref, cols_ref, seg_ref, normed_ref, conv_in_ref, dt_ref, pre_ref, y_ref, gy_ref, gz_ref,
+    carried_ref, wcat_ref, conv_ref, head_ref, spread_ref, chan_ref, *refs,
+    heads, inner, conv_width,
 ):
-    index = pl.program_id(0)
-    half = pl.num_programs(0) // 2
-
-    @pl.when(index == 0)
-    def _():
-        weights_ref[...] = jnp.zeros_like(weights_ref)
-        conv_grad_ref[...] = jnp.zeros_like(conv_grad_ref)
-        head_grad_ref[...] = jnp.zeros_like(head_grad_ref)
-
-    @pl.when((index == 0) | (index == half))
+    (ext_ref, flow_ref), refs = refs[-2:], refs[:-2]
+    sums_of, outs = split_refs(refs, 5)
+    sent_ref, kept_ref, wx_grad_ref, wbc_grad_ref, wdt_grad_ref, conv_grad_ref, head_grad_ref = outs
+    begin_sums((wx_grad_ref, wbc_grad_ref, wdt_grad_ref, conv_grad_ref, head_grad_ref), sums_of)
+
+    @pl.when(pl.program_id(0) == 0)
     def _():
         ext_ref[SPAN : SPAN + 8, :] = jnp.zeros((8, conv_width), jnp.float32)
         flow_ref[...] = jnp.zeros_like(flow_ref)
@@ -292,19 +311,11 @@
     conv_low = grad_conv_in.astype(jnp.bfloat16)
     dt_low = grad_dt.astype(jnp.bfloat16)
     low = jnp.concatenate([conv_low, gz_ref[...], dt_low], 1)
-    partial = dot(low, wcat_ref[...], LAST)
-
-    @pl.when(index < half)
-    def _():
-        sent_ref[...] = partial
-
-    @pl.when(index >= half)
-    def _():
-        kept_ref[...] = partial
-
+    store_halves(place_ref, dot(low, wcat_ref[...], LAST), sent_ref, kept_ref)
     normed = normed_ref[...]
-    weights_ref[0:conv_width, :] += dot(conv_low, normed, FIRST)
-    weights_ref[conv_width:, :] += dot(dt_low, normed, FIRST)
+    wx_grad_ref[...] += dot(normed, conv_low[:, :inner], FIRST)
+    wbc_grad_ref[...] += dot(normed, conv_low[:, inner:], FIRST)
+    wdt_grad_ref[...] += dot(dt_low, normed, FIRST)
 
 
 def upper_ones():
@@ -313,9 +324,19 @@
     return down <= across
 
 
-def finish_kernel(place_ref, own_ref, other_ref, hid_ref, cot_ref, gain_ref, out_ref):
-    half = pl.num_programs(0) // 2
-    mine = pl.program_id(0) // half == place_ref[0]
+def output_kernel(place_ref, own_ref, other_ref, hid_ref, cols_ref, *refs):
+    out_ref = refs[-1]
+
+    def write(values):
+        out_ref[...] = (hid_ref[...].astype(jnp.float32) + cols_ref[:, 4:5] * values).astype(
+            jnp.bfloat16
+        )
+
+    join_columns(place_ref, own_ref, other_ref, write)
+
+
+def finish_kernel(place_ref, own_ref, other_ref, hid_ref, cot_ref, gain_ref, *refs):
+    out_ref = refs[-1]
     hid = hid_ref[...].astype(jnp.float32)
     inv_rms = lax.rsqrt(jnp.mean(hid * hid, -1, keepdims=True) + EPS)
 
@@ -328,13 +349,7 @@
             - hid * (inv_rms * inv_rms * inv_rms * inner)
         )
 
-    @pl.when(mine)
-    def _():
-        write(own_ref[...])
-
-    @pl.when(jnp.logical_not(mine))
-    def _():
-        write(other_ref[...])
+    join_columns(place_ref, own_ref, other_ref, write)
 
 
 def partners(count, step):
@@ -373,24 +388,34 @@
     return values
 
 
-def dp_sum(values, count, first):
+def dp_order(count, first):
     order = steps_of(count)
-    order = order[first:2] + order[:first] + order[2:]
-    return axis_gather(axis_scatter(values, "dp", count, order), "dp", count, order)
-
-
-def wide_tensor_sum(sent, kept, count):
-    values = kept + lax.ppermute(sent, "tensor", partners(count, 1))
+    return order[first:2] + order[:first] + order[2:]
+
+
+def together(*values):
+    return lax.optimization_barrier(values)
+
+
+def chip_sum(sent, kept, count):
+    return kept + lax.ppermute(sent, "tensor", partners(count, 1))
+
+
+def far_sum(values, count):
     for step in steps_of(count)[1:]:
         values = values + lax.ppermute(values, "tensor", partners(count, step))
-    return values, lax.ppermute(values, "tensor", partners(count, 1))
+    return values
+
+
+def chip_other(values, count):
+    return lax.ppermute(values, "tensor", partners(count, 1))
 
 
 def pad_rows(values, multiple):
     return jnp.pad(values, ((0, -values.shape[0] % multiple), (0, 0)))
 
 
-def call(kernel, grid, prefetch, ins, in_specs, outs, out_specs, scratch, flops):
+def call(kernel, grid, prefetch, ins, in_specs, outs, out_specs, scratch, flops, alias=None):
     moved = sum(a.size * a.dtype.itemsize for a in ins) + sum(
         o.size * o.dtype.itemsize for o in outs
     )
@@ -404,6 +429,7 @@
             scratch_shapes=scratch,
         ),
         out_shape=outs,
+        input_output_aliases=alias or {},
         cost_estimate=pl.CostEstimate(flops=flops, bytes_accessed=moved, transcendentals=0),
     )(*prefetch, *ins)
 
@@ -496,146 +522,190 @@
     def whole(array):
         return pl.BlockSpec(array.shape, lambda *_: (0,) * len(array.shape))
 
-    def plain(columns):
-        return pl.BlockSpec((SPAN, columns), lambda i: (i, 0))
-
-    normed, conv_in, gate_in, dt_part, pre, y_flat, grad_in, carried, sums = call(
-        functools.partial(fwd_kernel, heads=heads, inner=inner, conv_width=conv_width),
-        (spans,),
-        (),
-        (hidden, cotangent, cols, seg_rows, gain, w_cat, w_out, conv_rows, head_rows, spread, chan),
-        [plain(width), plain(width), plain(16), pl.BlockSpec((1, 1, SPAN), lambda i: (i, 0, 0))]
-        + [whole(a) for a in (gain, w_cat, w_out, conv_rows, head_rows, spread, chan)],
-        (
-            shape(rows, width, dtype=bf16),
-            shape(rows, conv_width),
-            shape(rows, inner),
-            shape(rows, LANES),
-            shape(rows, conv_width),
-            shape(rows, inner),
-            shape(rows, inner),
-            shape(spans, states, inner, dtype=bf16),
-            shape(spans, 2, SPAN),
-        ),
-        [
-            plain(width), plain(conv_width), plain(inner), plain(LANES), plain(conv_width),
-            plain(inner), plain(inner),
-            pl.BlockSpec((1, states, inner), lambda i: (i, 0, 0)),
-            pl.BlockSpec((1, 2, SPAN), lambda i: (i, 0, 0)),
-        ],
-        [pltpu.VMEM((SPAN + 8, conv_width), f32), pltpu.VMEM((states, inner), f32)],
-        2 * rows * (width * (all_width + inner) + heads * SPAN * LANES),
-    )
-    for step in steps_of(n_tensor):
-        sums = sums + lax.ppermute(sums, "tensor", partners(n_tensor, step))
-    shift = (half_spans * (1 - mine)).astype(jnp.int32).reshape(1)
-
-    def turned(columns):
-        return pl.BlockSpec((SPAN, columns), lambda i, s: ((i + s[0]) % spans, 0))
-
-    sent_spec = pl.BlockSpec((SPAN, width), lambda i, s: (jnp.minimum(i, half_spans - 1), 0))
-    kept_spec = pl.BlockSpec((SPAN, width), lambda i, s: (jnp.maximum(i - half_spans, 0), 0))
-    mixed_sent, mixed_kept, grad_y, grad_z, early, gate_grad = call(
-        functools.partial(gate_kernel, inner=inner, inner_all=inner * n_tensor),
-        (spans,),
-        (shift,),
-        (sums, gate_in, y_flat, grad_in, cotangent, cols, normed, w_out, chan),
-        [
-            pl.BlockSpec((1, 2, SPAN), lambda i, s: ((i + s[0]) % spans, 0, 0)),
-            turned(inner), turned(inner), turned(inner), turned(width), turned(16),
-            turned(width), whole(w_out), whole(chan),
-        ],
-        (
-            shape(rows // 2, width),
-            shape(rows // 2, width),
-            shape(rows, inner),
-            shape(rows, inner, dtype=bf16),
-            shape(2 * inner, width),
-            shape(8, inner),
-        ),
-        [
-            sent_spec, kept_spec, turned(inner), turned(inner),
-            pl.BlockSpec((2 * inner, width), lambda i, s: (0, 0)),
-            pl.BlockSpec((8, inner), lambda i, s: (0, 0)),
-        ],
-        [],
-        2 * rows * width * inner * 3,
-    )
-    mixed_own, mixed_other = wide_tensor_sum(mixed_sent, mixed_kept, n_tensor)
-    early_sum = dp_sum(early, n_dp, 0)
-
-    def back_at(i, s):
-        turn = i // half_spans
-        return ((turn + s[0] // half_spans) % 2) * half_spans + half_spans - 1 - i % half_spans
+    def fixed(*dims):
+        return pl.BlockSpec(dims, lambda *_: (0,) * len(dims))
+
+    def local(columns):
+        return pl.BlockSpec((SPAN, columns), lambda i, *_: (i, 0))
 
     def back(columns):
-        return pl.BlockSpec((SPAN, columns), lambda i, s: (back_at(i, s), 0))
-
-    def low_at(i):
-        return half_spans - 1 - i % half_spans
-
-    partial_sent, partial_kept, late, conv_grad, head_grad = call(
-        functools.partial(bwd_kernel, heads=heads, inner=inner, conv_width=conv_width),
-        (spans,),
-        (shift,),
-        (
-            cols, seg_rows, normed, conv_in, dt_part, pre, y_flat, grad_y, grad_z, carried, w_cat,
-            conv_rows, head_rows, spread, chan,
-        ),
-        [
-            back(16), pl.BlockSpec((1, 1, SPAN), lambda i, s: (back_at(i, s), 0, 0)),
-            back(width), back(conv_width), back(LANES), back(conv_width), back(inner),
-            back(inner), back(inner),
-            pl.BlockSpec((1, states, inner), lambda i, s: (back_at(i, s), 0, 0)),
-        ]
-        + [whole(a) for a in (w_cat, conv_rows, head_rows, spread, chan)],
-        (
-            shape(rows // 2, width),
-            shape(rows // 2, width),
-            shape(conv_width + LANES, width),
+        return pl.BlockSpec((SPAN, columns), lambda i, *_: (half_spans - 1 - i, 0))
+
+    place = mine.astype(jnp.int32).reshape(1)
+    half_rows = rows // 2
+    grid = (half_spans,)
+
+    def forward(half):
+        base = half * half_spans
+        full = lambda columns: pl.BlockSpec((SPAN, columns), lambda i: (base + i, 0))
+        return call(
+            functools.partial(fwd_kernel, heads=heads, inner=inner, conv_width=conv_width),
+            grid,
+            (),
+            (
+                hidden, cotangent, cols, seg_rows, gain, w_cat, w_out, conv_rows, head_rows,
+                spread, chan,
+            ),
+            [
+                full(width), full(width), full(16),
+                pl.BlockSpec((1, 1, SPAN), lambda i: (base + i, 0, 0)),
+            ]
+            + [whole(a) for a in (gain, w_cat, w_out, conv_rows, head_rows, spread, chan)],
+            (
+                shape(half_rows, width, dtype=bf16),
+                shape(half_rows, conv_width),
+                shape(half_rows, inner),
+                shape(half_rows, LANES),
+                shape(half_rows, conv_width),
+                shape(half_rows, inner),
+                shape(half_rows, inner),
+                shape(half_spans, states, inner, dtype=bf16),
+                shape(half_spans, 2, SPAN),
+            ),
+            [
+                local(width), local(conv_width), local(inner), local(LANES), local(conv_width),
+                local(inner), local(inner),
+                pl.BlockSpec((1, states, inner), lambda i: (i, 0, 0)),
+                pl.BlockSpec((1, 2, SPAN), lambda i: (i, 0, 0)),
+            ],
+            [pltpu.VMEM((SPAN + 8, conv_width), f32), pltpu.VMEM((states, inner), f32)],
+            12_000_000_000,
+        )
+
+    def tensor_small(sums):
+        for step in steps_of(n_tensor):
+            sums = sums + lax.ppermute(sums, "tensor", partners(n_tensor, step))
+        return sums
+
+    def gate(half, sums, gate_in, y_flat, grad_in, normed, before):
+        base = half * half_spans
+        full = lambda columns: pl.BlockSpec((SPAN, columns), lambda i, s: (base + i, 0))
+        totals = (shape(inner, width), shape(width, inner), shape(8, inner))
+        return call(
+            functools.partial(gate_kernel, inner=inner, inner_all=inner * n_tensor),
+            grid,
+            (place,),
+            (sums, gate_in, y_flat, grad_in, cotangent, cols, normed, w_out, chan) + before,
+            [
+                pl.BlockSpec((1, 2, SPAN), lambda i, s: (i, 0, 0)),
+                local(inner), local(inner), local(inner), full(width), full(16),
+                local(width), whole(w_out), whole(chan),
+            ]
+            + [whole(a) for a in before],
+            (
+                shape(half_rows, width // 2),
+                shape(half_rows, width // 2),
+                shape(half_rows, inner),
+                shape(half_rows, inner, dtype=bf16),
+            )
+            + totals,
+            [local(width // 2), local(width // 2), local(inner), local(inner)]
+            + [fixed(*a.shape) for a in totals],
+            [],
+            8_000_000_000,
+        )
+
+    def backward(half, normed, conv_in, dt_part, pre, y_flat, grad_y, grad_z, carried, before):
+        base = half * half_spans
+        turn = lambda i: base + half_spans - 1 - i
+        full = lambda columns: pl.BlockSpec((SPAN, columns), lambda i, s: (turn(i), 0))
+        totals = (
+            shape(width, inner),
+            shape(width, bc_width),
+            shape(LANES, width),
             shape(8, conv_width),
             shape(8, LANES),
-        ),
-        [
-            pl.BlockSpec((SPAN, width), lambda i, s: (jnp.where(i < half_spans, low_at(i), 0), 0)),
-            pl.BlockSpec(
-                (SPAN, width),
-                lambda i, s: (jnp.where(i < half_spans, half_spans - 1, low_at(i)), 0),
-            ),
-            pl.BlockSpec((conv_width + LANES, width), lambda i, s: (0, 0)),
-            pl.BlockSpec((8, conv_width), lambda i, s: (0, 0)),
-            pl.BlockSpec((8, LANES), lambda i, s: (0, 0)),
-        ],
-        [
-            pltpu.VMEM((SPAN + 8, conv_width), f32),
-            pltpu.VMEM((states, inner), f32),
-        ],
-        2 * rows * (width * all_width * 2 + heads * SPAN * LANES * 2),
-    )
-    normed_own, normed_other = wide_tensor_sum(partial_sent, partial_kept, n_tensor)
-    w_wide = w_cat.T.astype(f32)
+        )
+        return call(
+            functools.partial(bwd_kernel, heads=heads, inner=inner, conv_width=conv_width),
+            grid,
+            (place,),
+            (
+                cols, seg_rows, normed, conv_in, dt_part, pre, y_flat, grad_y, grad_z, carried,
+                w_cat, conv_rows, head_rows, spread, chan,
+            )
+            + before,
+            [
+                full(16), pl.BlockSpec((1, 1, SPAN), lambda i, s: (turn(i), 0, 0)),
+                back(width), back(conv_width), back(LANES), back(conv_width), back(inner),
+                back(inner), back(inner),
+                pl.BlockSpec((1, states, inner), lambda i, s: (half_spans - 1 - i, 0, 0)),
+            ]
+            + [whole(a) for a in (w_cat, conv_rows, head_rows, spread, chan)]
+            + [whole(a) for a in before],
+            (shape(half_rows, width // 2), shape(half_rows, width // 2)) + totals,
+            [back(width // 2), back(width // 2)] + [fixed(*a.shape) for a in totals],
+            [pltpu.VMEM((SPAN + 8, conv_width), f32), pltpu.VMEM((states, inner), f32)],
+            20_000_000_000,
+        )
+
+    def placed(kernel, half, own, other, extras, extra_specs, dtype, before):
+        base = half * half_spans
+        full = lambda columns: pl.BlockSpec((SPAN, columns), lambda i, s: (base + i, 0))
+        specs = [whole(a) if spec is None else full(spec) for a, spec in zip(extras, extra_specs)]
+        (made,) = call(
+            kernel,
+            grid,
+            (place,),
+            (own, other) + extras + before,
+            [local(width // 2)] * 2 + specs + [pl.BlockSpec(memory_space=pl.ANY)] * len(before),
+            (shape(rows, width, dtype=dtype),),
+            [full(width)],
+            [],
+            3_000_000_000,
+            {3 + len(extras): 0} if before else None,
+        )
+        return made
+
+    normed_a, conv_a, z_a, dt_a, pre_a, y_a, gin_a, carried_a, sums_a = forward(0)
+    normed_b, conv_b, z_b, dt_b, pre_b, y_b, gin_b, carried_b, sums_b = forward(1)
+    sums_a = tensor_small(sums_a)
+    sums_b = tensor_small(sums_b)
+    sent, kept, gy_a, gz_a, *gate_sums = gate(0, sums_a, z_a, y_a, gin_a, normed_a, ())
+    mixed_a = chip_sum(sent, kept, n_tensor)
+    mixed_a, sums_b = together(mixed_a, sums_b)
+    far_mixed_a = far_sum(mixed_a, n_tensor)
+    sent, kept, gy_b, gz_b, *gate_sums = gate(
+        1, sums_b, z_b, y_b, gin_b, normed_b, tuple(gate_sums)
+    )
+    part_out, part_z, gate_grad = gate_sums
+    mixed_b = chip_sum(sent, kept, n_tensor)
+    mixed_b, gy_a = together(mixed_b, gy_a)
+    far_mixed_b = far_sum(mixed_b, n_tensor)
+    sent_a, kept_a, *bwd_sums = backward(
+        0, normed_a, conv_a, dt_a, pre_a, y_a, gy_a, gz_a, carried_a, ()
+    )
+    normed_sum_a = chip_sum(sent_a, kept_a, n_tensor)
+    order_y, order_z = dp_order(n_dp, 0), dp_order(n_dp, 1)
+    out_parts = axis_scatter(part_out, "dp", n_dp, order_y[:1])
+    z_parts = axis_scatter(part_z, "dp", n_dp, order_z[:1])
+    normed_sum_a, far_mixed_a, out_parts, z_parts, gy_b = together(
+        normed_sum_a, far_mixed_a, out_parts, z_parts, gy_b
+    )
+    far_normed_a = far_sum(normed_sum_a, n_tensor)
+    out_parts = axis_scatter(out_parts, "dp", n_dp, order_y[1:2])
+    z_parts = axis_scatter(z_parts, "dp", n_dp, order_z[1:2])
+    sent_b, kept_b, wx_part, wbc_part, wdt_part, conv_grad, head_grad = backward(
+        1, normed_b, conv_b, dt_b, pre_b, y_b, gy_b, gz_b, carried_b, tuple(bwd_sums)
+    )
+    sent_b, far_mixed_b, out_parts, z_parts, wx_part, wbc_part = together(
+        sent_b, far_mixed_b, out_parts, z_parts, wx_part, wbc_part
+    )
+    far_normed_b = far_sum(chip_sum(sent_b, kept_b, n_tensor), n_tensor)
+    wide = lambda values: values.astype(f32)
     norm_grad = (
-        jnp.sum(late[:conv_width] * w_wide[:conv_width], 0)
-        + jnp.sum(late[conv_width:] * w_wide[conv_width + inner :], 0)
-        + jnp.sum(early[inner:] * w_wide[conv_width : conv_width + inner], 0)
+        jnp.sum(wx_part * wide(w_x), 1)
+        + jnp.sum(part_z * wide(w_z), 1)
+        + jnp.sum(wbc_part * wide(w_bc), 1)
+        + jnp.sum(wdt_part[:heads].T * wide(w_dt), 1)
     ) / norm_gain
 
-    def widen(values):
+    def widen(values, columns):
         flat = values.reshape(-1)
-        return jnp.pad(flat, (0, -flat.size % width)).reshape(-1, width)
+        return jnp.pad(flat, (0, -flat.size % columns)).reshape(-1, columns)
 
     bc_small = jnp.concatenate([conv_grad[:5, inner:].reshape(-1), norm_grad])
-    bc_parts = pad_rows(
-        jnp.concatenate([late[inner:conv_width], widen(bc_small)], 0), 16 * n_dp
-    )
-    order = steps_of(n_dp)
-    order = order[1:2] + order[:1] + order[2:]
-    bc_parts = axis_scatter(bc_parts, "tensor", n_tensor, [1])
-    bc_parts = axis_scatter(bc_parts, "dp", n_dp, order)
-    for step in steps_of(n_tensor)[1:]:
-        bc_parts = bc_parts + lax.ppermute(bc_parts, "tensor", partners(n_tensor, step))
-    bc_parts = axis_gather(bc_parts, "dp", n_dp, order)
-    bc_parts = axis_gather(bc_parts, "tensor", n_tensor, [1])
+    bc_parts = pad_rows(jnp.concatenate([wbc_part, widen(bc_small, bc_width)], 0), 16 * n_dp)
     x_small = jnp.concatenate(
         [
             conv_grad[:5, :inner].reshape(-1),
@@ -643,52 +713,61 @@
             head_grad[0, :heads],
             head_grad[1, :heads],
             jnp.sum(conv_grad[5, :inner].reshape(heads, size), 1),
+            wdt_part[:heads].reshape(-1),
         ]
     )
-    x_parts = pad_rows(
-        jnp.concatenate(
-            [late[:inner], late[conv_width : conv_width + heads], widen(x_small)], 0
-        ),
-        8 * n_dp,
-    )
-    x_parts = dp_sum(x_parts, n_dp, 0)
-    x_small = x_parts[inner + heads :].reshape(-1)
-    bc_small = bc_parts[bc_width:].reshape(-1)
+    x_parts = pad_rows(jnp.concatenate([wx_part, widen(x_small, inner)], 0), 8 * n_dp)
+    x_parts = axis_scatter(x_parts, "dp", n_dp, order_y)
+    bc_parts = axis_scatter(bc_parts, "tensor", n_tensor, [1])
+    bc_parts = axis_scatter(bc_parts, "dp", n_dp, order_z)
+    out_parts = axis_scatter(out_parts, "dp", n_dp, order_y[2:])
+    z_parts = axis_scatter(z_parts, "dp", n_dp, order_z[2:])
+    for step in steps_of(n_tensor)[1:]:
+        bc_parts = bc_parts + lax.ppermute(bc_parts, "tensor", partners(n_tensor, step))
+    out_grad = axis_gather(out_parts, "dp", n_dp, order_y)
+    z_grad = axis_gather(z_parts, "dp", n_dp, order_z)
+    x_parts = axis_gather(x_parts, "dp", n_dp, order_y)
+    bc_parts = axis_gather(bc_parts, "dp", n_dp, order_z)
+    bc_parts = axis_gather(bc_parts, "tensor", n_tensor, [1])
+    output = placed(
+        output_kernel, 0, far_mixed_a, chip_other(far_mixed_a, n_tensor), (hidden, cols),
+        (width, 16), bf16, (),
+    )
+    output = placed(
+        output_kernel, 1, far_mixed_b, chip_other(far_mixed_b, n_tensor), (hidden, cols),
+        (width, 16), bf16, (output,),
+    )
+    grad_hidden = placed(
+        finish_kernel, 0, far_normed_a, chip_other(far_normed_a, n_tensor),
+        (hidden, cotangent, gain), (width, width, None), f32, (),
+    )
+    grad_hidden = placed(
+        finish_kernel, 1, far_normed_b, chip_other(far_normed_b, n_tensor),
+        (hidden, cotangent, gain), (width, width, None), f32, (grad_hidden,),
+    )
+    x_small = x_parts[width:].reshape(-1)
+    bc_small = bc_parts[width:].reshape(-1)
     at = (taps + 1) * inner
+    heads_at = at + inner
+    dt_at = heads_at + 3 * heads
     bc_at = (taps + 1) * bc_width
-    mixed = join_halves(mixed_own, mixed_other, mine)
-    output = (hidden.astype(f32) + cols[:, 4:5] * mixed).astype(bf16)
-    place = mine.astype(jnp.int32).reshape(1)
-    half_spec = pl.BlockSpec((SPAN, width), lambda i, s: (i % half_spans, 0))
-    row_spec = pl.BlockSpec((SPAN, width), lambda i, s: (i, 0))
-    (grad_hidden,) = call(
-        finish_kernel,
-        (spans,),
-        (place,),
-        (normed_own, normed_other, hidden, cotangent, gain),
-        [half_spec, half_spec, row_spec, row_spec, whole(gain)],
-        (shape(rows, width),),
-        [row_spec],
-        [],
-        rows * width * 10,
-    )
     return (
         output,
         grad_hidden,
         bc_small[bc_at : bc_at + width],
-        x_parts[:inner].T,
-        early_sum[inner:].T,
-        x_parts[inner : inner + heads].T,
-        bc_parts[:bc_width].T,
+        x_parts[:width],
+        z_grad,
+        x_small[dt_at : dt_at + heads * width].reshape(heads, width).T,
+        bc_parts[:width],
         x_small[: taps * inner].reshape(taps, inner),
         x_small[taps * inner : at],
         bc_small[: taps * bc_width].reshape(taps, bc_width),
         bc_small[taps * bc_width : bc_at],
-        x_small[at + inner : at + inner + heads],
-        x_small[at + inner + heads : at + inner + 2 * heads],
-        x_small[at + inner + 2 * heads : at + inner + 3 * heads],
+        x_small[heads_at : heads_at + heads],
+        x_small[heads_at + heads : heads_at + 2 * heads],
+        x_small[heads_at + 2 * heads : dt_at],
         x_small[at : at + inner],
-        early_sum[:inner],
+        out_grad,
     )
 
 

time: 408 us -> 339 us (0.83)
  waiting for transfers between devices: 175 us -> 96.6 us
  Pallas kernels: 97 us -> 117 us
  local copies, waits for them, and re-layouts: 49 us -> 38.4 us
    ppermute x1, waiting for transfers between devices: 92.4 us -> 2.98 us  [per_device(): lax.ppermute(bc_parts, 'tensor', partners(n_tensor, step))]
    pallas_call x4 -> x10, Pallas kernels: 97 us -> 117 us  [call(): pl.pallas_call(kernel, grid_spec=pltpu.PrefetchScalarGridSpec(num_scalar_...]
    ppermute x10 -> x13, waiting for transfers between devices: 28.3 us -> 41.4 us  [axis_scatter(): lax.ppermute(take_half(values, 1 - mine), axis, partners(count, step))]
    convert_element_type x2 -> x0, other arithmetic: 9.98 us -> none  [the longest x1 6.88 us: per_device(): output = (hidden.astype(f32) + cols[:, 4:5] * mixed).astype(bf16)]
    unnamed x50 -> x85, local copies, waits for them, and re-layouts: 8.9 us -> 1.93 us
    pallas_call x2 -> x0, local copies, waits for them, and re-layouts: 6.09 us -> none  [call(): pl.pallas_call(kernel, grid_spec=pltpu.PrefetchScalarGridSpec(num_scalar_...]
    ppermute x10 -> x13, waiting for transfers between devices: 51.3 us -> 45.3 us  [axis_gather(): other = lax.ppermute(values, axis, partners(count, step))]
    dynamic_slice x10 -> x13, local copies, waits for them, and re-layouts: 2.99 us -> 8.42 us  [take_half(): return lax.dynamic_slice_in_dim(values, which * half, half, 0)]
  transfers between devices with their start and end apart: 29 -> 43, of which waited for: 14 -> 23; matrix products, arithmetic and copies ran while one was open for 20% -> 21% of each run, Pallas kernels for 11% -> 23%
where the time goes in v3:
time: 339 us; the launch traced here: 337 us
  Pallas kernels  117 us (35%)
  waiting for transfers between devices  96.6 us (28%)
  other arithmetic  49.1 us (14%)
  local copies, waits for them, and re-layouts  38.4 us (11%)
  starting transfers between devices  33.8 us (10%)
    pallas_call x10, Pallas kernels, call(): pl.pallas_call(kernel, grid_spec=pltpu.PrefetchScalarGridSpec(num_scalar_...  117 us
    ppermute x13, waiting for transfers between devices, axis_gather(): other = lax.ppermute(values, axis, partners(count, step))  45.3 us
    ppermute x13, waiting for transfers between devices, axis_scatter(): lax.ppermute(take_half(values, 1 - mine), axis, partners(count, step))  41.4 us
    ppermute x13, starting transfers between devices, axis_scatter(): lax.ppermute(take_half(values, 1 - mine), axis, partners(count, step))  12.3 us
    select_n x13, other arithmetic, join_halves(): jnp.where(mine == 0, jnp.concatenate([own, other], 0), jnp.concatenate([o...  12.3 us
    add x4, other arithmetic, far_sum(): values = values + lax.ppermute(values, 'tensor', partners(count, step))  9.12 us
    ppermute x13, starting transfers between devices, axis_gather(): other = lax.ppermute(values, axis, partners(count, step))  8.51 us
    add x13, other arithmetic, axis_scatter(): values = take_half(values, mine) + sent  8.49 us
  transfers between devices with their start and end apart: 43, of which 23 were waited for; matrix products, arithmetic and copies ran while one was open for 21% of the time, Pallas kernels for 23%

profile of v3, /device:TPU:0, one launch (start us, length us, event | category | flops | bytes accessed | tf_op | source)
XLA Modules:
  0.0 336.9 jit_solution(14640337881599224899)
XLA Ops:
  12.0 1.4 fusion.1.wcat_ref
  13.3 13.9 %shard_map.298 = (bf16[1024,768]{1,0:T(8,128)(2,1)}, f32[1024,640]{1,0:T(8,128)}, f32[1024,384]{1,0:T(8,128)}, f32[1024,128]{1,0:T(8,128)}, f32[1024,640]{1,0:T(...) custom-call(bf16[2048,768]{1,0:T(8,128)(2,1)} %hid_ref.11, ...), custom_call_target="tpu_custom_call" | custom-call | flops 12000000000 | bytes 21388288 | tf_op jit(solution)/shard_map/pallas_call | solution.py:422
  29.5 2.8 collective-permute-start.1
  32.4 1.6 collective-permute-done.1
  34.6 9.9 %shard_map.299 = (f32[1024,384]{1,0:T(8,128)}, f32[1024,384]{1,0:T(8,128)}, f32[1024,384]{1,0:T(8,128)}, bf16[1024,384]{1,0:T(8,128)(2,1)}, f32[384,768]{1,0:T(8...) custom-call(s32[1]{0:T(128)} %bitcast.place_ref, f32[4,2,256]{2,1,0:T(2,128)} %add.233.sums_ref, ...), custom_call_target="tpu_custom_call" | custom-call | flops 8000000000 | bytes 18055168 | tf_op jit(solution)/shard_map/pallas_call | solution.py:422
  44.6 14.1 %shard_map.297 = (bf16[1024,768]{1,0:T(8,128)(2,1)}, f32[1024,640]{1,0:T(8,128)}, f32[1024,384]{1,0:T(8,128)}, f32[1024,128]{1,0:T(8,128)}, f32[1024,640]{1,0:T(...) custom-call(bf16[2048,768]{1,0:T(8,128)(2,1)} %hid_ref.11, ...), custom_call_target="tpu_custom_call" | custom-call | flops 12000000000 | bytes 21388288 | tf_op jit(solution)/shard_map/pallas_call | solution.py:422
  60.9 2.0 collective-permute-start.4
  62.9 1.6 collective-permute-done.4
  66.3 1.6 add.234
  67.9 9.8 %shard_map.300 = (f32[1024,384]{1,0:T(8,128)}, f32[1024,384]{1,0:T(8,128)}, f32[1024,384]{1,0:T(8,128)}, bf16[1024,384]{1,0:T(8,128)(2,1)}, f32[384,768]{1,0:T(8...) custom-call(s32[1]{0:T(128)} %bitcast.place_ref, f32[4,2,256]{2,1,0:T(2,128)} %add.236.sums_ref, ...), custom_call_target="tpu_custom_call" | custom-call | flops 8000000000 | bytes 20426752 | tf_op jit(solution)/shard_map/pallas_call | solution.py:422
  77.8 2.1 collective-permute-start.7
  80.0 1.5 collective-permute-done.5
  81.5 1.6 add.237
  83.1 24.0 %shard_map.301 = (f32[1024,384]{1,0:T(8,128)}, f32[1024,384]{1,0:T(8,128)}, f32[768,384]{1,0:T(8,128)}, f32[768,256]{1,0:T(8,128)}, f32[128,768]{1,0:T(8,128)}, /*index=5*/f32[8,640]{1,0:T(8,128)}, f32[8,128]{1,0:T(8,128)}) custom-call(s32[1]{0:T(128)} %bitcast.place_ref, f32[2048,16]{1,0:T(8,128)} %pad.36.cols_ref, f32[8,1,256]{2,1,0:T(1,128)} %bitcast.45, ...), custom_call_target="tpu_custom_call" | custom-call | flops 20000000000 | bytes 19238912 | tf_op jit(solution)/shard_map/pallas_call | solution.py:422
  107.4 1.9 constant_dynamic-slice_fusion.11
  109.3 2.1 collective-permute-start.9
  111.4 1.9 constant_dynamic-slice_fusion.12
  113.3 1.5 collective-permute-start.8
  114.8 1.4 slice_reduce_fusion.4
  116.2 1.7 multiply_reduce_fusion
  117.9 7.6 %collective-permute-done.9 = f32[384,384]{1,0:T(8,128)} collective-permute-done((f32[384,384]{1,0:T(8,128)}, f32[384,384]{1,0:T(8,128)}, u32[]{:S(2)}, u32[]{:S(2)}) %collective-permute-start.9) | collective-permute-done | bytes 589856 | tf_op jit(solution)/shard_map/ppermute | solution.py:378
  126.7 2.2 collective-permute-done.8
  130.1 1.6 collective-permute-start.10
  131.7 2.7 add.239.own_ref
  134.4 1.6 add.238
  136.7 1.5 collective-permute-start.12
  139.5 24.7 %shard_map.302 = (f32[1024,384]{1,0:T(8,128)}, f32[1024,384]{1,0:T(8,128)}, f32[768,384]{1,0:T(8,128)}, f32[768,256]{1,0:T(8,128)}, f32[128,768]{1,0:T(8,128)}, /*index=5*/f32[8,640]{1,0:T(8,128)}, f32[8,128]{1,0:T(8,128)}) custom-call(s32[1]{0:T(128)} %bitcast.place_ref, f32[2048,16]{1,0:T(8,128)} %pad.36.cols_ref, f32[8,1,256]{2,1,0:T(1,128)} %bitcast.46, ...), custom_call_target="tpu_custom_call" | custom-call | flops 20000000000 | bytes 21622784 | tf_op jit(solution)/shard_map/pallas_call | solution.py:422
  164.1 1.3 fusion.3
  168.1 1.3 slice.116
  171.4 1.3 reshape.137
  174.2 1.5 concatenate.144
  175.7 1.4 pad.42
  177.1 1.4 reshape.138
  179.8 2.7 add.248.own_ref
  185.4 2.6 collective-permute-start.39
  192.5 5.7 %collective-permute-done.39 = f32[48,768]{1,0:T(8,128)} collective-permute-done((f32[48,768]{1,0:T(8,128)}, f32[48,768]{1,0:T(8,128)}, u32[]{:S(2)}, u32[]{:S(2)}) %collective-permute-start.39) | collective-permute-done | bytes 147488 | tf_op jit(solution)/shard_map/ppermute | solution.py:378
  201.2 3.0 collective-permute-start.36
  204.3 9.9 %collective-permute-done.40 = f32[48,768]{1,0:T(8,128)S(1)} collective-permute-done((f32[48,768]{1,0:T(8,128)S(1)}, f32[48,768]{1,0:T(8,128)S(1)}, u32[]{:S(2)}, u32[]{:S(2)}) %collective-permute-start.40) | collective-permute-done | bytes 147488 | tf_op jit(solution)/shard_map/ppermute | solution.py:386
  214.3 1.7 collective-permute-done.36
  216.4 6.3 %collective-permute-done.21 = f32[224,256]{1,0:T(8,128)S(1)} collective-permute-done((f32[224,256]{1,0:T(8,128)S(1)}, f32[224,256]{1,0:T(8,128)S(1)}, u32[]{:S(2)}, u32[]{:S(2)}) %collective-permute-start.21) | collective-permute-done | bytes 229408 | tf_op jit(solution)/shard_map/ppermute | solution.py:378
  223.3 1.6 collective-permute-start.22
  226.0 4.6 %collective-permute-done.22 = f32[112,256]{1,0:T(8,128)S(1)} collective-permute-done((f32[112,256]{1,0:T(8,128)S(1)}, f32[112,256]{1,0:T(8,128)S(1)}, u32[]{:S(2)}, u32[]{:S(2)}) %collective-permute-start.22) | collective-permute-done | bytes 114720 | tf_op jit(solution)/shard_map/ppermute | solution.py:378
  231.1 4.9 %collective-permute-done.23 = f32[56,256]{1,0:T(8,128)S(1)} collective-permute-done((f32[56,256]{1,0:T(8,128)S(1)}, f32[56,256]{1,0:T(8,128)S(1)}, u32[]{:S(2)}, u32[]{:S(2)}) %collective-permute-start.23) | collective-permute-done | bytes 57376 | tf_op jit(solution)/shard_map/ppermute | solution.py:378
  237.3 3.0 collective-permute-done.24
  240.8 2.8 collective-permute-done.30
  245.7 3.1 collective-permute-done.25
  251.5 3.3 collective-permute-done.26
  257.2 6.0 %collective-permute-done.31 = f32[104,384]{1,0:T(8,128)} collective-permute-done((f32[104,384]{1,0:T(8,128)}, f32[104,384]{1,0:T(8,128)}, u32[]{:S(2)}, u32[]{:S(2)}) %collective-permute-start.31) | collective-permute-done | bytes 159776 | tf_op jit(solution)/shard_map/ppermute | solution.py:378
  264.2 13.7 %collective-permute-done.38 = f32[384,384]{1,0:T(8,128)} collective-permute-done((f32[384,384]{1,0:T(8,128)S(1)}, f32[384,384]{1,0:T(8,128)}, u32[]{:S(2)}, u32[]{:S(2)}) %collective-permute-start.38) | collective-permute-done | bytes 589856 | tf_op jit(solution)/shard_map/ppermute | solution.py:386
  278.9 7.8 %collective-permute-done.32 = f32[104,384]{1,0:T(8,128)S(1)} collective-permute-done((f32[104,384]{1,0:T(8,128)S(1)}, f32[104,384]{1,0:T(8,128)S(1)}, u32[]{:S(2)}, u32[]{:S(2)}) %collective-permute-start.32) | collective-permute-done | bytes 159776 | tf_op jit(solution)/shard_map/ppermute | solution.py:386
  286.7 2.1 collective-permute-start.33
  288.8 2.4 maximum_select_fusion.2
  291.2 1.6 add.255.own_ref
  292.8 2.3 collective-permute-done.27
  295.1 2.4 maximum_select_fusion.1
  298.9 2.0 add.254.own_ref
  302.1 4.5 %shard_map.303.refs_0_ = bf16[2048,768]{1,0:T(8,128)(2,1)} custom-call(s32[1]{0:T(128)} %bitcast.place_ref, f32[1024,384]{1,0:T(8,128)} %add.239.own_ref, f32[1024,384]{1,0:T(8,128)} %collective-permute-done.14.other_ref, bf16[2048,768]{1,0:T(8,128)(2,1)} %hid_ref.11, f32[2048,16]{1,0:T(8,128)} %pad.36.cols_ref), custom_call_target="tpu_custom_call" | custom-call | flops 3000000000 | bytes 9568256 | tf_op jit(solution)/shard_map/pallas_call | solution.py:422
  306.6 4.6 %shard_map.304 = bf16[2048,768]{1,0:T(8,128)(2,1)} custom-call(s32[1]{0:T(128)} %bitcast.place_ref, f32[1024,384]{1,0:T(8,128)} %add.248.own_ref, f32[1024,384]{1,0:T(8,128)} %collective-permute-done.13.other_ref, bf16[2048,768]{1,0:T(8,128)(2,1)} %hid_ref.11, f32[2048,16]{1,0:T(8,128)} %pad.36.cols_ref, ...), custom_call_target="tpu_custom_call", output_to_operand_aliasing={{}: (5, {})} | custom-call | flops 3000000000 | bytes 12713984 | tf_op jit(solution)/shard_map/pallas_call | solution.py:422
  311.2 1.6 maximum_select_fusion.3
  315.4 3.6 %collective-permute-done.34 = f32[416,384]{1,0:T(8,128)} collective-permute-done((f32[416,384]{1,0:T(8,128)}, f32[416,384]{1,0:T(8,128)}, u32[]{:S(2)}, u32[]{:S(2)}) %collective-permute-start.34) | collective-permute-done | bytes 639008 | tf_op jit(solution)/shard_map/ppermute | solution.py:386
  319.0 1.9 maximum_select_fusion
  323.6 1.4 slice_reduce_fusion.1
  325.6 5.7 %shard_map.305.refs_0_ = f32[2048,768]{1,0:T(8,128)} custom-call(s32[1]{0:T(128)} %bitcast.place_ref, f32[1024,384]{1,0:T(8,128)} %copy-done, f32[1024,384]{1,0:T(8,128)} %collective-permute-done.19.other_ref, bf16[2048,768]{1,0:T(8,128)(2,1)} %hid_ref.11, bf16[2048,768]{1,0:T(8,128)(2,1)} %cot_ref.11, f32[1,768]{1,0:T(1,128)} %broadcast_in_dim.12.gain_ref), custom_call_target="tpu_custom_call" | custom-call | flops 3000000000 | bytes 15731712 | tf_op jit(solution)/shard_map/pallas_call | solution.py:422
  331.2 5.6 %shard_map.306 = f32[2048,768]{1,0:T(8,128)} custom-call(s32[1]{0:T(128)} %bitcast.place_ref, f32[1024,384]{1,0:T(8,128)} %copy-done.1, f32[1024,384]{1,0:T(8,128)} %collective-permute-done.17.other_ref, bf16[2048,768]{1,0:T(8,128)(2,1)} %hid_ref.11, bf16[2048,768]{1,0:T(8,128)(2,1)} %cot_ref.11, ...), custom_call_target="tpu_custom_call", output_to_operand_aliasing={{}: (6, {})} | custom-call | flops 3000000000 | bytes 22023168 | tf_op jit(solution)/shard_map/pallas_call | solution.py:422
  (233 shorter events, 61.6 us)
Async XLA Ops:
  6.9 4.4 %copy-start.31 = (f32[4,384]{1,0:T(4,128)S(1)}, f32[4,384]{1,0:T(4,128)}, u32[]{:S(2)}) copy-start(f32[4,384]{1,0:T(4,128)} %param.27) | copy-start | bytes 18436
  6.9 4.4 %copy-start.32 = (f32[4,256]{1,0:T(4,128)S(1)}, f32[4,256]{1,0:T(4,128)}, u32[]{:S(2)}) copy-start(f32[4,256]{1,0:T(4,128)} %param.29) | copy-start | bytes 12292
  6.9 5.0 %copy-start.6 = (bf16[768,384]{1,0:T(8,128)(2,1)S(1)}, bf16[768,384]{1,0:T(8,128)(2,1)}, u32[]{:S(2)}) copy-start(bf16[768,384]{1,0:T(8,128)(2,1)} %param.24) | copy-start | bytes 1769476
  6.9 5.0 %copy-start.7 = (bf16[768,384]{1,0:T(8,128)(2,1)S(1)}, bf16[768,384]{1,0:T(8,128)(2,1)}, u32[]{:S(2)}) copy-start(bf16[768,384]{1,0:T(8,128)(2,1)} %param.23) | copy-start | bytes 1769476
  6.9 5.0 %copy-start.15 = (bf16[768,256]{1,0:T(8,128)(2,1)S(1)}, bf16[768,256]{1,0:T(8,128)(2,1)}, u32[]{:S(2)}) copy-start(bf16[768,256]{1,0:T(8,128)(2,1)} %param.26) | copy-start | bytes 1179652
  27.2 1.6 collective-permute-start
  29.5 4.5 %collective-permute-start.1 = (f32[4,2,256]{2,1,0:T(2,128)S(1)}, f32[4,2,256]{2,1,0:T(2,128)S(1)}, u32[]{:S(2)}, u32[]{:S(2)}) collective-permute-start(f32[4,2,256]{2,1,0:T(2,128)S(1)} %add.232), channel_id=1, source_target_pairs={{0,2},{1,3},{2,0},{3,1},{4,6},{5,7},{6,4},{7,5},{8,10},{9,11},{10,... | collective-permute-start | bytes 24584 | tf_op jit(solution)/shard_map/ppermute | solution.py:577
  44.5 21.9 %copy-start.18 = (f32[1024,384]{1,0:T(8,128)S(1)}, f32[1024,384]{1,0:T(8,128)}, u32[]{:S(2)}) copy-start(f32[1024,384]{1,0:T(8,128)} %get-tuple-element.90) | copy-start | bytes 4718596
  44.5 20.7 %collective-permute-start.2 = (f32[1024,384]{1,0:T(8,128)}, f32[1024,384]{1,0:T(8,128)S(1)}, u32[]{:S(2)}, u32[]{:S(2)}) collective-permute-start(f32[1024,384]{1,0:T(8,128)} %get-tuple-element.91), channel_id=1, source_target_pairs={{0,1},{1,0},{2,3},{3,2},{4,5},{5,4},{6,7},{7,6},{8,9},{9,8},{10,11... | collective-permute-start | bytes 4718600 | tf_op jit(solution)/shard_map/ppermute | solution.py:401
  58.7 1.5 collective-permute-start.3
  60.9 3.7 %collective-permute-start.4 = (f32[4,2,256]{2,1,0:T(2,128)S(1)}, f32[4,2,256]{2,1,0:T(2,128)S(1)}, u32[]{:S(2)}, u32[]{:S(2)}) collective-permute-start(f32[4,2,256]{2,1,0:T(2,128)S(1)} %add.235), channel_id=1, source_target_pairs={{0,2},{1,3},{2,0},{3,1},{4,6},{5,7},{6,4},{7,5},{8,10},{9,11},{10,... | collective-permute-start | bytes 24584 | tf_op jit(solution)/shard_map/ppermute | solution.py:577
  77.8 3.7 %collective-permute-start.5 = (f32[1024,384]{1,0:T(8,128)}, f32[1024,384]{1,0:T(8,128)S(1)}, u32[]{:S(2)}, u32[]{:S(2)}) collective-permute-start(f32[1024,384]{1,0:T(8,128)} %get-tuple-element.100), channel_id=1, source_target_pairs={{0,1},{1,0},{2,3},{3,2},{4,5},{5,4},{6,7},{7,6},{8,9},{9,8},{10,11... | collective-permute-start | bytes 4718600 | tf_op jit(solution)/shard_map/ppermute | solution.py:401
  77.8 53.8 %collective-permute-start.7 = (f32[1024,384]{1,0:T(8,128)S(1)}, f32[1024,384]{1,0:T(8,128)}, u32[]{:S(2)}, u32[]{:S(2)}) collective-permute-start(f32[1024,384]{1,0:T(8,128)S(1)} %add.234), channel_id=1, source_target_pairs={{0,2},{1,3},{2,0},{3,1},{4,6},{5,7},{6,4},{7,5},{8,10},{9,11},{10,... | collective-permute-start | bytes 4718600 | tf_op jit(solution)/shard_map/ppermute | solution.py:406
  107.1 27.3 %collective-permute-start.6 = (f32[1024,384]{1,0:T(8,128)}, f32[1024,384]{1,0:T(8,128)}, u32[]{:S(2)}, u32[]{:S(2)}) collective-permute-start(f32[1024,384]{1,0:T(8,128)} %get-tuple-element.106), channel_id=1, source_target_pairs={{0,1},{1,0},{2,3},{3,2},{4,5},{5,4},{6,7},{7,6},{8,9},{9,8},{10,11... | collective-permute-start | bytes 4718600 | tf_op jit(solution)/shard_map/ppermute | solution.py:401
  109.3 16.3 %collective-permute-start.9 = (f32[384,384]{1,0:T(8,128)}, f32[384,384]{1,0:T(8,128)}, u32[]{:S(2)}, u32[]{:S(2)}) collective-permute-start(f32[384,384]{1,0:T(8,128)} %constant_dynamic-slice_fusion.11), channel_id=1, source_target_pairs={{0,8},{4,12},{8,0},{12,4},{16,24},{20,28},{24,16},{28,20},{1,9},{5... | collective-permute-start | bytes 1769480 | tf_op jit(solution)/shard_map/ppermute | solution.py:378
  113.3 15.6 %collective-permute-start.8 = (f32[192,768]{1,0:T(8,128)}, f32[192,768]{1,0:T(8,128)}, u32[]{:S(2)}, u32[]{:S(2)}) collective-permute-start(f32[192,768]{1,0:T(8,128)} %constant_dynamic-slice_fusion.12), channel_id=1, source_target_pairs={{0,4},{4,0},{8,12},{12,8},{16,20},{20,16},{24,28},{28,24},{1,5},{5... | collective-permute-start | bytes 1769480 | tf_op jit(solution)/shard_map/ppermute | solution.py:378
  114.8 10.7 %copy-start.4 = (f32[768,384]{1,0:T(8,128)S(1)}, f32[768,384]{1,0:T(8,128)}, u32[]{:S(2)}) copy-start(f32[768,384]{1,0:T(8,128)} %get-tuple-element.109) | copy-start | bytes 3538948
  116.2 12.7 %copy-start.22 = (f32[384,768]{1,0:T(8,128)S(1)}, f32[384,768]{1,0:T(8,128)}, u32[]{:S(2)}) copy-start(f32[384,768]{1,0:T(8,128)} %get-tuple-element.108) | copy-start | bytes 3538948
  126.7 9.3 %copy-start.11 = (f32[384,384]{1,0:T(8,128)}, f32[384,384]{1,0:T(8,128)S(1)}, u32[]{:S(2)}) copy-start(f32[384,384]{1,0:T(8,128)S(1)} %dynamic-slice_add_fusion.1) | copy-start | bytes 1769476
  130.1 8.2 %copy-start.13 = (f32[192,768]{1,0:T(8,128)}, f32[192,768]{1,0:T(8,128)S(1)}, u32[]{:S(2)}) copy-start(f32[192,768]{1,0:T(8,128)S(1)} %dynamic-slice_add_fusion.2) | copy-start | bytes 1769476
  130.1 49.7 %collective-permute-start.10 = (f32[1024,384]{1,0:T(8,128)S(1)}, f32[1024,384]{1,0:T(8,128)}, u32[]{:S(2)}, u32[]{:S(2)}) collective-permute-start(f32[1024,384]{1,0:T(8,128)S(1)} %add.237), channel_id=1, source_target_pairs={{0,2},{1,3},{2,0},{3,1},{4,6},{5,7},{6,4},{7,5},{8,10},{9,11},{10,... | collective-permute-start | bytes 4718600 | tf_op jit(solution)/shard_map/ppermute | solution.py:406
  136.7 45.8 %collective-permute-start.12 = (f32[192,384]{1,0:T(8,128)}, f32[192,384]{1,0:T(8,128)}, u32[]{:S(2)}, u32[]{:S(2)}) collective-permute-start(f32[192,384]{1,0:T(8,128)} %constant_dynamic-slice_fusion.9), channel_id=1, source_target_pairs={{0,4},{4,0},{8,12},{12,8},{16,20},{20,16},{24,28},{28,24},{1,5},{5... | collective-permute-start | bytes 884744 | tf_op jit(solution)/shard_map/ppermute | solution.py:378
  139.0 44.6 %collective-permute-start.11 = (f32[96,768]{1,0:T(8,128)}, f32[96,768]{1,0:T(8,128)}, u32[]{:S(2)}, u32[]{:S(2)}) collective-permute-start(f32[96,768]{1,0:T(8,128)} %constant_dynamic-slice_fusion.10), channel_id=1, source_target_pairs={{0,8},{4,12},{8,0},{12,4},{16,24},{20,28},{24,16},{28,20},{1,9},{5... | collective-permute-start | bytes 884744 | tf_op jit(solution)/shard_map/ppermute | solution.py:378
  179.2 4.5 %copy-start.14 = (f32[192,768]{1,0:T(8,128)S(1)}, f32[192,768]{1,0:T(8,128)}, u32[]{:S(2)}) copy-start(f32[192,768]{1,0:T(8,128)} %copy-done.13) | copy-start | bytes 1769476
  179.2 107.5 %collective-permute-start.18 = (f32[1024,384]{1,0:T(8,128)S(1)}, f32[1024,384]{1,0:T(8,128)}, u32[]{:S(2)}, u32[]{:S(2)}) collective-permute-start(f32[1024,384]{1,0:T(8,128)S(1)} %add.238), channel_id=1, source_target_pairs={{0,2},{1,3},{2,0},{3,1},{4,6},{5,7},{6,4},{7,5},{8,10},{9,11},{10,... | collective-permute-start | bytes 4718600 | tf_op jit(solution)/shard_map/ppermute | solution.py:406
  182.5 6.6 %copy-start.3 = (f32[768,384]{1,0:T(8,128)S(1)}, f32[768,384]{1,0:T(8,128)}, u32[]{:S(2)}) copy-start(f32[768,384]{1,0:T(8,128)} %get-tuple-element.132) | copy-start | bytes 3538948
  182.5 6.6 %copy-start.8 = (bf16[768,384]{1,0:T(8,128)(2,1)S(1)}, bf16[768,384]{1,0:T(8,128)(2,1)}, u32[]{:S(2)}) copy-start(bf16[768,384]{1,0:T(8,128)(2,1)} %param.23) | copy-start | bytes 1769476
  183.6 5.6 %copy-start.24 = (f32[19,384]{1,0:T(8,128)S(1)}, f32[19,384]{1,0:T(8,128)}, u32[]{:S(2)}) copy-start(f32[19,384]{1,0:T(8,128)} %reshape.138) | copy-start | bytes 87556
  185.4 12.8 %collective-permute-start.39 = (f32[48,768]{1,0:T(8,128)}, f32[48,768]{1,0:T(8,128)}, u32[]{:S(2)}, u32[]{:S(2)}) collective-permute-start(f32[48,768]{1,0:T(8,128)} %constant_dynamic-slice_fusion), channel_id=1, source_target_pairs={{0,16},{4,20},{8,24},{12,28},{16,0},{20,4},{24,8},{28,12},{1,17},{... | collective-permute-start | bytes 442376 | tf_op jit(solution)/shard_map/ppermute | solution.py:378
  188.7 11.6 %collective-permute-start.35 = (f32[96,384]{1,0:T(8,128)}, f32[96,384]{1,0:T(8,128)}, u32[]{:S(2)}, u32[]{:S(2)}) collective-permute-start(f32[96,384]{1,0:T(8,128)} %constant_dynamic-slice_fusion.1), channel_id=1, source_target_pairs={{0,16},{4,20},{8,24},{12,28},{16,0},{20,4},{24,8},{28,12},{1,17},{... | collective-permute-start | bytes 442376 | tf_op jit(solution)/shard_map/ppermute | solution.py:378
  190.3 33.0 %collective-permute-start.29 = (f32[416,384]{1,0:T(8,128)}, f32[416,384]{1,0:T(8,128)}, u32[]{:S(2)}, u32[]{:S(2)}) collective-permute-start(f32[416,384]{1,0:T(8,128)} %constant_dynamic-slice_fusion.4), channel_id=1, source_target_pairs={{0,4},{4,0},{8,12},{12,8},{16,20},{20,16},{24,28},{28,24},{1,5},{5... | collective-permute-start | bytes 1916936 | tf_op jit(solution)/shard_map/ppermute | solution.py:378
  191.0 7.2 %copy-start.21 = (f32[96,768]{1,0:T(8,128)S(1)}, f32[96,768]{1,0:T(8,128)}, u32[]{:S(2)}) copy-start(f32[96,768]{1,0:T(8,128)} %copy-done.20) | copy-start | bytes 884740
  191.1 7.2 %copy-start.38 = (f32[1024,384]{1,0:T(8,128)S(1)}, f32[1024,384]{1,0:T(8,128)}, u32[]{:S(2)}) copy-start(f32[1024,384]{1,0:T(8,128)} %get-tuple-element.128) | copy-start | bytes 4718596
  192.4 8.8 %collective-permute-start.20 = (f32[448,256]{1,0:T(8,128)S(1)}, f32[448,256]{1,0:T(8,128)S(1)}, u32[]{:S(2)}, u32[]{:S(2)}) collective-permute-start(f32[448,256]{1,0:T(8,128)S(1)} %constant_dynamic-slice_fusion.8), channel_id=1, source_target_pairs={{0,1},{1,0},{2,3},{3,2},{4,5},{5,4},{6,7},{7,6},{8,9},{9,8},{10,11... | collective-permute-start | bytes 1376264 | tf_op jit(solution)/shard_map/ppermute | solution.py:378
  198.2 46.1 %collective-permute-start.15 = (f32[1024,384]{1,0:T(8,128)S(1)}, f32[1024,384]{1,0:T(8,128)S(1)}, u32[]{:S(2)}, u32[]{:S(2)}) collective-permute-start(f32[1024,384]{1,0:T(8,128)S(1)} %copy-done.38), channel_id=1, source_target_pairs={{0,1},{1,0},{2,3},{3,2},{4,5},{5,4},{6,7},{7,6},{8,9},{9,8},{10,11... | collective-permute-start | bytes 4718600 | tf_op jit(solution)/shard_map/ppermute | solution.py:401
  200.3 14.0 %collective-permute-start.40 = (f32[48,768]{1,0:T(8,128)S(1)}, f32[48,768]{1,0:T(8,128)S(1)}, u32[]{:S(2)}, u32[]{:S(2)}) collective-permute-start(f32[48,768]{1,0:T(8,128)S(1)} %dynamic-slice_add_fusion.9), channel_id=1, source_target_pairs={{0,16},{4,20},{8,24},{12,28},{16,0},{20,4},{24,8},{28,12},{1,17},{... | collective-permute-start | bytes 442376 | tf_op jit(solution)/shard_map/ppermute | solution.py:386
  201.2 14.8 %collective-permute-start.36 = (f32[96,384]{1,0:T(8,128)S(1)}, f32[96,384]{1,0:T(8,128)S(1)}, u32[]{:S(2)}, u32[]{:S(2)}) collective-permute-start(f32[96,384]{1,0:T(8,128)S(1)} %dynamic-slice_add_fusion.10), channel_id=1, source_target_pairs={{0,16},{4,20},{8,24},{12,28},{16,0},{20,4},{24,8},{28,12},{1,17},{... | collective-permute-start | bytes 442376 | tf_op jit(solution)/shard_map/ppermute | solution.py:386
  214.2 8.5 %collective-permute-start.21 = (f32[224,256]{1,0:T(8,128)S(1)}, f32[224,256]{1,0:T(8,128)S(1)}, u32[]{:S(2)}, u32[]{:S(2)}) collective-permute-start(f32[224,256]{1,0:T(8,128)S(1)} %constant_dynamic-slice_fusion.7), channel_id=1, source_target_pairs={{0,8},{4,12},{8,0},{12,4},{16,24},{20,28},{24,16},{28,20},{1,9},{5... | collective-permute-start | bytes 688136 | tf_op jit(solution)/shard_map/ppermute | solution.py:378
  216.0 20.1 %collective-permute-start.41 = (f32[96,768]{1,0:T(8,128)S(1)}, f32[96,768]{1,0:T(8,128)S(1)}, u32[]{:S(2)}, u32[]{:S(2)}) collective-permute-start(f32[96,768]{1,0:T(8,128)S(1)} %maximum_select_fusion.10), channel_id=1, source_target_pairs={{0,8},{4,12},{8,0},{12,4},{16,24},{20,28},{24,16},{28,20},{1,9},{5... | collective-permute-start | bytes 884744 | tf_op jit(solution)/shard_map/ppermute | solution.py:386
  222.7 27.2 %collective-permute-start.37 = (f32[192,384]{1,0:T(8,128)S(1)}, f32[192,384]{1,0:T(8,128)S(1)}, u32[]{:S(2)}, u32[]{:S(2)}) collective-permute-start(f32[192,384]{1,0:T(8,128)S(1)} %maximum_select_fusion.9), channel_id=1, source_target_pairs={{0,4},{4,0},{8,12},{12,8},{16,20},{20,16},{24,28},{28,24},{1,5},{5... | collective-permute-start | bytes 884744 | tf_op jit(solution)/shard_map/ppermute | solution.py:386
  223.3 7.4 %collective-permute-start.22 = (f32[112,256]{1,0:T(8,128)S(1)}, f32[112,256]{1,0:T(8,128)S(1)}, u32[]{:S(2)}, u32[]{:S(2)}) collective-permute-start(f32[112,256]{1,0:T(8,128)S(1)} %constant_dynamic-slice_fusion.6), channel_id=1, source_target_pairs={{0,4},{4,0},{8,12},{12,8},{16,20},{20,16},{24,28},{28,24},{1,5},{5... | collective-permute-start | bytes 344072 | tf_op jit(solution)/shard_map/ppermute | solution.py:378
  230.7 13.7 %copy-start.17 = (f32[1024,384]{1,0:T(8,128)S(1)}, f32[1024,384]{1,0:T(8,128)}, u32[]{:S(2)}) copy-start(f32[1024,384]{1,0:T(8,128)} %get-tuple-element.127) | copy-start | bytes 4718596
  230.7 5.3 %collective-permute-start.23 = (f32[56,256]{1,0:T(8,128)S(1)}, f32[56,256]{1,0:T(8,128)S(1)}, u32[]{:S(2)}, u32[]{:S(2)}) collective-permute-start(f32[56,256]{1,0:T(8,128)S(1)} %constant_dynamic-slice_fusion.5), channel_id=1, source_target_pairs={{0,16},{4,20},{8,24},{12,28},{16,0},{20,4},{24,8},{28,12},{1,17},{... | collective-permute-start | bytes 172040 | tf_op jit(solution)/shard_map/ppermute | solution.py:378
  236.0 7.6 %collective-permute-start.30 = (f32[208,384]{1,0:T(8,128)S(1)}, f32[208,384]{1,0:T(8,128)S(1)}, u32[]{:S(2)}, u32[]{:S(2)}) collective-permute-start(f32[208,384]{1,0:T(8,128)S(1)} %constant_dynamic-slice_fusion.3), channel_id=1, source_target_pairs={{0,8},{4,12},{8,0},{12,4},{16,24},{20,28},{24,16},{28,20},{1,9},{5... | collective-permute-start | bytes 958472 | tf_op jit(solution)/shard_map/ppermute | solution.py:378
  236.0 4.2 %collective-permute-start.24 = (f32[56,256]{1,0:T(8,128)S(1)}, f32[56,256]{1,0:T(8,128)S(1)}, u32[]{:S(2)}, u32[]{:S(2)}) collective-permute-start(f32[56,256]{1,0:T(8,128)S(1)} %dynamic-slice_add_fusion.12), channel_id=1, source_target_pairs={{0,2},{1,3},{2,0},{3,1},{4,6},{5,7},{6,4},{7,5},{8,10},{9,11},{10,... | collective-permute-start | bytes 172040 | tf_op jit(solution)/shard_map/ppermute | solution.py:726
  240.3 23.0 %collective-permute-start.42 = (f32[192,768]{1,0:T(8,128)S(1)}, f32[192,768]{1,0:T(8,128)}, u32[]{:S(2)}, u32[]{:S(2)}) collective-permute-start(f32[192,768]{1,0:T(8,128)S(1)} %maximum_select_fusion.6), channel_id=1, source_target_pairs={{0,4},{4,0},{8,12},{12,8},{16,20},{20,16},{24,28},{28,24},{1,5},{5... | collective-permute-start | bytes 1769480 | tf_op jit(solution)/shard_map/ppermute | solution.py:386
  243.6 5.1 %collective-permute-start.25 = (f32[56,256]{1,0:T(8,128)S(1)}, f32[56,256]{1,0:T(8,128)S(1)}, u32[]{:S(2)}, u32[]{:S(2)}) collective-permute-start(f32[56,256]{1,0:T(8,128)S(1)} %add.272), channel_id=1, source_target_pairs={{0,16},{4,20},{8,24},{12,28},{16,0},{20,4},{24,8},{28,12},{1,17},{... | collective-permute-start | bytes 172040 | tf_op jit(solution)/shard_map/ppermute | solution.py:386
  244.3 57.8 %collective-permute-start.14 = (f32[1024,384]{1,0:T(8,128)}, f32[1024,384]{1,0:T(8,128)}, u32[]{:S(2)}, u32[]{:S(2)}) collective-permute-start(f32[1024,384]{1,0:T(8,128)} %add.239.own_ref), channel_id=1, source_target_pairs={{0,1},{1,0},{2,3},{3,2},{4,5},{5,4},{6,7},{7,6},{8,9},{9,8},{10,11... | collective-permute-start | bytes 4718600 | tf_op jit(solution)/shard_map/ppermute | solution.py:411
  248.7 49.6 %collective-permute-start.16 = (f32[1024,384]{1,0:T(8,128)}, f32[1024,384]{1,0:T(8,128)}, u32[]{:S(2)}, u32[]{:S(2)}) collective-permute-start(f32[1024,384]{1,0:T(8,128)} %add.253), channel_id=1, source_target_pairs={{0,2},{1,3},{2,0},{3,1},{4,6},{5,7},{6,4},{7,5},{8,10},{9,11},{10,... | collective-permute-start | bytes 4718600 | tf_op jit(solution)/shard_map/ppermute | solution.py:406
  249.9 4.9 %copy-start.23 = (f32[192,384]{1,0:T(8,128)}, f32[192,384]{1,0:T(8,128)S(1)}, u32[]{:S(2)}) copy-start(f32[192,384]{1,0:T(8,128)S(1)} %collective-permute-done.37) | copy-start | bytes 884740
  249.9 4.9 %collective-permute-start.26 = (f32[112,256]{1,0:T(8,128)S(1)}, f32[112,256]{1,0:T(8,128)S(1)}, u32[]{:S(2)}, u32[]{:S(2)}) collective-permute-start(f32[112,256]{1,0:T(8,128)S(1)} %maximum_select_fusion.12), channel_id=1, source_target_pairs={{0,4},{4,0},{8,12},{12,8},{16,20},{20,16},{24,28},{28,24},{1,5},{5... | collective-permute-start | bytes 344072 | tf_op jit(solution)/shard_map/ppermute | solution.py:386
  254.8 8.5 %collective-permute-start.31 = (f32[104,384]{1,0:T(8,128)}, f32[104,384]{1,0:T(8,128)}, u32[]{:S(2)}, u32[]{:S(2)}) collective-permute-start(f32[104,384]{1,0:T(8,128)} %constant_dynamic-slice_fusion.2), channel_id=1, source_target_pairs={{0,16},{4,20},{8,24},{12,28},{16,0},{20,4},{24,8},{28,12},{1,17},{... | collective-permute-start | bytes 479240 | tf_op jit(solution)/shard_map/ppermute | solution.py:378
  257.2 31.6 %copy-start.9 = (f32[384,384]{1,0:T(8,128)}, f32[384,384]{1,0:T(8,128)S(1)}, u32[]{:S(2)}) copy-start(f32[384,384]{1,0:T(8,128)S(1)} %maximum_select_fusion.5) | copy-start | bytes 1769476
  263.2 14.6 %collective-permute-start.38 = (f32[384,384]{1,0:T(8,128)S(1)}, f32[384,384]{1,0:T(8,128)}, u32[]{:S(2)}, u32[]{:S(2)}) collective-permute-start(f32[384,384]{1,0:T(8,128)S(1)} %maximum_select_fusion.5), channel_id=1, source_target_pairs={{0,8},{4,12},{8,0},{12,4},{16,24},{20,28},{24,16},{28,20},{1,9},{5... | collective-permute-start | bytes 1769480 | tf_op jit(solution)/shard_map/ppermute | solution.py:386
  263.3 43.4 %collective-permute-start.13 = (f32[1024,384]{1,0:T(8,128)}, f32[1024,384]{1,0:T(8,128)}, u32[]{:S(2)}, u32[]{:S(2)}) collective-permute-start(f32[1024,384]{1,0:T(8,128)} %add.248.own_ref), channel_id=1, source_target_pairs={{0,1},{1,0},{2,3},{3,2},{4,5},{5,4},{6,7},{7,6},{8,9},{9,8},{10,11... | collective-permute-start | bytes 4718600 | tf_op jit(solution)/shard_map/ppermute | solution.py:411
  277.9 8.8 %collective-permute-start.32 = (f32[104,384]{1,0:T(8,128)S(1)}, f32[104,384]{1,0:T(8,128)S(1)}, u32[]{:S(2)}, u32[]{:S(2)}) collective-permute-start(f32[104,384]{1,0:T(8,128)S(1)} %dynamic-slice_add_fusion.8), channel_id=1, source_target_pairs={{0,16},{4,20},{8,24},{12,28},{16,0},{20,4},{24,8},{28,12},{1,17},{... | collective-permute-start | bytes 479240 | tf_op jit(solution)/shard_map/ppermute | solution.py:386
  286.7 8.5 %collective-permute-start.27 = (f32[224,256]{1,0:T(8,128)S(1)}, f32[224,256]{1,0:T(8,128)S(1)}, u32[]{:S(2)}, u32[]{:S(2)}) collective-permute-start(f32[224,256]{1,0:T(8,128)S(1)} %maximum_select_fusion.11), channel_id=1, source_target_pairs={{0,8},{4,12},{8,0},{12,4},{16,24},{20,28},{24,16},{28,20},{1,9},{5... | collective-permute-start | bytes 688136 | tf_op jit(solution)/shard_map/ppermute | solution.py:386
  286.7 14.2 %collective-permute-start.33 = (f32[208,384]{1,0:T(8,128)S(1)}, f32[208,384]{1,0:T(8,128)S(1)}, u32[]{:S(2)}, u32[]{:S(2)}) collective-permute-start(f32[208,384]{1,0:T(8,128)S(1)} %maximum_select_fusion.8), channel_id=1, source_target_pairs={{0,8},{4,12},{8,0},{12,4},{16,24},{20,28},{24,16},{28,20},{1,9},{5... | collective-permute-start | bytes 958472 | tf_op jit(solution)/shard_map/ppermute | solution.py:386
  292.8 5.6 %copy-start = (f32[1024,384]{1,0:T(8,128)}, f32[1024,384]{1,0:T(8,128)S(1)}, u32[]{:S(2)}) copy-start(f32[1024,384]{1,0:T(8,128)S(1)} %add.255.own_ref) | copy-start | bytes 4718596
  295.1 30.4 %collective-permute-start.19 = (f32[1024,384]{1,0:T(8,128)S(1)}, f32[1024,384]{1,0:T(8,128)}, u32[]{:S(2)}, u32[]{:S(2)}) collective-permute-start(f32[1024,384]{1,0:T(8,128)S(1)} %add.255.own_ref), channel_id=1, source_target_pairs={{0,1},{1,0},{2,3},{3,2},{4,5},{5,4},{6,7},{7,6},{8,9},{9,8},{10,11... | collective-permute-start | bytes 4718600 | tf_op jit(solution)/shard_map/ppermute | solution.py:411
  298.4 12.8 %collective-permute-start.28 = (f32[448,256]{1,0:T(8,128)}, f32[448,256]{1,0:T(8,128)}, u32[]{:S(2)}, u32[]{:S(2)}) collective-permute-start(f32[448,256]{1,0:T(8,128)} %maximum_select_fusion.7), channel_id=1, source_target_pairs={{0,1},{1,0},{2,3},{3,2},{4,5},{5,4},{6,7},{7,6},{8,9},{9,8},{10,11... | collective-permute-start | bytes 1376264 | tf_op jit(solution)/shard_map/ppermute | solution.py:386
  300.9 5.7 %copy-start.1 = (f32[1024,384]{1,0:T(8,128)}, f32[1024,384]{1,0:T(8,128)S(1)}, u32[]{:S(2)}) copy-start(f32[1024,384]{1,0:T(8,128)S(1)} %add.254.own_ref) | copy-start | bytes 4718596
  300.9 30.3 %collective-permute-start.17 = (f32[1024,384]{1,0:T(8,128)S(1)}, f32[1024,384]{1,0:T(8,128)}, u32[]{:S(2)}, u32[]{:S(2)}) collective-permute-start(f32[1024,384]{1,0:T(8,128)S(1)} %add.254.own_ref), channel_id=1, source_target_pairs={{0,1},{1,0},{2,3},{3,2},{4,5},{5,4},{6,7},{7,6},{8,9},{9,8},{10,11... | collective-permute-start | bytes 4718600 | tf_op jit(solution)/shard_map/ppermute | solution.py:411
  302.1 16.9 %collective-permute-start.34 = (f32[416,384]{1,0:T(8,128)}, f32[416,384]{1,0:T(8,128)}, u32[]{:S(2)}, u32[]{:S(2)}) collective-permute-start(f32[416,384]{1,0:T(8,128)} %maximum_select_fusion.4), channel_id=1, source_target_pairs={{0,4},{4,0},{8,12},{12,8},{16,20},{20,16},{24,28},{28,24},{1,5},{5... | collective-permute-start | bytes 1916936 | tf_op jit(solution)/shard_map/ppermute | solution.py:386
  (19 other events, 47.9 us)

commit v4 on v3

--- a/solution.py
+++ b/solution.py
@@ -56,6 +56,11 @@
     down = lax.broadcasted_iota(jnp.int32, (SPAN, SPAN), 0)
     across = lax.broadcasted_iota(jnp.int32, (SPAN, SPAN), 1)
     return down >= across
+
+
+def flag_columns(rows):
+    blank = jnp.zeros((LANES - rows.shape[0], rows.shape[1]), jnp.float32)
+    return jnp.concatenate([rows, blank], 0).T
 
 
 def as_low(flags):
@@ -75,7 +80,7 @@
 
 
 def fwd_kernel(
-    hid_ref, cot_ref, cols_ref, seg_ref, gain_ref, wcat_ref, wout_ref, conv_ref, head_ref,
+    hid_ref, cot_ref, flags_ref, gain_ref, wcat_ref, wout_ref, conv_ref, head_ref,
     spread_ref, chan_ref, normed_ref, conv_in_ref, z_ref, dt_ref, pre_ref, y_ref, gin_ref,
     carried_ref, sums_ref, ext_ref, state_ref, *, heads, inner, conv_width,
 ):
@@ -84,7 +89,7 @@
         ext_ref[0:8, :] = jnp.zeros((8, conv_width), jnp.float32)
         state_ref[...] = jnp.zeros_like(state_ref)
 
-    cols = cols_ref[...]
+    cols = flag_columns(flags_ref[...])
     hid = hid_ref[...].astype(jnp.float32)
     inv_rms = lax.rsqrt(jnp.mean(hid * hid, -1, keepdims=True) + EPS)
     normed = (hid * inv_rms * gain_ref[...]).astype(jnp.bfloat16)
@@ -109,7 +114,7 @@
     c_low = active[:, inner + states :].astype(jnp.bfloat16)
     lower = lower_ones()
     _, _, falls, falls_t, step_x, in_x, out_x, linked = span_decays(
-        dt_part, cols, seg_ref[0], head_ref[...], spread_ref[...], lower
+        dt_part, cols, flags_ref[0:1], head_ref[...], spread_ref[...], lower
     )
     kernel = dot(c_low, b_low, LAST)
     inputs = (step_x * x_conv).astype(jnp.bfloat16)
@@ -146,8 +151,8 @@
     sums_ref[0] = jnp.where(lane == 0, squares, cross).T[0:2]
 
 
-def split_refs(refs, count):
-    return (refs[:count], refs[count:]) if len(refs) > 7 else ((), refs)
+def split_refs(refs, count, outs):
+    return (refs[:count], refs[count:]) if len(refs) > outs else ((), refs)
 
 
 def begin_sums(targets, sources):
@@ -184,12 +189,13 @@
 
 
 def gate_kernel(
-    place_ref, sums_ref, z_ref, y_ref, gin_ref, cot_ref, cols_ref, normed_ref, wout_ref, chan_ref,
+    place_ref, sums_ref, z_ref, y_ref, gin_ref, cot_ref, flags_ref, normed_ref, wout_ref, chan_ref,
     *refs, inner, inner_all,
 ):
-    sums_of, outs = split_refs(refs, 3)
-    sent_ref, kept_ref, gy_ref, gz_ref, wout_grad_ref, wz_grad_ref, gain_ref = outs
-    begin_sums((wout_grad_ref, wz_grad_ref, gain_ref), sums_of)
+    sums_of, outs = split_refs(refs, 2, 6)
+    sent_ref, kept_ref, gy_ref, gz_ref, early_ref, gain_ref = outs
+    begin_sums((early_ref, gain_ref), sums_of)
+    live = flag_columns(flags_ref[...])[:, 4:5]
 
     sums = sums_ref[0]
     copies = inner // LANES
@@ -204,8 +210,8 @@
     scaled = gated * inv_gate
     out_in = (scaled * chan_ref[1:2]).astype(jnp.bfloat16)
     store_halves(place_ref, dot(out_in, wout_ref[...]), sent_ref, kept_ref)
-    grad_mix = (cols_ref[:, 4:5] * cot_ref[...].astype(jnp.float32)).astype(jnp.bfloat16)
-    wout_grad_ref[...] += dot(out_in, grad_mix, FIRST)
+    grad_mix = (live * cot_ref[...].astype(jnp.float32)).astype(jnp.bfloat16)
+    early_ref[0:inner, :] += dot(out_in, grad_mix, FIRST)
     grad_in = gin_ref[...]
     gain_ref[0:1, :] += jnp.sum(grad_in * scaled, 0, keepdims=True)
     grad_gated = inv_gate * (
@@ -214,25 +220,28 @@
     gy_ref[...] = grad_gated * active
     grad_z = (grad_gated * y_flat * (sig * (1.0 + gate_in * (1.0 - sig)))).astype(jnp.bfloat16)
     gz_ref[...] = grad_z
-    wz_grad_ref[...] += dot(normed_ref[...], grad_z, FIRST)
+    early_ref[inner : 2 * inner, :] += dot(grad_z, normed_ref[...], FIRST)
 
 
 def bwd_kernel(
-    place_ref, cols_ref, seg_ref, normed_ref, conv_in_ref, dt_ref, pre_ref, y_ref, gy_ref, gz_ref,
+    place_ref, flags_ref, normed_ref, conv_in_ref, dt_ref, pre_ref, y_ref, gy_ref, gz_ref,
     carried_ref, wcat_ref, conv_ref, head_ref, spread_ref, chan_ref, *refs,
     heads, inner, conv_width,
 ):
     (ext_ref, flow_ref), refs = refs[-2:], refs[:-2]
-    sums_of, outs = split_refs(refs, 5)
-    sent_ref, kept_ref, wx_grad_ref, wbc_grad_ref, wdt_grad_ref, conv_grad_ref, head_grad_ref = outs
-    begin_sums((wx_grad_ref, wbc_grad_ref, wdt_grad_ref, conv_grad_ref, head_grad_ref), sums_of)
+    befores, outs = split_refs(refs, 5, 4)
+    sent_ref, kept_ref, upper_ref, below_ref = outs
+    begin_sums((upper_ref, below_ref), befores[:2])
+    width = normed_ref.shape[1]
+    top = width // 2
+    small = below_ref.at[top:, :]
 
     @pl.when(pl.program_id(0) == 0)
     def _():
         ext_ref[SPAN : SPAN + 8, :] = jnp.zeros((8, conv_width), jnp.float32)
         flow_ref[...] = jnp.zeros_like(flow_ref)
 
-    cols = cols_ref[...]
+    cols = flag_columns(flags_ref[...])
     pre = pre_ref[...]
     sig = sigmoid(pre)
     active = pre * sig
@@ -245,7 +254,7 @@
     spread = spread_ref[...]
     head_rows = head_ref[...]
     dt_in, step, falls, falls_t, step_x, in_x, out_x, linked = span_decays(
-        dt_ref[...], cols, seg_ref[0], head_rows, spread, lower
+        dt_ref[...], cols, flags_ref[0:1], head_rows, spread, lower
     )
     kernel = dot(c_low, b_low, LAST)
     inputs = (step_x * x_conv).astype(jnp.bfloat16)
@@ -293,29 +302,55 @@
     rate_sum = crossing[0:1] - dot_left_exact(earlier, grad_log, 3)
     grad_step = dot_right_exact(grad_inputs * x_conv, spread, LAST) + rate_sum * head_rows[1:2]
     grad_dt = grad_step * sigmoid(dt_in)
-    head_grad_ref[0:1, :] += jnp.sum(grad_dt, 0, keepdims=True)
-    head_grad_ref[1:2, :] += jnp.sum(rate_sum * step, 0, keepdims=True) * head_rows[1:2]
+    small[7:8, 0:LANES] += jnp.sum(grad_dt, 0, keepdims=True)
+    small[8:9, 0:LANES] += jnp.sum(rate_sum * step, 0, keepdims=True) * head_rows[1:2]
     grad_x = grad_y * chan_ref[0:1] + grad_inputs * step_x
-    conv_grad_ref[5:6, 0:inner] += jnp.sum(grad_y * x_conv, 0, keepdims=True)
+    small[5:6, 0:inner] += jnp.sum(grad_y * x_conv, 0, keepdims=True)
     grad_pre = jnp.concatenate([grad_x, grad_b, grad_c], 1) * slope
     conv_in = conv_in_ref[...]
     ext_ref[0:SPAN, :] = grad_pre
     grad_conv_in = conv_ref[0:1] * grad_pre
-    conv_grad_ref[0:1, :] += jnp.sum(grad_pre * conv_in, 0, keepdims=True)
-    conv_grad_ref[4:5, :] += jnp.sum(grad_pre, 0, keepdims=True)
+    small[0:1, :] += jnp.sum(grad_pre * conv_in, 0, keepdims=True)
+    small[4:5, :] += jnp.sum(grad_pre, 0, keepdims=True)
     for lag in range(1, 4):
         term = ext_ref[lag : lag + SPAN, :] * cols[:, 7 + lag : 8 + lag]
         grad_conv_in = grad_conv_in + conv_ref[lag : lag + 1] * term
-        conv_grad_ref[lag : lag + 1, :] += jnp.sum(term * conv_in, 0, keepdims=True)
+        small[lag : lag + 1, :] += jnp.sum(term * conv_in, 0, keepdims=True)
     ext_ref[SPAN : SPAN + 8, :] = grad_pre[0:8]
     conv_low = grad_conv_in.astype(jnp.bfloat16)
     dt_low = grad_dt.astype(jnp.bfloat16)
     low = jnp.concatenate([conv_low, gz_ref[...], dt_low], 1)
     store_halves(place_ref, dot(low, wcat_ref[...], LAST), sent_ref, kept_ref)
     normed = normed_ref[...]
-    wx_grad_ref[...] += dot(normed, conv_low[:, :inner], FIRST)
-    wbc_grad_ref[...] += dot(normed, conv_low[:, inner:], FIRST)
-    wdt_grad_ref[...] += dot(dt_low, normed, FIRST)
+    upper_ref[...] += dot(normed[:, :top], conv_low, FIRST)
+    below_ref[0:top, :] += dot(normed[:, top:], conv_low, FIRST)
+    dt_grad = dot(dt_low, normed, FIRST)
+    small[16 : 16 + heads, 0:inner] += dt_grad[0:heads, :inner]
+    small[24 : 24 + heads, 0 : width - inner] += dt_grad[0:heads, inner:]
+
+    if befores:
+        early_ref, gate_grad_ref, gain_ref = befores[2:]
+
+        @pl.when(pl.program_id(0) == pl.num_programs(0) - 1)
+        def _():
+            small[6:7, 0:inner] = gate_grad_ref[0:1, :]
+            weights = wcat_ref[:, 0:conv_width].astype(jnp.float32)
+            first = jnp.sum(upper_ref[...] * weights[:top], 1, keepdims=True)
+            second = jnp.sum(below_ref[0:top, :] * weights[top:], 1, keepdims=True)
+            dt_all = jnp.concatenate(
+                [small[16 : 16 + heads, 0:inner], small[24 : 24 + heads, 0 : width - inner]], 1
+            )
+            blank = jnp.zeros((LANES - heads, width), jnp.float32)
+            dt_all = jnp.concatenate([dt_all, blank], 0).T
+            rest = jnp.concatenate([early_ref[inner : 2 * inner, :].T, dt_all], 1)
+            third = jnp.sum(
+                rest * wcat_ref[:, conv_width:].astype(jnp.float32), 1, keepdims=True
+            )
+            total = jnp.concatenate([first, second], 0) + third
+            row = jnp.broadcast_to(total, (width, LANES)).T[0:1] / gain_ref[...]
+            part = conv_width - inner
+            for place in range(width // part):
+                small[9 + place : 10 + place, inner:] = row[:, place * part : (place + 1) * part]
 
 
 def upper_ones():
@@ -324,11 +359,12 @@
     return down <= across
 
 
-def output_kernel(place_ref, own_ref, other_ref, hid_ref, cols_ref, *refs):
+def output_kernel(place_ref, own_ref, other_ref, hid_ref, flags_ref, *refs):
     out_ref = refs[-1]
+    live = flag_columns(flags_ref[...])[:, 4:5]
 
     def write(values):
-        out_ref[...] = (hid_ref[...].astype(jnp.float32) + cols_ref[:, 4:5] * values).astype(
+        out_ref[...] = (hid_ref[...].astype(jnp.float32) + live * values).astype(
             jnp.bfloat16
         )
 
@@ -378,6 +414,15 @@
         sent = lax.ppermute(take_half(values, 1 - mine), axis, partners(count, step))
         values = take_half(values, mine) + sent
     return values
+
+
+def half_sent(values, axis, count, step):
+    mine = (lax.axis_index(axis) // step) % 2
+    return lax.ppermute(take_half(values, 1 - mine), axis, partners(count, step))
+
+
+def half_kept(values, axis, step):
+    return take_half(values, (lax.axis_index(axis) // step) % 2)
 
 
 def axis_gather(values, axis, count, order):
@@ -482,24 +527,23 @@
         behind = jnp.concatenate([seg_ids[lag:], jnp.full((lag,), -1, jnp.int32)])
         return behind == seg_ids
 
-    cols = jnp.stack(
+    flags = jnp.stack(
         [
             seg_ids.astype(f32),
             conv_link(1).astype(f32),
             conv_link(2).astype(f32),
             conv_link(3).astype(f32),
             (positions < counts[0]).astype(f32),
-            (seg_spans == seg_end).reshape(rows).astype(f32),
-            (seg_spans == seg_prev).reshape(rows).astype(f32),
+            (seg_spans == seg_end).astype(f32).reshape(rows),
+            (seg_spans == seg_prev).astype(f32).reshape(rows),
             jnp.zeros((rows,), f32),
             conv_link_next(1).astype(f32),
             conv_link_next(2).astype(f32),
             conv_link_next(3).astype(f32),
-        ],
-        1,
-    )
-    cols = jnp.pad(cols, ((0, 0), (0, 16 - cols.shape[1])))
-    seg_rows = seg_spans.astype(f32)[:, None, :]
+        ]
+        + [jnp.zeros((rows,), f32)] * 5,
+        0,
+    )
     w_cat = jnp.concatenate([w_x, w_bc, w_z, jnp.pad(w_dt, ((0, 0), (0, LANES - heads)))], 1)
     conv_rows = jnp.concatenate(
         [
@@ -535,41 +579,36 @@
     half_rows = rows // 2
     grid = (half_spans,)
 
-    def forward(half):
-        base = half * half_spans
-        full = lambda columns: pl.BlockSpec((SPAN, columns), lambda i: (base + i, 0))
+    def forward():
+        full = lambda columns: pl.BlockSpec((SPAN, columns), lambda i: (i, 0))
         return call(
             functools.partial(fwd_kernel, heads=heads, inner=inner, conv_width=conv_width),
-            grid,
+            (spans,),
             (),
             (
-                hidden, cotangent, cols, seg_rows, gain, w_cat, w_out, conv_rows, head_rows,
-                spread, chan,
+                hidden, cotangent, flags, gain, w_cat, w_out, conv_rows, head_rows, spread, chan,
+            ),
+            [full(width), full(width), pl.BlockSpec((16, SPAN), lambda i: (0, i))]
+            + [whole(a) for a in (gain, w_cat, w_out, conv_rows, head_rows, spread, chan)],
+            (
+                shape(rows, width, dtype=bf16),
+                shape(rows, conv_width),
+                shape(rows, inner),
+                shape(rows, LANES),
+                shape(rows, conv_width),
+                shape(rows, inner),
+                shape(rows, inner),
+                shape(spans, states, inner, dtype=bf16),
+                shape(spans, 2, SPAN),
             ),
             [
-                full(width), full(width), full(16),
-                pl.BlockSpec((1, 1, SPAN), lambda i: (base + i, 0, 0)),
-            ]
-            + [whole(a) for a in (gain, w_cat, w_out, conv_rows, head_rows, spread, chan)],
-            (
-                shape(half_rows, width, dtype=bf16),
-                shape(half_rows, conv_width),
-                shape(half_rows, inner),
-                shape(half_rows, LANES),
-                shape(half_rows, conv_width),
-                shape(half_rows, inner),
-                shape(half_rows, inner),
-                shape(half_spans, states, inner, dtype=bf16),
-                shape(half_spans, 2, SPAN),
-            ),
-            [
-                local(width), local(conv_width), local(inner), local(LANES), local(conv_width),
-                local(inner), local(inner),
+                full(width), full(conv_width), full(inner), full(LANES), full(conv_width),
+                full(inner), full(inner),
                 pl.BlockSpec((1, states, inner), lambda i: (i, 0, 0)),
                 pl.BlockSpec((1, 2, SPAN), lambda i: (i, 0, 0)),
             ],
             [pltpu.VMEM((SPAN + 8, conv_width), f32), pltpu.VMEM((states, inner), f32)],
-            12_000_000_000,
+            20_000_000_000,
         )
 
     def tensor_small(sums):
@@ -580,16 +619,17 @@
     def gate(half, sums, gate_in, y_flat, grad_in, normed, before):
         base = half * half_spans
         full = lambda columns: pl.BlockSpec((SPAN, columns), lambda i, s: (base + i, 0))
-        totals = (shape(inner, width), shape(width, inner), shape(8, inner))
+        totals = (shape(2 * inner, width), shape(8, inner))
         return call(
             functools.partial(gate_kernel, inner=inner, inner_all=inner * n_tensor),
             grid,
             (place,),
-            (sums, gate_in, y_flat, grad_in, cotangent, cols, normed, w_out, chan) + before,
+            (sums, gate_in, y_flat, grad_in, cotangent, flags, normed, w_out, chan) + before,
             [
-                pl.BlockSpec((1, 2, SPAN), lambda i, s: (i, 0, 0)),
-                local(inner), local(inner), local(inner), full(width), full(16),
-                local(width), whole(w_out), whole(chan),
+                pl.BlockSpec((1, 2, SPAN), lambda i, s: (base + i, 0, 0)),
+                full(inner), full(inner), full(inner), full(width),
+                pl.BlockSpec((16, SPAN), lambda i, s: (0, base + i)),
+                full(width), whole(w_out), whole(chan),
             ]
             + [whole(a) for a in before],
             (
@@ -609,27 +649,21 @@
         base = half * half_spans
         turn = lambda i: base + half_spans - 1 - i
         full = lambda columns: pl.BlockSpec((SPAN, columns), lambda i, s: (turn(i), 0))
-        totals = (
-            shape(width, inner),
-            shape(width, bc_width),
-            shape(LANES, width),
-            shape(8, conv_width),
-            shape(8, LANES),
-        )
+        totals = (shape(width // 2, conv_width), shape(width // 2 + 64, conv_width))
         return call(
             functools.partial(bwd_kernel, heads=heads, inner=inner, conv_width=conv_width),
             grid,
             (place,),
             (
-                cols, seg_rows, normed, conv_in, dt_part, pre, y_flat, grad_y, grad_z, carried,
+                flags, normed, conv_in, dt_part, pre, y_flat, grad_y, grad_z, carried,
                 w_cat, conv_rows, head_rows, spread, chan,
             )
             + before,
             [
-                full(16), pl.BlockSpec((1, 1, SPAN), lambda i, s: (turn(i), 0, 0)),
-                back(width), back(conv_width), back(LANES), back(conv_width), back(inner),
+                pl.BlockSpec((16, SPAN), lambda i, s: (0, turn(i))),
+                full(width), full(conv_width), full(LANES), full(conv_width), full(inner),
                 back(inner), back(inner),
-                pl.BlockSpec((1, states, inner), lambda i, s: (half_spans - 1 - i, 0, 0)),
+                pl.BlockSpec((1, states, inner), lambda i, s: (turn(i), 0, 0)),
             ]
             + [whole(a) for a in (w_cat, conv_rows, head_rows, spread, chan)]
             + [whole(a) for a in before],
@@ -642,7 +676,11 @@
     def placed(kernel, half, own, other, extras, extra_specs, dtype, before):
         base = half * half_spans
         full = lambda columns: pl.BlockSpec((SPAN, columns), lambda i, s: (base + i, 0))
-        specs = [whole(a) if spec is None else full(spec) for a, spec in zip(extras, extra_specs)]
+        flag_spec = pl.BlockSpec((16, SPAN), lambda i, s: (0, base + i))
+        specs = [
+            whole(a) if spec is None else flag_spec if spec == 16 else full(spec)
+            for a, spec in zip(extras, extra_specs)
+        ]
         (made,) = call(
             kernel,
             grid,
@@ -657,86 +695,60 @@
         )
         return made
 
-    normed_a, conv_a, z_a, dt_a, pre_a, y_a, gin_a, carried_a, sums_a = forward(0)
-    normed_b, conv_b, z_b, dt_b, pre_b, y_b, gin_b, carried_b, sums_b = forward(1)
-    sums_a = tensor_small(sums_a)
-    sums_b = tensor_small(sums_b)
-    sent, kept, gy_a, gz_a, *gate_sums = gate(0, sums_a, z_a, y_a, gin_a, normed_a, ())
+    normed, conv_in, gate_in, dt_part, pre, y_flat, grad_in, carried, sums = forward()
+    sums = tensor_small(sums)
+    sent, kept, gy_a, gz_a, *gate_sums = gate(0, sums, gate_in, y_flat, grad_in, normed, ())
     mixed_a = chip_sum(sent, kept, n_tensor)
-    mixed_a, sums_b = together(mixed_a, sums_b)
+    mixed_a, sums = together(mixed_a, sums)
     far_mixed_a = far_sum(mixed_a, n_tensor)
     sent, kept, gy_b, gz_b, *gate_sums = gate(
-        1, sums_b, z_b, y_b, gin_b, normed_b, tuple(gate_sums)
-    )
-    part_out, part_z, gate_grad = gate_sums
+        1, sums, gate_in, y_flat, grad_in, normed, tuple(gate_sums)
+    )
+    early, gate_grad = gate_sums
     mixed_b = chip_sum(sent, kept, n_tensor)
+    order_y, order_z = dp_order(n_dp, 0), dp_order(n_dp, 1)
+    early_sent = half_sent(early, "dp", n_dp, order_y[0])
     mixed_b, gy_a = together(mixed_b, gy_a)
     far_mixed_b = far_sum(mixed_b, n_tensor)
     sent_a, kept_a, *bwd_sums = backward(
-        0, normed_a, conv_a, dt_a, pre_a, y_a, gy_a, gz_a, carried_a, ()
-    )
+        0, normed, conv_in, dt_part, pre, y_flat, gy_a, gz_a, carried, ()
+    )
+    early_kept, sent_a = together(early, sent_a)
+    early_parts = half_kept(early_kept, "dp", order_y[0]) + early_sent
+    sent_a, far_mixed_a, early_parts, gy_b = together(sent_a, far_mixed_a, early_parts, gy_b)
     normed_sum_a = chip_sum(sent_a, kept_a, n_tensor)
-    order_y, order_z = dp_order(n_dp, 0), dp_order(n_dp, 1)
-    out_parts = axis_scatter(part_out, "dp", n_dp, order_y[:1])
-    z_parts = axis_scatter(part_z, "dp", n_dp, order_z[:1])
-    normed_sum_a, far_mixed_a, out_parts, z_parts, gy_b = together(
-        normed_sum_a, far_mixed_a, out_parts, z_parts, gy_b
+    early_parts = axis_scatter(early_parts, "dp", n_dp, order_y[1:2])
+    sent_b, kept_b, upper, below = backward(
+        1, normed, conv_in, dt_part, pre, y_flat, gy_b, gz_b, carried,
+        tuple(bwd_sums) + (early, gate_grad, gain),
+    )
+    sent_b, far_mixed_b, normed_sum_a, early_parts, upper, below = together(
+        sent_b, far_mixed_b, normed_sum_a, early_parts, upper, below
     )
     far_normed_a = far_sum(normed_sum_a, n_tensor)
-    out_parts = axis_scatter(out_parts, "dp", n_dp, order_y[1:2])
-    z_parts = axis_scatter(z_parts, "dp", n_dp, order_z[1:2])
-    sent_b, kept_b, wx_part, wbc_part, wdt_part, conv_grad, head_grad = backward(
-        1, normed_b, conv_b, dt_b, pre_b, y_b, gy_b, gz_b, carried_b, tuple(bwd_sums)
-    )
-    sent_b, far_mixed_b, out_parts, z_parts, wx_part, wbc_part = together(
-        sent_b, far_mixed_b, out_parts, z_parts, wx_part, wbc_part
-    )
-    far_normed_b = far_sum(chip_sum(sent_b, kept_b, n_tensor), n_tensor)
-    wide = lambda values: values.astype(f32)
-    norm_grad = (
-        jnp.sum(wx_part * wide(w_x), 1)
-        + jnp.sum(part_z * wide(w_z), 1)
-        + jnp.sum(wbc_part * wide(w_bc), 1)
-        + jnp.sum(wdt_part[:heads].T * wide(w_dt), 1)
-    ) / norm_gain
-
-    def widen(values, columns):
-        flat = values.reshape(-1)
-        return jnp.pad(flat, (0, -flat.size % columns)).reshape(-1, columns)
-
-    bc_small = jnp.concatenate([conv_grad[:5, inner:].reshape(-1), norm_grad])
-    bc_parts = pad_rows(jnp.concatenate([wbc_part, widen(bc_small, bc_width)], 0), 16 * n_dp)
-    x_small = jnp.concatenate(
-        [
-            conv_grad[:5, :inner].reshape(-1),
-            gate_grad[0],
-            head_grad[0, :heads],
-            head_grad[1, :heads],
-            jnp.sum(conv_grad[5, :inner].reshape(heads, size), 1),
-            wdt_part[:heads].reshape(-1),
-        ]
-    )
-    x_parts = pad_rows(jnp.concatenate([wx_part, widen(x_small, inner)], 0), 8 * n_dp)
-    x_parts = axis_scatter(x_parts, "dp", n_dp, order_y)
-    bc_parts = axis_scatter(bc_parts, "tensor", n_tensor, [1])
-    bc_parts = axis_scatter(bc_parts, "dp", n_dp, order_z)
-    out_parts = axis_scatter(out_parts, "dp", n_dp, order_y[2:])
-    z_parts = axis_scatter(z_parts, "dp", n_dp, order_z[2:])
-    for step in steps_of(n_tensor)[1:]:
-        bc_parts = bc_parts + lax.ppermute(bc_parts, "tensor", partners(n_tensor, step))
-    out_grad = axis_gather(out_parts, "dp", n_dp, order_y)
-    z_grad = axis_gather(z_parts, "dp", n_dp, order_z)
-    x_parts = axis_gather(x_parts, "dp", n_dp, order_y)
-    bc_parts = axis_gather(bc_parts, "dp", n_dp, order_z)
-    bc_parts = axis_gather(bc_parts, "tensor", n_tensor, [1])
+    normed_sum_b = chip_sum(sent_b, kept_b, n_tensor)
+    upper = axis_scatter(upper, "dp", n_dp, order_y[:1])
+    below = axis_scatter(below, "dp", n_dp, order_z[:1])
+    normed_sum_b, upper, below = together(normed_sum_b, upper, below)
+    far_normed_b = far_sum(normed_sum_b, n_tensor)
+    upper = axis_scatter(upper, "dp", n_dp, order_y[1:])
+    below = axis_scatter(below, "dp", n_dp, order_z[1:])
+    early_parts = axis_scatter(early_parts, "dp", n_dp, order_y[2:])
+    shared = tensor_small(jnp.concatenate([upper[:, inner:], below[:, inner:]], 0))
+    upper = jnp.concatenate([upper[:, :inner], shared[: upper.shape[0]]], 1)
+    below = jnp.concatenate([below[:, :inner], shared[upper.shape[0] :]], 1)
     output = placed(
-        output_kernel, 0, far_mixed_a, chip_other(far_mixed_a, n_tensor), (hidden, cols),
+        output_kernel, 0, far_mixed_a, chip_other(far_mixed_a, n_tensor), (hidden, flags),
         (width, 16), bf16, (),
     )
     output = placed(
-        output_kernel, 1, far_mixed_b, chip_other(far_mixed_b, n_tensor), (hidden, cols),
+        output_kernel, 1, far_mixed_b, chip_other(far_mixed_b, n_tensor), (hidden, flags),
         (width, 16), bf16, (output,),
     )
+    upper, below, output = together(upper, below, output)
+    early_sum = axis_gather(early_parts, "dp", n_dp, order_y)
+    upper = axis_gather(upper, "dp", n_dp, order_y)
+    below = axis_gather(below, "dp", n_dp, order_z)
     grad_hidden = placed(
         finish_kernel, 0, far_normed_a, chip_other(far_normed_a, n_tensor),
         (hidden, cotangent, gain), (width, width, None), f32, (),
@@ -745,29 +757,29 @@
         finish_kernel, 1, far_normed_b, chip_other(far_normed_b, n_tensor),
         (hidden, cotangent, gain), (width, width, None), f32, (grad_hidden,),
     )
-    x_small = x_parts[width:].reshape(-1)
-    bc_small = bc_parts[width:].reshape(-1)
-    at = (taps + 1) * inner
-    heads_at = at + inner
-    dt_at = heads_at + 3 * heads
-    bc_at = (taps + 1) * bc_width
+    top = width // 2
+    small = below[top:]
+    norm_rows = width // bc_width
+    dt_grad = jnp.concatenate(
+        [small[16 : 16 + heads, :inner], small[24 : 24 + heads, : width - inner]], 1
+    )
     return (
         output,
         grad_hidden,
-        bc_small[bc_at : bc_at + width],
-        x_parts[:width],
-        z_grad,
-        x_small[dt_at : dt_at + heads * width].reshape(heads, width).T,
-        bc_parts[:width],
-        x_small[: taps * inner].reshape(taps, inner),
-        x_small[taps * inner : at],
-        bc_small[: taps * bc_width].reshape(taps, bc_width),
-        bc_small[taps * bc_width : bc_at],
-        x_small[heads_at : heads_at + heads],
-        x_small[heads_at + heads : heads_at + 2 * heads],
-        x_small[heads_at + 2 * heads : dt_at],
-        x_small[at : at + inner],
-        out_grad,
+        small[9 : 9 + norm_rows, inner:].reshape(-1),
+        jnp.concatenate([upper[:, :inner], below[:top, :inner]], 0),
+        early_sum[inner:].T,
+        dt_grad.T,
+        jnp.concatenate([upper[:, inner:], below[:top, inner:]], 0),
+        small[:taps, :inner],
+        small[taps, :inner],
+        small[:taps, inner:],
+        small[taps, inner:],
+        small[7, :heads],
+        small[8, :heads],
+        jnp.sum(small[5, :inner].reshape(heads, size), 1),
+        small[6, :inner],
+        early_sum[:inner],
     )
 
 

time: 339 us -> 333 us (0.982)
  local copies, waits for them, and re-layouts: 38.4 us -> 29.6 us
  starting transfers between devices: 33.8 us -> 41.3 us
    ppermute x4, waiting for transfers between devices: 5.33 us -> 35.3 us  [tensor_small(): sums = sums + lax.ppermute(sums, 'tensor', partners(n_tensor, step))]
    ppermute x13 -> x8, waiting for transfers between devices: 41.4 us -> 18.7 us  [axis_scatter(): lax.ppermute(take_half(values, 1 - mine), axis, partners(count, step))]
    ppermute x13 -> x9, waiting for transfers between devices: 45.3 us -> 22.7 us  [axis_gather(): other = lax.ppermute(values, axis, partners(count, step))]
    ppermute x4, waiting for transfers between devices: 0.01 us -> 16.7 us  [far_sum(): values = values + lax.ppermute(values, 'tensor', partners(count, step))]
    slice x16 -> x17, local copies, waits for them, and re-layouts: 12.6 us -> 7.51 us  [the longest x1 1.79 us: per_device(): early_sum[:inner]]
    ppermute x13 -> x9, starting transfers between devices: 8.51 us -> 13.1 us  [axis_gather(): other = lax.ppermute(values, axis, partners(count, step))]
    reshape x7 -> x1, local copies, waits for them, and re-layouts: 4.65 us -> 0.6 us  [per_device(): small[9:9 + norm_rows, inner:].reshape(-1)]
    select_n x13 -> x9, other arithmetic: 12.3 us -> 9.07 us  [join_halves(): jnp.where(mine == 0, jnp.concatenate([own, other], 0), jnp.concatenate([o...]
  transfers between devices with their start and end apart: 43 -> 34, of which waited for: 23 -> 17; matrix products, arithmetic and copies ran while one was open for 21% -> 16% of each run, Pallas kernels for 23% -> 19%
where the time goes in v4:
time: 333 us; the launch traced here: 331 us
  Pallas kernels  115 us (35%)
  waiting for transfers between devices  97 us (29%)
  other arithmetic  46 us (14%)
  starting transfers between devices  41.3 us (12%)
  local copies, waits for them, and re-layouts  29.6 us (9%)
    pallas_call x9, Pallas kernels, call(): pl.pallas_call(kernel, grid_spec=pltpu.PrefetchScalarGridSpec(num_scalar_...  115 us
    ppermute x4, waiting for transfers between devices, tensor_small(): sums = sums + lax.ppermute(sums, 'tensor', partners(n_tensor, step))  35.3 us
    ppermute x9, waiting for transfers between devices, axis_gather(): other = lax.ppermute(values, axis, partners(count, step))  22.7 us
    ppermute x8, waiting for transfers between devices, axis_scatter(): lax.ppermute(take_half(values, 1 - mine), axis, partners(count, step))  18.7 us
    ppermute x4, waiting for transfers between devices, far_sum(): values = values + lax.ppermute(values, 'tensor', partners(count, step))  16.7 us
    ppermute x8, starting transfers between devices, axis_scatter(): lax.ppermute(take_half(values, 1 - mine), axis, partners(count, step))  14.9 us
    ppermute x9, starting transfers between devices, axis_gather(): other = lax.ppermute(values, axis, partners(count, step))  13.1 us
    select_n x9, other arithmetic, join_halves(): jnp.where(mine == 0, jnp.concatenate([own, other], 0), jnp.concatenate([o...  9.07 us
  transfers between devices with their start and end apart: 34, of which 17 were waited for; matrix products, arithmetic and copies ran while one was open for 16% of the time, Pallas kernels for 19%

profile of v4, /device:TPU:0, one launch (start us, length us, event | category | flops | bytes accessed | tf_op | source)
XLA Modules:
  0.0 331.2 jit_solution(469743919462957225)
XLA Ops:
  7.3 1.3 broadcast_in_dim.11.gain_ref.refs_4_
  12.2 1.3 select_maximum_fusion.3.head_ref
  13.4 1.3 select_maximum_fusion.conv_ref
  14.7 2.8 fusion.1.wcat_ref
  17.7 1.4 stack.75.flags_ref
  19.1 25.2 %shard_map.297 = (bf16[2048,768]{1,0:T(8,128)(2,1)}, f32[2048,640]{1,0:T(8,128)}, f32[2048,384]{1,0:T(8,128)}, f32[2048,128]{1,0:T(8,128)}, f32[2048,640]{1,0:T(...) custom-call(bf16[2048,768]{1,0:T(8,128)(2,1)} %hid_ref.9, ...), custom_call_target="tpu_custom_call" | custom-call | flops 20000000000 | bytes 33840128 | tf_op jit(solution)/shard_map/pallas_call | solution.py:467
  46.6 2.9 collective-permute-start.1
  49.5 1.7 collective-permute-done.1
  51.8 9.6 %shard_map.298 = (f32[1024,384]{1,0:T(8,128)}, f32[1024,384]{1,0:T(8,128)}, f32[1024,384]{1,0:T(8,128)}, bf16[1024,384]{1,0:T(8,128)(2,1)}, f32[768,768]{1,0:T(8,128)}, /*index=5*/f32[8,384]{1,0:T(8,128)}) custom-call(s32[1]{0:T(128)} %bitcast.place_ref, f32[8,2,256]{2,1,0:T(2,128)} %add.173.sums_ref, f32[2048,384]{1,0:T(8,128)} %get-tuple-element.73.z_ref, ...), custom_call_target="tpu_custom_call" | custom-call | flops 8000000000 | bytes 24354816 | tf_op jit(solution)/shard_map/pallas_call | solution.py:467
  61.5 3.6 %collective-permute-done.2 = f32[1024,384]{1,0:T(8,128)S(1)} collective-permute-done((f32[1024,384]{1,0:T(8,128)}, f32[1024,384]{1,0:T(8,128)S(1)}, u32[]{:S(2)}, u32[]{:S(2)}) %collective-permute-start.2) | collective-permute-done | bytes 1572896 | tf_op jit(solution)/shard_map/ppermute | solution.py:446
  65.1 1.6 add.174
  66.7 11.1 %shard_map.299 = (f32[1024,384]{1,0:T(8,128)}, f32[1024,384]{1,0:T(8,128)}, f32[1024,384]{1,0:T(8,128)}, bf16[1024,384]{1,0:T(8,128)(2,1)}, f32[768,768]{1,0:T(8,128)}, /*index=5*/f32[8,384]{1,0:T(8,128)}) custom-call(s32[1]{0:T(128)} %bitcast.place_ref, f32[8,2,256]{2,1,0:T(2,128)} %add.173.sums_ref, f32[2048,384]{1,0:T(8,128)} %get-tuple-element.73.z_ref, ...), custom_call_target="tpu_custom_call" | custom-call | flops 8000000000 | bytes 26726400 | tf_op jit(solution)/shard_map/pallas_call | solution.py:467
  78.1 2.5 constant_dynamic-slice_fusion.8
  80.6 2.0 collective-permute-start.5
  82.6 1.5 collective-permute-start.4
  84.1 1.2 copy-done.10
  85.3 1.6 add.175
  86.9 22.9 %shard_map.300 = (f32[1024,384]{1,0:T(8,128)}, f32[1024,384]{1,0:T(8,128)}, f32[384,640]{1,0:T(8,128)}, f32[448,640]{1,0:T(8,128)}) custom-call(s32[1]{0:T(128)} %bitcast.place_ref, f32[16,2048]{1,0:T(8,128)} %stack.75.flags_ref, bf16[2048,768]{1,0:T(8,128)(2,1)} %get-tuple-element.67.normed_ref, f32[2048,640]{1,0:T(8,128)} %get-tuple-element.68.conv_in_ref, ...), custom_call_target="tpu_custom_call" | custom-call | flops 20000000000 | bytes 28282880 | tf_op jit(solution)/shard_map/pallas_call | solution.py:467
  109.8 9.3 %collective-permute-done.4 = f32[1024,384]{1,0:T(8,128)} collective-permute-done((f32[1024,384]{1,0:T(8,128)S(1)}, f32[1024,384]{1,0:T(8,128)}, u32[]{:S(2)}, u32[]{:S(2)}) %collective-permute-start.4) | collective-permute-done | bytes 1572896 | tf_op jit(solution)/shard_map/ppermute | solution.py:451
  119.1 2.7 add.176.own_ref
  121.8 1.4 dynamic-slice_add_fusion
  124.2 1.6 collective-permute-start.8
  126.0 1.5 collective-permute-start.6
  127.5 25.9 %shard_map.301 = (f32[1024,384]{1,0:T(8,128)}, f32[1024,384]{1,0:T(8,128)}, f32[384,640]{1,0:T(8,128)}, f32[448,640]{1,0:T(8,128)}) custom-call(s32[1]{0:T(128)} %bitcast.place_ref, f32[16,2048]{1,0:T(8,128)} %stack.75.flags_ref, bf16[2048,768]{1,0:T(8,128)(2,1)} %get-tuple-element.67.normed_ref, f32[2048,640]{1,0:T(8,128)} %get-tuple-element.68.conv_in_ref, ...), custom_call_target="tpu_custom_call" | custom-call | flops 20000000000 | bytes 32787456 | tf_op jit(solution)/shard_map/pallas_call | solution.py:467
  153.4 2.0 dynamic-slice_add_fusion.1
  155.4 7.3 %collective-permute-done.6 = f32[1024,384]{1,0:T(8,128)} collective-permute-done((f32[1024,384]{1,0:T(8,128)S(1)}, f32[1024,384]{1,0:T(8,128)}, u32[]{:S(2)}, u32[]{:S(2)}) %collective-permute-start.6) | collective-permute-done | bytes 1572896 | tf_op jit(solution)/shard_map/ppermute | solution.py:451
  162.7 1.6 add.181.own_ref
  164.3 2.1 add.182
  167.0 2.2 constant_dynamic-slice_fusion.5
  169.6 1.7 constant_dynamic-slice_fusion
  171.3 2.6 collective-permute-start.30
  175.2 4.7 %shard_map.302.refs_0_ = bf16[2048,768]{1,0:T(8,128)(2,1)} custom-call(s32[1]{0:T(128)} %bitcast.place_ref, f32[1024,384]{1,0:T(8,128)} %add.176.own_ref, f32[1024,384]{1,0:T(8,128)} %collective-permute-done.19.other_ref, bf16[2048,768]{1,0:T(8,128)(2,1)} %hid_ref.9, f32[16,2048]{1,0:T(8,128)} %stack.75.flags_ref), custom_call_target="tpu_custom_call" | custom-call | flops 3000000000 | bytes 9568256 | tf_op jit(solution)/shard_map/pallas_call | solution.py:467
  179.9 8.8 %collective-permute-done.30 = f32[96,768]{1,0:T(8,128)S(1)} collective-permute-done((f32[96,768]{1,0:T(8,128)}, f32[96,768]{1,0:T(8,128)S(1)}, u32[]{:S(2)}, u32[]{:S(2)}) %collective-permute-start.30) | collective-permute-done | bytes 294944 | tf_op jit(solution)/shard_map/ppermute | solution.py:414
  188.7 1.5 collective-permute-start.22
  191.2 3.3 %collective-permute-start.31 = (f32[96,768]{1,0:T(8,128)S(1)}, f32[96,768]{1,0:T(8,128)S(1)}, u32[]{:S(2)}, u32[]{:S(2)}) collective-permute-start(f32[96,768]{1,0:T(8,128)S(1)} %dynamic-slice_add_fusion.4), channel_id=1, source_target_pairs={{0,16},{4,20},{8,24},{12,28},{16,0},{20,4},{24,8},{28,12},{1,17},{... | collective-permute-start | bytes 884744 | tf_op jit(solution)/shard_map/ppermute | solution.py:431
  194.5 1.2 dynamic-slice_add_fusion.3
  195.8 1.1 dynamic-slice_add_fusion.2
  196.9 2.7 add.187
  199.7 1.4 collective-permute-start.12
  201.1 5.9 %collective-permute-done.31 = f32[96,768]{1,0:T(8,128)S(1)} collective-permute-done((f32[96,768]{1,0:T(8,128)S(1)}, f32[96,768]{1,0:T(8,128)S(1)}, u32[]{:S(2)}, u32[]{:S(2)}) %collective-permute-start.31) | collective-permute-done | bytes 294944 | tf_op jit(solution)/shard_map/ppermute | solution.py:431
  208.4 1.2 collective-permute-done.12
  209.7 4.3 %collective-permute-start.13 = (f32[48,640]{1,0:T(8,128)S(1)}, f32[48,640]{1,0:T(8,128)S(1)}, u32[]{:S(2)}, u32[]{:S(2)}) collective-permute-start(f32[48,640]{1,0:T(8,128)S(1)} %constant_dynamic-slice_fusion.3), channel_id=1, source_target_pairs={{0,16},{4,20},{8,24},{12,28},{16,0},{20,4},{24,8},{28,12},{1,17},{... | collective-permute-start | bytes 368648 | tf_op jit(solution)/shard_map/ppermute | solution.py:414
  214.0 2.3 collective-permute-done.14
  216.4 3.4 %collective-permute-start.15 = (f32[56,640]{1,0:T(8,128)S(1)}, f32[56,640]{1,0:T(8,128)S(1)}, u32[]{:S(2)}, u32[]{:S(2)}) collective-permute-start(f32[56,640]{1,0:T(8,128)S(1)} %constant_dynamic-slice_fusion.1), channel_id=1, source_target_pairs={{0,16},{4,20},{8,24},{12,28},{16,0},{20,4},{24,8},{28,12},{1,17},{... | collective-permute-start | bytes 430088 | tf_op jit(solution)/shard_map/ppermute | solution.py:414
  219.9 4.3 %collective-permute-done.13 = f32[48,640]{1,0:T(8,128)S(1)} collective-permute-done((f32[48,640]{1,0:T(8,128)S(1)}, f32[48,640]{1,0:T(8,128)S(1)}, u32[]{:S(2)}, u32[]{:S(2)}) %collective-permute-start.13) | collective-permute-done | bytes 122912 | tf_op jit(solution)/shard_map/ppermute | solution.py:414
  224.2 2.1 collective-permute-done.15
  229.7 1.8 collective-permute-start.17
  231.5 4.7 %shard_map.303 = bf16[2048,768]{1,0:T(8,128)(2,1)} custom-call(s32[1]{0:T(128)} %bitcast.place_ref, f32[1024,384]{1,0:T(8,128)} %copy-done, f32[1024,384]{1,0:T(8,128)} %collective-permute-done.18.other_ref, bf16[2048,768]{1,0:T(8,128)(2,1)} %hid_ref.9, f32[16,2048]{1,0:T(8,128)} %stack.75.flags_ref, ...), custom_call_target="tpu_custom_call", output_to_operand_aliasing={{}: (5, {})} | custom-call | flops 3000000000 | bytes 12713984 | tf_op jit(solution)/shard_map/pallas_call | solution.py:467
  236.2 32.5 %collective-permute-done.17 = f32[104,256]{1,0:T(8,128)} collective-permute-done((f32[104,256]{1,0:T(8,128)S(1)}, f32[104,256]{1,0:T(8,128)}, u32[]{:S(2)}, u32[]{:S(2)}) %collective-permute-start.17) | collective-permute-done | bytes 106528 | tf_op jit(solution)/shard_map/ppermute | solution.py:616
  269.7 4.7 %collective-permute-start.27 = (f32[48,640]{1,0:T(8,128)S(1)}, f32[48,640]{1,0:T(8,128)S(1)}, u32[]{:S(2)}, u32[]{:S(2)}) collective-permute-start(f32[48,640]{1,0:T(8,128)S(1)} %pad_maximum_fusion.3), channel_id=1, source_target_pairs={{0,16},{4,20},{8,24},{12,28},{16,0},{20,4},{24,8},{28,12},{1,17},{... | collective-permute-start | bytes 368648 | tf_op jit(solution)/shard_map/ppermute | solution.py:431
  274.5 9.3 %collective-permute-done.27 = f32[48,640]{1,0:T(8,128)S(1)} collective-permute-done((f32[48,640]{1,0:T(8,128)S(1)}, f32[48,640]{1,0:T(8,128)S(1)}, u32[]{:S(2)}, u32[]{:S(2)}) %collective-permute-start.27) | collective-permute-done | bytes 122912 | tf_op jit(solution)/shard_map/ppermute | solution.py:431
  284.1 2.3 collective-permute-done.24
  286.4 1.6 collective-permute-start.25
  288.0 3.6 %collective-permute-done.28 = f32[96,640]{1,0:T(8,128)S(1)} collective-permute-done((f32[96,640]{1,0:T(8,128)S(1)}, f32[96,640]{1,0:T(8,128)S(1)}, u32[]{:S(2)}, u32[]{:S(2)}) %collective-permute-start.28) | collective-permute-done | bytes 245792 | tf_op jit(solution)/shard_map/ppermute | solution.py:431
  292.4 1.5 collective-permute-start.29
  293.9 2.9 maximum_select_fusion
  298.0 2.0 add.209.own_ref
  300.1 1.8 fusion.13
  302.0 2.7 copy.44
  305.3 1.6 maximum_select_fusion.3
  308.5 5.7 %shard_map.304.refs_0_ = f32[2048,768]{1,0:T(8,128)} custom-call(s32[1]{0:T(128)} %bitcast.place_ref, f32[1024,384]{1,0:T(8,128)} %copy-done.1, f32[1024,384]{1,0:T(8,128)} %collective-permute-done.23.other_ref, bf16[2048,768]{1,0:T(8,128)(2,1)} %hid_ref.9, bf16[2048,768]{1,0:T(8,128)(2,1)} %cot_ref.9, f32[1,768]{1,0:T(1,128)} %broadcast_in_dim.11.gain_ref.refs_4_), custom_call_target="tpu_custom_call" | custom-call | flops 3000000000 | bytes 15731712 | tf_op jit(solution)/shard_map/pallas_call | solution.py:467
  314.2 1.8 maximum_select_fusion.2
  321.9 2.0 pad_maximum_fusion.1
  325.6 5.6 %shard_map.305 = f32[2048,768]{1,0:T(8,128)} custom-call(s32[1]{0:T(128)} %bitcast.place_ref, f32[1024,384]{1,0:T(8,128)} %copy-done.2, f32[1024,384]{1,0:T(8,128)} %collective-permute-done.21.other_ref, bf16[2048,768]{1,0:T(8,128)(2,1)} %hid_ref.9, bf16[2048,768]{1,0:T(8,128)(2,1)} %cot_ref.9, ...), custom_call_target="tpu_custom_call", output_to_operand_aliasing={{}: (6, {})} | custom-call | flops 3000000000 | bytes 22023168 | tf_op jit(solution)/shard_map/pallas_call | solution.py:467
  (142 shorter events, 35.6 us)
Async XLA Ops:
  14.7 2.8 copy-start.14
  44.2 1.6 collective-permute-start
  46.6 4.6 %collective-permute-start.1 = (f32[8,2,256]{2,1,0:T(2,128)S(1)}, f32[8,2,256]{2,1,0:T(2,128)S(1)}, u32[]{:S(2)}, u32[]{:S(2)}) collective-permute-start(f32[8,2,256]{2,1,0:T(2,128)S(1)} %add.172), channel_id=1, source_target_pairs={{0,2},{1,3},{2,0},{3,1},{4,6},{5,7},{6,4},{7,5},{8,10},{9,11},{10,... | collective-permute-start | bytes 49160 | tf_op jit(solution)/shard_map/ppermute | solution.py:616
  61.4 3.7 %collective-permute-start.2 = (f32[1024,384]{1,0:T(8,128)}, f32[1024,384]{1,0:T(8,128)S(1)}, u32[]{:S(2)}, u32[]{:S(2)}) collective-permute-start(f32[1024,384]{1,0:T(8,128)} %get-tuple-element.76), channel_id=1, source_target_pairs={{0,1},{1,0},{2,3},{3,2},{4,5},{5,4},{6,7},{7,6},{8,9},{9,8},{10,11... | collective-permute-start | bytes 4718600 | tf_op jit(solution)/shard_map/ppermute | solution.py:446
  77.9 6.2 %collective-permute-start.3 = (f32[1024,384]{1,0:T(8,128)}, f32[1024,384]{1,0:T(8,128)S(1)}, u32[]{:S(2)}, u32[]{:S(2)}) collective-permute-start(f32[1024,384]{1,0:T(8,128)} %get-tuple-element.82), channel_id=1, source_target_pairs={{0,1},{1,0},{2,3},{3,2},{4,5},{5,4},{6,7},{7,6},{8,9},{9,8},{10,11... | collective-permute-start | bytes 4718600 | tf_op jit(solution)/shard_map/ppermute | solution.py:446
  78.1 7.2 %copy-start.9 = (f32[1024,384]{1,0:T(8,128)S(1)}, f32[1024,384]{1,0:T(8,128)}, u32[]{:S(2)}) copy-start(f32[1024,384]{1,0:T(8,128)} %get-tuple-element.81) | copy-start | bytes 4718596
  80.6 41.2 %collective-permute-start.5 = (f32[384,768]{1,0:T(8,128)}, f32[384,768]{1,0:T(8,128)}, u32[]{:S(2)}, u32[]{:S(2)}) collective-permute-start(f32[384,768]{1,0:T(8,128)} %constant_dynamic-slice_fusion.8), channel_id=1, source_target_pairs={{0,4},{4,0},{8,12},{12,8},{16,20},{20,16},{24,28},{28,24},{1,5},{5... | collective-permute-start | bytes 3538952 | tf_op jit(solution)/shard_map/ppermute | solution.py:421
  82.6 36.5 %collective-permute-start.4 = (f32[1024,384]{1,0:T(8,128)S(1)}, f32[1024,384]{1,0:T(8,128)}, u32[]{:S(2)}, u32[]{:S(2)}) collective-permute-start(f32[1024,384]{1,0:T(8,128)S(1)} %add.174), channel_id=1, source_target_pairs={{0,2},{1,3},{2,0},{3,1},{4,6},{5,7},{6,4},{7,5},{8,10},{9,11},{10,... | collective-permute-start | bytes 4718600 | tf_op jit(solution)/shard_map/ppermute | solution.py:451
  84.1 1.2 copy-start.10
  109.7 12.1 %copy-start.5 = (f32[768,768]{1,0:T(8,128)S(1)}, f32[768,768]{1,0:T(8,128)}, u32[]{:S(2)}) copy-start(f32[768,768]{1,0:T(8,128)} %get-tuple-element.90.refs_2_) | copy-start | bytes 7077892
  123.2 51.5 %collective-permute-start.19 = (f32[1024,384]{1,0:T(8,128)}, f32[1024,384]{1,0:T(8,128)}, u32[]{:S(2)}, u32[]{:S(2)}) collective-permute-start(f32[1024,384]{1,0:T(8,128)} %add.176.own_ref), channel_id=1, source_target_pairs={{0,1},{1,0},{2,3},{3,2},{4,5},{5,4},{6,7},{7,6},{8,9},{9,8},{10,11... | collective-permute-start | bytes 4718600 | tf_op jit(solution)/shard_map/ppermute | solution.py:456
  124.2 29.2 %collective-permute-start.8 = (f32[192,768]{1,0:T(8,128)}, f32[192,768]{1,0:T(8,128)}, u32[]{:S(2)}, u32[]{:S(2)}) collective-permute-start(f32[192,768]{1,0:T(8,128)} %constant_dynamic-slice_fusion.7), channel_id=1, source_target_pairs={{0,8},{4,12},{8,0},{12,4},{16,24},{20,28},{24,16},{28,20},{1,9},{5... | collective-permute-start | bytes 1769480 | tf_op jit(solution)/shard_map/ppermute | solution.py:414
  125.8 38.5 %collective-permute-start.7 = (f32[1024,384]{1,0:T(8,128)}, f32[1024,384]{1,0:T(8,128)}, u32[]{:S(2)}, u32[]{:S(2)}) collective-permute-start(f32[1024,384]{1,0:T(8,128)} %get-tuple-element.101), channel_id=1, source_target_pairs={{0,1},{1,0},{2,3},{3,2},{4,5},{5,4},{6,7},{7,6},{8,9},{9,8},{10,11... | collective-permute-start | bytes 4718600 | tf_op jit(solution)/shard_map/ppermute | solution.py:446
  126.0 36.7 %collective-permute-start.6 = (f32[1024,384]{1,0:T(8,128)S(1)}, f32[1024,384]{1,0:T(8,128)}, u32[]{:S(2)}, u32[]{:S(2)}) collective-permute-start(f32[1024,384]{1,0:T(8,128)S(1)} %add.175), channel_id=1, source_target_pairs={{0,2},{1,3},{2,0},{3,1},{4,6},{5,7},{6,4},{7,5},{8,10},{9,11},{10,... | collective-permute-start | bytes 4718600 | tf_op jit(solution)/shard_map/ppermute | solution.py:451
  155.4 8.9 %copy-start.11 = (f32[1024,384]{1,0:T(8,128)S(1)}, f32[1024,384]{1,0:T(8,128)}, u32[]{:S(2)}) copy-start(f32[1024,384]{1,0:T(8,128)} %get-tuple-element.100) | copy-start | bytes 4718596
  164.2 2.4 copy-start
  166.4 22.3 %copy-start.3 = (f32[1024,384]{1,0:T(8,128)}, f32[1024,384]{1,0:T(8,128)S(1)}, u32[]{:S(2)}) copy-start(f32[1024,384]{1,0:T(8,128)S(1)} %add.182) | copy-start | bytes 4718596
  166.4 30.5 %collective-permute-start.9 = (f32[1024,384]{1,0:T(8,128)}, f32[1024,384]{1,0:T(8,128)}, u32[]{:S(2)}, u32[]{:S(2)}) collective-permute-start(f32[1024,384]{1,0:T(8,128)} %get-tuple-element.105), channel_id=1, source_target_pairs={{0,1},{1,0},{2,3},{3,2},{4,5},{5,4},{6,7},{7,6},{8,9},{9,8},{10,11... | collective-permute-start | bytes 4718600 | tf_op jit(solution)/shard_map/ppermute | solution.py:446
  166.6 7.3 %copy-start.13 = (f32[384,640]{1,0:T(8,128)S(1)}, f32[384,640]{1,0:T(8,128)}, u32[]{:S(2)}) copy-start(f32[384,640]{1,0:T(8,128)} %get-tuple-element.106) | copy-start | bytes 2949124
  166.6 64.9 %collective-permute-start.18 = (f32[1024,384]{1,0:T(8,128)S(1)}, f32[1024,384]{1,0:T(8,128)}, u32[]{:S(2)}, u32[]{:S(2)}) collective-permute-start(f32[1024,384]{1,0:T(8,128)S(1)} %add.181.own_ref), channel_id=1, source_target_pairs={{0,1},{1,0},{2,3},{3,2},{4,5},{5,4},{6,7},{7,6},{8,9},{9,8},{10,11... | collective-permute-start | bytes 4718600 | tf_op jit(solution)/shard_map/ppermute | solution.py:456
  169.2 26.6 %collective-permute-start.11 = (f32[224,640]{1,0:T(8,128)}, f32[224,640]{1,0:T(8,128)}, u32[]{:S(2)}, u32[]{:S(2)}) collective-permute-start(f32[224,640]{1,0:T(8,128)} %constant_dynamic-slice_fusion.5), channel_id=1, source_target_pairs={{0,8},{4,12},{8,0},{12,4},{16,24},{20,28},{24,16},{28,20},{1,9},{5... | collective-permute-start | bytes 1720328 | tf_op jit(solution)/shard_map/ppermute | solution.py:414
  171.3 17.4 %collective-permute-start.30 = (f32[96,768]{1,0:T(8,128)}, f32[96,768]{1,0:T(8,128)S(1)}, u32[]{:S(2)}, u32[]{:S(2)}) collective-permute-start(f32[96,768]{1,0:T(8,128)} %constant_dynamic-slice_fusion), channel_id=1, source_target_pairs={{0,16},{4,20},{8,24},{12,28},{16,0},{20,4},{24,8},{28,12},{1,17},{... | collective-permute-start | bytes 884744 | tf_op jit(solution)/shard_map/ppermute | solution.py:414
  174.7 16.5 %collective-permute-start.10 = (f32[192,640]{1,0:T(8,128)}, f32[192,640]{1,0:T(8,128)}, u32[]{:S(2)}, u32[]{:S(2)}) collective-permute-start(f32[192,640]{1,0:T(8,128)} %constant_dynamic-slice_fusion.6), channel_id=1, source_target_pairs={{0,4},{4,0},{8,12},{12,8},{16,20},{20,16},{24,28},{28,24},{1,5},{5... | collective-permute-start | bytes 1474568 | tf_op jit(solution)/shard_map/ppermute | solution.py:414
  179.9 15.9 %copy-start.12 = (f32[448,640]{1,0:T(8,128)S(1)}, f32[448,640]{1,0:T(8,128)}, u32[]{:S(2)}) copy-start(f32[448,640]{1,0:T(8,128)} %get-tuple-element.107) | copy-start | bytes 3440644
  188.7 40.4 %collective-permute-start.22 = (f32[1024,384]{1,0:T(8,128)S(1)}, f32[1024,384]{1,0:T(8,128)S(1)}, u32[]{:S(2)}, u32[]{:S(2)}) collective-permute-start(f32[1024,384]{1,0:T(8,128)S(1)} %add.182), channel_id=1, source_target_pairs={{0,2},{1,3},{2,0},{3,1},{4,6},{5,7},{6,4},{7,5},{8,10},{9,11},{10,... | collective-permute-start | bytes 4718600 | tf_op jit(solution)/shard_map/ppermute | solution.py:451
  191.2 5.8 %copy-start.8 = (f32[1024,384]{1,0:T(8,128)S(1)}, f32[1024,384]{1,0:T(8,128)}, u32[]{:S(2)}) copy-start(f32[1024,384]{1,0:T(8,128)} %get-tuple-element.97) | copy-start | bytes 4718596
  191.2 15.8 %collective-permute-start.31 = (f32[96,768]{1,0:T(8,128)S(1)}, f32[96,768]{1,0:T(8,128)S(1)}, u32[]{:S(2)}, u32[]{:S(2)}) collective-permute-start(f32[96,768]{1,0:T(8,128)S(1)} %dynamic-slice_add_fusion.4), channel_id=1, source_target_pairs={{0,16},{4,20},{8,24},{12,28},{16,0},{20,4},{24,8},{28,12},{1,17},{... | collective-permute-start | bytes 884744 | tf_op jit(solution)/shard_map/ppermute | solution.py:431
  199.7 9.9 %collective-permute-start.12 = (f32[96,640]{1,0:T(8,128)S(1)}, f32[96,640]{1,0:T(8,128)S(1)}, u32[]{:S(2)}, u32[]{:S(2)}) collective-permute-start(f32[96,640]{1,0:T(8,128)S(1)} %constant_dynamic-slice_fusion.4), channel_id=1, source_target_pairs={{0,8},{4,12},{8,0},{12,4},{16,24},{20,28},{24,16},{28,20},{1,9},{5... | collective-permute-start | bytes 737288 | tf_op jit(solution)/shard_map/ppermute | solution.py:414
  207.1 20.4 %collective-permute-start.32 = (f32[192,768]{1,0:T(8,128)S(1)}, f32[192,768]{1,0:T(8,128)S(1)}, u32[]{:S(2)}, u32[]{:S(2)}) collective-permute-start(f32[192,768]{1,0:T(8,128)S(1)} %maximum_select_fusion.4), channel_id=1, source_target_pairs={{0,8},{4,12},{8,0},{12,4},{16,24},{20,28},{24,16},{28,20},{1,9},{5... | collective-permute-start | bytes 1769480 | tf_op jit(solution)/shard_map/ppermute | solution.py:431
  207.8 8.5 %collective-permute-start.14 = (f32[112,640]{1,0:T(8,128)S(1)}, f32[112,640]{1,0:T(8,128)S(1)}, u32[]{:S(2)}, u32[]{:S(2)}) collective-permute-start(f32[112,640]{1,0:T(8,128)S(1)} %constant_dynamic-slice_fusion.2), channel_id=1, source_target_pairs={{0,4},{4,0},{8,12},{12,8},{16,20},{20,16},{24,28},{28,24},{1,5},{5... | collective-permute-start | bytes 860168 | tf_op jit(solution)/shard_map/ppermute | solution.py:414
  209.7 14.5 %collective-permute-start.13 = (f32[48,640]{1,0:T(8,128)S(1)}, f32[48,640]{1,0:T(8,128)S(1)}, u32[]{:S(2)}, u32[]{:S(2)}) collective-permute-start(f32[48,640]{1,0:T(8,128)S(1)} %constant_dynamic-slice_fusion.3), channel_id=1, source_target_pairs={{0,16},{4,20},{8,24},{12,28},{16,0},{20,4},{24,8},{28,12},{1,17},{... | collective-permute-start | bytes 368648 | tf_op jit(solution)/shard_map/ppermute | solution.py:414
  216.4 9.9 %collective-permute-start.15 = (f32[56,640]{1,0:T(8,128)S(1)}, f32[56,640]{1,0:T(8,128)S(1)}, u32[]{:S(2)}, u32[]{:S(2)}) collective-permute-start(f32[56,640]{1,0:T(8,128)S(1)} %constant_dynamic-slice_fusion.1), channel_id=1, source_target_pairs={{0,16},{4,20},{8,24},{12,28},{16,0},{20,4},{24,8},{28,12},{1,17},{... | collective-permute-start | bytes 430088 | tf_op jit(solution)/shard_map/ppermute | solution.py:414
  224.2 4.9 %copy-start.4 = (f32[1024,384]{1,0:T(8,128)S(1)}, f32[1024,384]{1,0:T(8,128)}, u32[]{:S(2)}) copy-start(f32[1024,384]{1,0:T(8,128)} %copy-done.3) | copy-start | bytes 4718596
  226.4 3.4 %collective-permute-start.16 = (f32[104,256]{1,0:T(8,128)S(1)}, f32[104,256]{1,0:T(8,128)S(1)}, u32[]{:S(2)}, u32[]{:S(2)}) collective-permute-start(f32[104,256]{1,0:T(8,128)S(1)} %pad_maximum_fusion.4), channel_id=1, source_target_pairs={{0,1},{1,0},{2,3},{3,2},{4,5},{5,4},{6,7},{7,6},{8,9},{9,8},{10,11... | collective-permute-start | bytes 319496 | tf_op jit(solution)/shard_map/ppermute | solution.py:616
  228.6 65.3 %collective-permute-start.33 = (f32[384,768]{1,0:T(8,128)}, f32[384,768]{1,0:T(8,128)}, u32[]{:S(2)}, u32[]{:S(2)}) collective-permute-start(f32[384,768]{1,0:T(8,128)} %maximum_select_fusion.1), channel_id=1, source_target_pairs={{0,4},{4,0},{8,12},{12,8},{16,20},{20,16},{24,28},{28,24},{1,5},{5... | collective-permute-start | bytes 3538952 | tf_op jit(solution)/shard_map/ppermute | solution.py:431
  229.3 7.0 %copy-start.1 = (f32[1024,384]{1,0:T(8,128)}, f32[1024,384]{1,0:T(8,128)S(1)}, u32[]{:S(2)}) copy-start(f32[1024,384]{1,0:T(8,128)S(1)} %add.210.own_ref) | copy-start | bytes 4718596
  229.3 79.3 %collective-permute-start.23 = (f32[1024,384]{1,0:T(8,128)S(1)}, f32[1024,384]{1,0:T(8,128)}, u32[]{:S(2)}, u32[]{:S(2)}) collective-permute-start(f32[1024,384]{1,0:T(8,128)S(1)} %add.210.own_ref), channel_id=1, source_target_pairs={{0,1},{1,0},{2,3},{3,2},{4,5},{5,4},{6,7},{7,6},{8,9},{9,8},{10,11... | collective-permute-start | bytes 4718600 | tf_op jit(solution)/shard_map/ppermute | solution.py:456
  229.4 68.6 %collective-permute-start.20 = (f32[1024,384]{1,0:T(8,128)}, f32[1024,384]{1,0:T(8,128)}, u32[]{:S(2)}, u32[]{:S(2)}) collective-permute-start(f32[1024,384]{1,0:T(8,128)} %add.187), channel_id=1, source_target_pairs={{0,2},{1,3},{2,0},{3,1},{4,6},{5,7},{6,4},{7,5},{8,10},{9,11},{10,... | collective-permute-start | bytes 4718600 | tf_op jit(solution)/shard_map/ppermute | solution.py:451
  229.7 39.0 %collective-permute-start.17 = (f32[104,256]{1,0:T(8,128)S(1)}, f32[104,256]{1,0:T(8,128)}, u32[]{:S(2)}, u32[]{:S(2)}) collective-permute-start(f32[104,256]{1,0:T(8,128)S(1)} %fusion.12), channel_id=1, source_target_pairs={{0,2},{1,3},{2,0},{3,1},{4,6},{5,7},{6,4},{7,5},{8,10},{9,11},{10,... | collective-permute-start | bytes 319496 | tf_op jit(solution)/shard_map/ppermute | solution.py:616
  269.7 14.1 %collective-permute-start.27 = (f32[48,640]{1,0:T(8,128)S(1)}, f32[48,640]{1,0:T(8,128)S(1)}, u32[]{:S(2)}, u32[]{:S(2)}) collective-permute-start(f32[48,640]{1,0:T(8,128)S(1)} %pad_maximum_fusion.3), channel_id=1, source_target_pairs={{0,16},{4,20},{8,24},{12,28},{16,0},{20,4},{24,8},{28,12},{1,17},{... | collective-permute-start | bytes 368648 | tf_op jit(solution)/shard_map/ppermute | solution.py:431
  274.5 11.9 %collective-permute-start.24 = (f32[56,640]{1,0:T(8,128)S(1)}, f32[56,640]{1,0:T(8,128)S(1)}, u32[]{:S(2)}, u32[]{:S(2)}) collective-permute-start(f32[56,640]{1,0:T(8,128)S(1)} %pad_maximum_fusion.2), channel_id=1, source_target_pairs={{0,16},{4,20},{8,24},{12,28},{16,0},{20,4},{24,8},{28,12},{1,17},{... | collective-permute-start | bytes 430088 | tf_op jit(solution)/shard_map/ppermute | solution.py:431
  283.9 7.7 %collective-permute-start.28 = (f32[96,640]{1,0:T(8,128)S(1)}, f32[96,640]{1,0:T(8,128)S(1)}, u32[]{:S(2)}, u32[]{:S(2)}) collective-permute-start(f32[96,640]{1,0:T(8,128)S(1)} %maximum_select_fusion.8), channel_id=1, source_target_pairs={{0,8},{4,12},{8,0},{12,4},{16,24},{20,28},{24,16},{28,20},{1,9},{5... | collective-permute-start | bytes 737288 | tf_op jit(solution)/shard_map/ppermute | solution.py:431
  286.4 10.3 %collective-permute-start.25 = (f32[112,640]{1,0:T(8,128)S(1)}, f32[112,640]{1,0:T(8,128)S(1)}, u32[]{:S(2)}, u32[]{:S(2)}) collective-permute-start(f32[112,640]{1,0:T(8,128)S(1)} %maximum_select_fusion.7), channel_id=1, source_target_pairs={{0,4},{4,0},{8,12},{12,8},{16,20},{20,16},{24,28},{28,24},{1,5},{5... | collective-permute-start | bytes 860168 | tf_op jit(solution)/shard_map/ppermute | solution.py:431
  292.4 12.9 %collective-permute-start.29 = (f32[192,640]{1,0:T(8,128)}, f32[192,640]{1,0:T(8,128)}, u32[]{:S(2)}, u32[]{:S(2)}) collective-permute-start(f32[192,640]{1,0:T(8,128)} %maximum_select_fusion.6), channel_id=1, source_target_pairs={{0,4},{4,0},{8,12},{12,8},{16,20},{20,16},{24,28},{28,24},{1,5},{5... | collective-permute-start | bytes 1474568 | tf_op jit(solution)/shard_map/ppermute | solution.py:431
  297.6 16.6 %collective-permute-start.26 = (f32[224,640]{1,0:T(8,128)}, f32[224,640]{1,0:T(8,128)}, u32[]{:S(2)}, u32[]{:S(2)}) collective-permute-start(f32[224,640]{1,0:T(8,128)} %maximum_select_fusion.5), channel_id=1, source_target_pairs={{0,8},{4,12},{8,0},{12,4},{16,24},{20,28},{24,16},{28,20},{1,9},{5... | collective-permute-start | bytes 1720328 | tf_op jit(solution)/shard_map/ppermute | solution.py:431
  300.0 2.0 copy-start.2
  300.0 25.5 %collective-permute-start.21 = (f32[1024,384]{1,0:T(8,128)S(1)}, f32[1024,384]{1,0:T(8,128)}, u32[]{:S(2)}, u32[]{:S(2)}) collective-permute-start(f32[1024,384]{1,0:T(8,128)S(1)} %add.209.own_ref), channel_id=1, source_target_pairs={{0,1},{1,0},{2,3},{3,2},{4,5},{5,4},{6,7},{7,6},{8,9},{9,8},{10,11... | collective-permute-start | bytes 4718600 | tf_op jit(solution)/shard_map/ppermute | solution.py:456
  316.8 7.2 %copy-start.6 = (f32[384,384]{1,0:T(8,128)S(1)}, f32[384,384]{1,0:T(8,128)}, u32[]{:S(2)}) copy-start(f32[384,384]{1,0:T(8,128)} %slice.146) | copy-start | bytes 1769476
  321.3 2.7 copy-start.7
